TPU v7x, 32 devices: a whole 2x2x4 slice. The times are simulated.
32 devices in a mesh: seq: 8 (over z, y), head: 4 (over x, core).
Axes of the slice: x: 2, y: 2, z: 4, core: 2. Of those that a mesh axis runs over, the one named last changes fastest.
Arguments:
- queries: bfloat16 [8192, 32, 128], P('seq', 'head'), may hold values from -150 to 150
- keyvals: bfloat16 [8192, 4, 128], P('seq', 'head'), may hold values from -6.5 to 6.5
- selected: int32 [128, 16], P('seq'), may hold values from 0 to 127, as said below
- d_out: bfloat16 [8192, 32, 128], P('seq', 'head'), may hold values from -40 to 40
Outputs:
- grad_queries: bfloat16 [8192, 32, 128], P('seq', 'head')
- grad_kv: bfloat16 [8192, 4, 128], P('seq', 'head')
Inputs may be any that keep to these rules, and one draw needn't show every extreme that they name: `selected`: tiles form shards of 16 in order, as do the query blocks. Block b names tile 0 in slot 0, tile b in slot 1 and tile max(b - 1, 0) in slot 2, and no tile above b; tiles may repeat in a row. So slot 0 names a tile of shard 0, and slot 2 of the first block of a shard d >= 1 names a tile of shard d - 1. In blocks of shard d >= 1, slots 3 to 8 name tiles of lower shards; in blocks of shard 0 they name tiles of shard 0; slots 6 + 3 to 15 of every block name tiles of the block's own shard. For every shard d >= 1 and every lower shard e, the blocks of d together name, over all their slots, exactly 3 distinct tiles of e.
All inputs are finite; a program needn't handle non-finite values.
Results may differ from a plain program's by a relative error of at most 0.005.
Values may be sent and summed in bfloat16 or wider, within the bound.
No kernel may reach another device: no remote copies, remote signals or barrier semaphores. Data moves between devices by JAX's collectives and lax.ppermute only.
A program may use at most 128 MiB of HBM per device.

v0:
```python
import math

import jax
import jax.numpy as jnp
from jax import lax
from jax.sharding import PartitionSpec as P

TILE = 64
SEL = 16
CAP = 3


def partner_2(block, axis, apart):
    count = lax.axis_size(axis)
    route = []
    for low in range(count):
        high = low | 1 << apart
        if high != low and high < count:
            route += [(low, high), (high, low)]
    return lax.ppermute(block, axis, route)


def live_slots(selected):
    slot_ids = jnp.arange(SEL, dtype=jnp.int32)
    earlier = slot_ids[None, :] < slot_ids[:, None]
    repeats = selected[:, :, None] == selected[:, None, :]
    return jnp.logical_not(jnp.any(repeats & earlier[None, :, :], axis=2))


def attend_tiles(query_blk, dout_blk, key_sel, value_sel, live_mask, block_ids, sel_ids):
    inv_root = query_blk.shape[-1] ** (-0.5)
    query_pos = block_ids[:, None] * TILE + jnp.arange(TILE, dtype=jnp.int32)[None, :]
    key_pos = (
        sel_ids[:, :, None] * TILE + jnp.arange(TILE, dtype=jnp.int32)[None, None, :]
    ).reshape(sel_ids.shape[0], SEL * TILE)
    key_live = jnp.repeat(live_mask, TILE, axis=1)
    allowed = key_live[:, None, None, :] & (
        key_pos[:, None, None, :] <= query_pos[:, None, :, None]
    )
    scores = (
        jnp.einsum("gqhd,gnd->ghqn", query_blk, key_sel, preferred_element_type=jnp.float32)
        * inv_root
    )
    masked = jnp.where(allowed, scores, -jnp.inf)
    row_max = jnp.max(masked, axis=3, keepdims=True)
    raised = jnp.where(allowed, jnp.exp(masked - row_max), 0.0)
    prob_rows = raised / jnp.sum(raised, axis=3, keepdims=True)
    weights = prob_rows.astype(jnp.bfloat16)
    d_prob = jnp.einsum("gqhd,gnd->ghqn", dout_blk, value_sel, preferred_element_type=jnp.float32)
    row_delta = jnp.sum(prob_rows * d_prob, axis=3, keepdims=True)
    dscore = (prob_rows * (d_prob - row_delta)).astype(jnp.bfloat16)
    grad_q = (
        jnp.einsum("ghqn,gnd->gqhd", dscore, key_sel, preferred_element_type=jnp.float32) * inv_root
    )
    grad_k = (
        jnp.einsum("ghqn,gqhd->gnd", dscore, query_blk, preferred_element_type=jnp.float32)
        * inv_root
    )
    grad_v = jnp.einsum("ghqn,gqhd->gnd", weights, dout_blk, preferred_element_type=jnp.float32)
    return (grad_q, grad_k, grad_v)


def on_device(queries, keyvals, selected, d_out):
    tok_rows, head_count, head_dim = queries.shape
    blocks = tok_rows // TILE
    shards = lax.axis_size("seq")
    my_shard = lax.axis_index("seq")
    is_even = lax.axis_index("head") % 2 == 0
    my_half = keyvals[:, 0, :]
    partner = partner_2(my_half, "head", 0)
    key_rows = jnp.where(is_even, my_half, partner)
    value_rows = jnp.where(is_even, partner, my_half)
    own_tiles = jnp.stack([key_rows, value_rows], axis=1).reshape(blocks, TILE, 2, head_dim)
    live_mask = live_slots(selected)
    owner_shard = selected // blocks
    local_tile = selected % blocks
    tile_ids = jnp.arange(shards * blocks, dtype=jnp.int32)
    matches = selected[:, :, None] == tile_ids[None, None, :]
    wanted_hits = matches & live_mask[:, :, None] & (owner_shard != my_shard)[:, :, None]
    wanted = jnp.any(wanted_hits, axis=(0, 1)).reshape(shards, blocks)
    rank_in_owner = jnp.cumsum(wanted.astype(jnp.int32), axis=1) - 1
    slot_ids = jnp.arange(CAP, dtype=jnp.int32)
    placed = wanted[:, :, None] & (rank_in_owner[:, :, None] == slot_ids[None, None, :])
    asked_tile = jnp.sum(
        placed.astype(jnp.int32) * jnp.arange(blocks, dtype=jnp.int32)[None, :, None], axis=1
    )
    filled = jnp.any(placed, axis=1)
    request = jnp.where(filled, asked_tile, -1)
    incoming = lax.all_to_all(request, "seq", split_axis=0, concat_axis=0, tiled=True)
    replies = own_tiles[jnp.clip(incoming, 0, blocks - 1)]
    replies = jnp.where(
        (incoming >= 0)[:, :, None, None, None], replies, jnp.zeros((), jnp.bfloat16)
    )
    fetched = lax.all_to_all(replies, "seq", split_axis=0, concat_axis=0, tiled=True)
    workspace = jnp.concatenate(
        [own_tiles, fetched.reshape((shards * CAP, TILE, 2, head_dim))], axis=0
    )
    rank_flat = rank_in_owner.reshape(-1)
    rank_of = jnp.sum(jnp.where(matches, rank_flat[None, None, :], 0), axis=2)
    slot_index = jnp.where(
        owner_shard == my_shard, local_tile, blocks + owner_shard * CAP + rank_of
    )
    per_step = math.gcd(blocks, 4)
    rounds = blocks // per_step
    query_blocks = queries.reshape(blocks, TILE, head_count, head_dim)
    dout_blocks = d_out.reshape(blocks, TILE, head_count, head_dim)
    ws_keys = workspace[:, :, 0, :]
    ws_values = workspace[:, :, 1, :]

    def step(totals, step_index):
        first_row = step_index * per_step
        slot_sel = lax.dynamic_slice_in_dim(slot_index, first_row, per_step, 0)
        sel_ids = lax.dynamic_slice_in_dim(selected, first_row, per_step, 0)
        live_blk = lax.dynamic_slice_in_dim(live_mask, first_row, per_step, 0)
        query_blk = lax.dynamic_slice_in_dim(query_blocks, first_row, per_step, 0)
        dout_blk = lax.dynamic_slice_in_dim(dout_blocks, first_row, per_step, 0)
        key_sel = ws_keys[slot_sel].reshape(per_step, SEL * TILE, head_dim)
        value_sel = ws_values[slot_sel].reshape(per_step, SEL * TILE, head_dim)
        block_ids = my_shard * blocks + first_row + jnp.arange(per_step, dtype=jnp.int32)
        grad_q, grad_k, grad_v = attend_tiles(
            query_blk, dout_blk, key_sel, value_sel, live_blk, block_ids, sel_ids
        )
        slot_grads = jnp.stack(
            [
                grad_k.reshape(per_step, SEL, TILE, head_dim),
                grad_v.reshape(per_step, SEL, TILE, head_dim),
            ],
            axis=3,
        )
        totals = totals.at[slot_sel].add(slot_grads)
        return (totals, grad_q.astype(jnp.bfloat16))

    start_sums = jnp.zeros(workspace.shape, jnp.float32)
    ws_grad, grad_q_all = lax.scan(step, start_sums, jnp.arange(rounds, dtype=jnp.int32))
    grad_queries = grad_q_all.reshape(tok_rows, head_count, head_dim)
    tail_shape = ws_grad.shape[1:]
    send_back = ws_grad[blocks:].reshape((shards, CAP) + tail_shape)
    came_back = lax.all_to_all(send_back, "seq", split_axis=0, concat_axis=0, tiled=True)
    target = jnp.where(incoming >= 0, incoming, blocks).reshape(-1)
    owned_sums = (
        ws_grad[:blocks]
        .at[target]
        .add(came_back.reshape((shards * CAP,) + tail_shape), mode="drop")
    )
    kept_half = jnp.where(is_even, owned_sums[:, :, 0, :], owned_sums[:, :, 1, :])
    other_half = jnp.where(is_even, owned_sums[:, :, 1, :], owned_sums[:, :, 0, :])
    kept_half, other_half = (kept_half, other_half)
    summed = kept_half + partner_2(other_half, "head", 0)
    grad_kv = summed.reshape(tok_rows, 1, head_dim).astype(jnp.bfloat16)
    return (grad_queries, grad_kv)


def solution(mesh):
    in_specs = (
        P("seq", "head", None),
        P("seq", "head", None),
        P("seq", None),
        P("seq", "head", None),
    )
    out_specs = (P("seq", "head", None), P("seq", "head", None))
    return jax.shard_map(
        on_device, mesh=mesh, in_specs=in_specs, out_specs=out_specs, check_vma=False
    )
```

profile of v0, /device:TPU:0, one launch (start us, length us, event | category | flops | bytes accessed | tf_op | source)
XLA Modules:
  0.0 292.8 jit_solution(16966995865055851307)
XLA Ops:
  5.2 6.9 %all-to-all-start = ((s32[8,1,3]{2,1,0:T(1,128)}), s32[8,1,3]{2,1,0:T(1,128)S(1)}, u32[]{:S(2)}, u32[]{:S(2)}) async-start(s32[8,1,3]{2,1,0:T(1,128)} %copy.87), calls=%async_computation | async-start | bytes 8192 | tf_op jit(solution)/shard_map/all_to_all | solution.py:89
  12.1 6.4 %all-to-all-done = s32[8,1,3]{2,1,0:T(1,128)S(1)} async-done(((s32[8,1,3]{2,1,0:T(1,128)}), s32[8,1,3]{2,1,0:T(1,128)S(1)}, u32[]{:S(2)}, u32[]{:S(2)}) %all-to-all-start) | async-done | bytes 128 | tf_op jit(solution)/shard_map/all_to_all | solution.py:89
  21.7 3.5 %all-to-all-start.1 = ((bf16[8,3,64,2,128]{4,2,1,3,0:T(8,128)(2,1)}), bf16[8,3,64,2,128]{4,2,1,3,0:T(8,128)(2,1)S(1)}, u32[]{:S(2)}, u32[]{:S(2)}) async-start(bf16[8,3,64,2,128]{4,2,1,3,0:T(8,128)(2,1)} %copy.92), calls=%async_computation.1 | async-start | bytes 1572864 | tf_op jit(solution)/shard_map/all_to_all | solution.py:94
  25.8 19.1 %all-to-all-done.1 = bf16[8,3,64,2,128]{4,2,1,3,0:T(8,128)(2,1)S(1)} async-done(((bf16[8,3,64,2,128]{4,2,1,3,0:T(8,128)(2,1)}), bf16[8,3,64,2,128]{4,2,1,3,0:T(8,128)(2,1)S(1)}, u32[]{:S(2)}, u32[]{:S(2)}) %all-to-all-start.1) | async-done | bytes 786464 | tf_op jit(solution)/shard_map/all_to_all | solution.py:94
  46.4 192.2 %while.14 = (s32[]{:T(128)}, f32[40,64,2,128]{3,1,2,0:T(8,128)S(1)}, bf16[4,4,64,8,128]{4,3,2,1,0:T(8,128)(2,1)}, s32[4]{0:T(128)S(1)}, s32[16,16]{1,0:T(8,128)S...) while((s32[]{:T(128)}, ...), condition=%wide.region_11.12_spmd, body=%wide.region_6.11_spmd.sunk | while | flops 2717389312 | bytes 156475600 | solution.py:134
  56.2 8.5 %fusion.73 = (f32[4,8,64]{2,1,0:T(8,128)}, f32[4,8,64,1024]{3,2,1,0:T(8,128)}) fusion(pred[4,64,1024]{2,1,0:T(8,128)(4,1)S(1)} %compare_and_fusion.2, bf16[4,1024,128,1]{2,1,3,0:T(8,128)(2,1)} %bitcast.133, bf16[4,64,8,128]{3,2,1,0:T(8,128)(2,1)} %get-tuple-element.335), kind=kOutput, calls=%fused_computation.87.clone.1 | convolution fusion | flops 547357696 | bytes 10231808 | tf_op jit(solution)/shard_map/while/body/eval_jaxpr/sub | solution.py:46
  66.4 5.4 %fusion.75 = (f32[4,8,64]{2,1,0:T(8,128)S(1)}, f32[4,1024,64,8]{1,2,3,0:T(8,128)S(1)}) fusion(f32[4,8,64,1024]{3,2,1,0:T(8,128)} %get-tuple-element.336, f32[4,8,64]{2,1,0:T(8,128)} %get-tuple-element.337, bf16[4,1024,128,1]{2,1,3,0:T(8,128)(2,1)} %bitcast.137, bf16[4,64,8,128]{3,2,1,0:T(8,128)(2,1)} %get-tuple-element.333), kind=kOutput, calls=%fused_computation.8.clone.1 | convolution fusion | flops 543160320 | bytes 18366464 | tf_op jit(solution)/shard_map/while/body/eval_jaxpr/gqhd,gnd->ghqn/dot_general | solution.py:49
  80.7 8.8 %scatter_fusion = f32[40,64,2,128]{3,1,2,0:T(8,128)S(1)} fusion(f32[40,64,2,128]{3,1,2,0:T(8,128)S(1)} %get-tuple-element.357, s32[64]{0:T(128)S(1)} %reshape.322, f32[64,64,2,128]{3,1,2,0:T(8,128)} %bitcast.130), kind=kCustom, calls=%fused_computation.3.clone.1 | custom fusion | flops 1048576 | bytes 12583168 | tf_op jit(solution)/shard_map/while/body/eval_jaxpr/scatter-add | solution.py:130
  89.5 3.8 %fusion.77 = bf16[1,4,64,8,128]{4,2,3,1,0:T(8,128)(2,1)S(1)} fusion(bf16[4,1024,128,1]{2,1,3,0:T(8,128)(2,1)} %bitcast.134, bf16[4,8,64,1024]{3,2,1,0:T(8,128)(2,1)} %copy-done), kind=kOutput, calls=%fused_computation.24.clone.1 | convolution fusion | flops 537395200 | bytes 5767168 | tf_op jit(solution)/shard_map/while/body/eval_jaxpr/ghqn,gnd->gqhd/dot_general | solution.py:53
  104.3 8.5 %fusion.73 = (f32[4,8,64]{2,1,0:T(8,128)}, f32[4,8,64,1024]{3,2,1,0:T(8,128)}) fusion(pred[4,64,1024]{2,1,0:T(8,128)(4,1)S(1)} %compare_and_fusion.2, bf16[4,1024,128,1]{2,1,3,0:T(8,128)(2,1)} %bitcast.133, bf16[4,64,8,128]{3,2,1,0:T(8,128)(2,1)} %get-tuple-element.335), kind=kOutput, calls=%fused_computation.87.clone.1 | convolution fusion | flops 547357696 | bytes 10231808 | tf_op jit(solution)/shard_map/while/body/eval_jaxpr/sub | solution.py:46
  114.4 5.4 %fusion.75 = (f32[4,8,64]{2,1,0:T(8,128)S(1)}, f32[4,1024,64,8]{1,2,3,0:T(8,128)S(1)}) fusion(f32[4,8,64,1024]{3,2,1,0:T(8,128)} %get-tuple-element.336, f32[4,8,64]{2,1,0:T(8,128)} %get-tuple-element.337, bf16[4,1024,128,1]{2,1,3,0:T(8,128)(2,1)} %bitcast.137, bf16[4,64,8,128]{3,2,1,0:T(8,128)(2,1)} %get-tuple-element.333), kind=kOutput, calls=%fused_computation.8.clone.1 | convolution fusion | flops 543160320 | bytes 18366464 | tf_op jit(solution)/shard_map/while/body/eval_jaxpr/gqhd,gnd->ghqn/dot_general | solution.py:49
  128.8 8.8 %scatter_fusion = f32[40,64,2,128]{3,1,2,0:T(8,128)S(1)} fusion(f32[40,64,2,128]{3,1,2,0:T(8,128)S(1)} %get-tuple-element.357, s32[64]{0:T(128)S(1)} %reshape.322, f32[64,64,2,128]{3,1,2,0:T(8,128)} %bitcast.130), kind=kCustom, calls=%fused_computation.3.clone.1 | custom fusion | flops 1048576 | bytes 12583168 | tf_op jit(solution)/shard_map/while/body/eval_jaxpr/scatter-add | solution.py:130
  137.6 3.8 %fusion.77 = bf16[1,4,64,8,128]{4,2,3,1,0:T(8,128)(2,1)S(1)} fusion(bf16[4,1024,128,1]{2,1,3,0:T(8,128)(2,1)} %bitcast.134, bf16[4,8,64,1024]{3,2,1,0:T(8,128)(2,1)} %copy-done), kind=kOutput, calls=%fused_computation.24.clone.1 | convolution fusion | flops 537395200 | bytes 5767168 | tf_op jit(solution)/shard_map/while/body/eval_jaxpr/ghqn,gnd->gqhd/dot_general | solution.py:53
  152.3 8.5 %fusion.73 = (f32[4,8,64]{2,1,0:T(8,128)}, f32[4,8,64,1024]{3,2,1,0:T(8,128)}) fusion(pred[4,64,1024]{2,1,0:T(8,128)(4,1)S(1)} %compare_and_fusion.2, bf16[4,1024,128,1]{2,1,3,0:T(8,128)(2,1)} %bitcast.133, bf16[4,64,8,128]{3,2,1,0:T(8,128)(2,1)} %get-tuple-element.335), kind=kOutput, calls=%fused_computation.87.clone.1 | convolution fusion | flops 547357696 | bytes 10231808 | tf_op jit(solution)/shard_map/while/body/eval_jaxpr/sub | solution.py:46
  162.5 5.4 %fusion.75 = (f32[4,8,64]{2,1,0:T(8,128)S(1)}, f32[4,1024,64,8]{1,2,3,0:T(8,128)S(1)}) fusion(f32[4,8,64,1024]{3,2,1,0:T(8,128)} %get-tuple-element.336, f32[4,8,64]{2,1,0:T(8,128)} %get-tuple-element.337, bf16[4,1024,128,1]{2,1,3,0:T(8,128)(2,1)} %bitcast.137, bf16[4,64,8,128]{3,2,1,0:T(8,128)(2,1)} %get-tuple-element.333), kind=kOutput, calls=%fused_computation.8.clone.1 | convolution fusion | flops 543160320 | bytes 18366464 | tf_op jit(solution)/shard_map/while/body/eval_jaxpr/gqhd,gnd->ghqn/dot_general | solution.py:49
  176.8 8.8 %scatter_fusion = f32[40,64,2,128]{3,1,2,0:T(8,128)S(1)} fusion(f32[40,64,2,128]{3,1,2,0:T(8,128)S(1)} %get-tuple-element.357, s32[64]{0:T(128)S(1)} %reshape.322, f32[64,64,2,128]{3,1,2,0:T(8,128)} %bitcast.130), kind=kCustom, calls=%fused_computation.3.clone.1 | custom fusion | flops 1048576 | bytes 12583168 | tf_op jit(solution)/shard_map/while/body/eval_jaxpr/scatter-add | solution.py:130
  185.6 3.8 %fusion.77 = bf16[1,4,64,8,128]{4,2,3,1,0:T(8,128)(2,1)S(1)} fusion(bf16[4,1024,128,1]{2,1,3,0:T(8,128)(2,1)} %bitcast.134, bf16[4,8,64,1024]{3,2,1,0:T(8,128)(2,1)} %copy-done), kind=kOutput, calls=%fused_computation.24.clone.1 | convolution fusion | flops 537395200 | bytes 5767168 | tf_op jit(solution)/shard_map/while/body/eval_jaxpr/ghqn,gnd->gqhd/dot_general | solution.py:53
  200.4 8.5 %fusion.73 = (f32[4,8,64]{2,1,0:T(8,128)}, f32[4,8,64,1024]{3,2,1,0:T(8,128)}) fusion(pred[4,64,1024]{2,1,0:T(8,128)(4,1)S(1)} %compare_and_fusion.2, bf16[4,1024,128,1]{2,1,3,0:T(8,128)(2,1)} %bitcast.133, bf16[4,64,8,128]{3,2,1,0:T(8,128)(2,1)} %get-tuple-element.335), kind=kOutput, calls=%fused_computation.87.clone.1 | convolution fusion | flops 547357696 | bytes 10231808 | tf_op jit(solution)/shard_map/while/body/eval_jaxpr/sub | solution.py:46
  210.5 5.4 %fusion.75 = (f32[4,8,64]{2,1,0:T(8,128)S(1)}, f32[4,1024,64,8]{1,2,3,0:T(8,128)S(1)}) fusion(f32[4,8,64,1024]{3,2,1,0:T(8,128)} %get-tuple-element.336, f32[4,8,64]{2,1,0:T(8,128)} %get-tuple-element.337, bf16[4,1024,128,1]{2,1,3,0:T(8,128)(2,1)} %bitcast.137, bf16[4,64,8,128]{3,2,1,0:T(8,128)(2,1)} %get-tuple-element.333), kind=kOutput, calls=%fused_computation.8.clone.1 | convolution fusion | flops 543160320 | bytes 18366464 | tf_op jit(solution)/shard_map/while/body/eval_jaxpr/gqhd,gnd->ghqn/dot_general | solution.py:49
  224.9 8.8 %scatter_fusion = f32[40,64,2,128]{3,1,2,0:T(8,128)S(1)} fusion(f32[40,64,2,128]{3,1,2,0:T(8,128)S(1)} %get-tuple-element.357, s32[64]{0:T(128)S(1)} %reshape.322, f32[64,64,2,128]{3,1,2,0:T(8,128)} %bitcast.130), kind=kCustom, calls=%fused_computation.3.clone.1 | custom fusion | flops 1048576 | bytes 12583168 | tf_op jit(solution)/shard_map/while/body/eval_jaxpr/scatter-add | solution.py:130
  233.7 3.8 %fusion.77 = bf16[1,4,64,8,128]{4,2,3,1,0:T(8,128)(2,1)S(1)} fusion(bf16[4,1024,128,1]{2,1,3,0:T(8,128)(2,1)} %bitcast.134, bf16[4,8,64,1024]{3,2,1,0:T(8,128)(2,1)} %copy-done), kind=kOutput, calls=%fused_computation.24.clone.1 | convolution fusion | flops 537395200 | bytes 5767168 | tf_op jit(solution)/shard_map/while/body/eval_jaxpr/ghqn,gnd->gqhd/dot_general | solution.py:53
  239.9 4.3 %all-to-all-start.2 = ((f32[8,3,64,2,128]{4,2,3,1,0:T(8,128)}), f32[8,3,64,2,128]{4,2,3,1,0:T(8,128)}, u32[]{:S(2)}, u32[]{:S(2)}) async-start(f32[8,3,64,2,128]{4,2,3,1,0:T(8,128)} %bitcast.138), calls=%async_computation.2 | async-start | bytes 3145728 | tf_op jit(solution)/shard_map/all_to_all | solution.py:138
  246.5 34.2 %all-to-all-done.2 = f32[8,3,64,2,128]{4,2,3,1,0:T(8,128)} async-done(((f32[8,3,64,2,128]{4,2,3,1,0:T(8,128)}), f32[8,3,64,2,128]{4,2,3,1,0:T(8,128)}, u32[]{:S(2)}, u32[]{:S(2)}) %all-to-all-start.2) | async-done | bytes 1572896 | tf_op jit(solution)/shard_map/all_to_all | solution.py:138
  280.7 6.8 %scatter_fusion.1 = f32[16,64,2,128]{3,1,2,0:T(8,128)} fusion(f32[16,64,2,128]{3,1,2,0:T(8,128)} %slice.22, s32[24]{0:T(128)S(1)} %fusion.38, f32[24,64,2,128]{3,1,2,0:T(8,128)} %bitcast.35), kind=kCustom, calls=%fused_computation.4 | custom fusion | flops 393216 | bytes 4718688 | tf_op jit(solution)/shard_map/scatter-add | solution.py:143
  (256 shorter events, 101.8 us)
Async XLA Ops:
  0.6 18.2 %collective-permute-start = (bf16[1024,128]{1,0:T(8,128)(2,1)}, bf16[1024,128]{1,0:T(8,128)(2,1)S(1)}, u32[]{:S(2)}, u32[]{:S(2)}) collective-permute-start(bf16[1024,128]{1,0:T(8,128)(2,1)} %bitcast.147), channel_id=1, source_target_pairs={{0,1},{1,0},{2,3},{3,2},{4,5},{5,4},{6,7},{7,6},{8,9},{9,8},{10,11... | collective-permute-start | bytes 786440 | tf_op jit(solution)/shard_map/ppermute | solution.py:20
  5.2 13.2 %all-to-all-start = ((s32[8,1,3]{2,1,0:T(1,128)}), s32[8,1,3]{2,1,0:T(1,128)S(1)}, u32[]{:S(2)}, u32[]{:S(2)}) async-start(s32[8,1,3]{2,1,0:T(1,128)} %copy.87), calls=%async_computation | async-start | bytes 8192 | tf_op jit(solution)/shard_map/all_to_all | solution.py:89
  18.9 6.5 %copy-start.3 = (s32[16,16]{1,0:T(8,128)S(1)}, s32[16,16]{1,0:T(8,128)}, u32[]{:S(2)}) copy-start(s32[16,16]{1,0:T(8,128)} %param.8) | copy-start | bytes 3076
  21.7 23.2 %all-to-all-start.1 = ((bf16[8,3,64,2,128]{4,2,1,3,0:T(8,128)(2,1)}), bf16[8,3,64,2,128]{4,2,1,3,0:T(8,128)(2,1)S(1)}, u32[]{:S(2)}, u32[]{:S(2)}) async-start(bf16[8,3,64,2,128]{4,2,1,3,0:T(8,128)(2,1)} %copy.92), calls=%async_computation.1 | async-start | bytes 1572864 | tf_op jit(solution)/shard_map/all_to_all | solution.py:94
  66.4 5.4 %slice-start = ((s8[8388608]{0:T(1024)(128)(4,1)}), s8[4194304]{0:T(1024)(128)(4,1)S(1)}, s32[]{:S(2)}) async-start(s8[8388608]{0:T(1024)(128)(4,1)} %bitcast.131), calls=%async_computation.3 | async-start | bytes 8388608 | tf_op jit(solution)/shard_map/while
  66.4 6.3 %slice-start.1 = ((s8[8388608]{0:T(1024)(128)(4,1)}), s8[4194304]{0:T(1024)(128)(4,1)S(1)}, s32[]{:S(2)}) async-start(s8[8388608]{0:T(1024)(128)(4,1)} %bitcast.131), calls=%async_computation.4 | async-start | bytes 8388608 | tf_op jit(solution)/shard_map/while
  66.4 6.3 %copy-start.5 = (f32[4,8,64]{2,1,0:T(8,128)S(1)}, f32[4,8,64]{2,1,0:T(8,128)}, u32[]{:S(2)}) copy-start(f32[4,8,64]{2,1,0:T(8,128)} %get-tuple-element.337) | copy-start | bytes 24580 | tf_op jit(solution)/shard_map/while
  89.5 5.0 %copy-start.4 = (s32[16,16]{1,0:T(8,128)S(1)}, s32[16,16]{1,0:T(8,128)}, u32[]{:S(2)}) copy-start(s32[16,16]{1,0:T(8,128)} %get-tuple-element.409) | copy-start | bytes 3076 | tf_op jit(solution)/shard_map/while
  89.5 5.0 %copy-start.7 = (s32[16,16]{1,0:T(8,128)S(1)}, s32[16,16]{1,0:T(8,128)}, u32[]{:S(2)}) copy-start(s32[16,16]{1,0:T(8,128)} %copy-done.6) | copy-start | bytes 3076 | tf_op jit(solution)/shard_map/while
  114.4 5.4 %slice-start = ((s8[8388608]{0:T(1024)(128)(4,1)}), s8[4194304]{0:T(1024)(128)(4,1)S(1)}, s32[]{:S(2)}) async-start(s8[8388608]{0:T(1024)(128)(4,1)} %bitcast.131), calls=%async_computation.3 | async-start | bytes 8388608 | tf_op jit(solution)/shard_map/while
  114.4 6.3 %slice-start.1 = ((s8[8388608]{0:T(1024)(128)(4,1)}), s8[4194304]{0:T(1024)(128)(4,1)S(1)}, s32[]{:S(2)}) async-start(s8[8388608]{0:T(1024)(128)(4,1)} %bitcast.131), calls=%async_computation.4 | async-start | bytes 8388608 | tf_op jit(solution)/shard_map/while
  114.4 6.3 %copy-start.5 = (f32[4,8,64]{2,1,0:T(8,128)S(1)}, f32[4,8,64]{2,1,0:T(8,128)}, u32[]{:S(2)}) copy-start(f32[4,8,64]{2,1,0:T(8,128)} %get-tuple-element.337) | copy-start | bytes 24580 | tf_op jit(solution)/shard_map/while
  137.5 5.0 %copy-start.4 = (s32[16,16]{1,0:T(8,128)S(1)}, s32[16,16]{1,0:T(8,128)}, u32[]{:S(2)}) copy-start(s32[16,16]{1,0:T(8,128)} %get-tuple-element.409) | copy-start | bytes 3076 | tf_op jit(solution)/shard_map/while
  162.5 5.4 %slice-start = ((s8[8388608]{0:T(1024)(128)(4,1)}), s8[4194304]{0:T(1024)(128)(4,1)S(1)}, s32[]{:S(2)}) async-start(s8[8388608]{0:T(1024)(128)(4,1)} %bitcast.131), calls=%async_computation.3 | async-start | bytes 8388608 | tf_op jit(solution)/shard_map/while
  162.5 6.3 %slice-start.1 = ((s8[8388608]{0:T(1024)(128)(4,1)}), s8[4194304]{0:T(1024)(128)(4,1)S(1)}, s32[]{:S(2)}) async-start(s8[8388608]{0:T(1024)(128)(4,1)} %bitcast.131), calls=%async_computation.4 | async-start | bytes 8388608 | tf_op jit(solution)/shard_map/while
  162.5 6.3 %copy-start.5 = (f32[4,8,64]{2,1,0:T(8,128)S(1)}, f32[4,8,64]{2,1,0:T(8,128)}, u32[]{:S(2)}) copy-start(f32[4,8,64]{2,1,0:T(8,128)} %get-tuple-element.337) | copy-start | bytes 24580 | tf_op jit(solution)/shard_map/while
  185.6 5.0 %copy-start.4 = (s32[16,16]{1,0:T(8,128)S(1)}, s32[16,16]{1,0:T(8,128)}, u32[]{:S(2)}) copy-start(s32[16,16]{1,0:T(8,128)} %get-tuple-element.409) | copy-start | bytes 3076 | tf_op jit(solution)/shard_map/while
  210.5 5.4 %slice-start = ((s8[8388608]{0:T(1024)(128)(4,1)}), s8[4194304]{0:T(1024)(128)(4,1)S(1)}, s32[]{:S(2)}) async-start(s8[8388608]{0:T(1024)(128)(4,1)} %bitcast.131), calls=%async_computation.3 | async-start | bytes 8388608 | tf_op jit(solution)/shard_map/while
  210.5 6.3 %slice-start.1 = ((s8[8388608]{0:T(1024)(128)(4,1)}), s8[4194304]{0:T(1024)(128)(4,1)S(1)}, s32[]{:S(2)}) async-start(s8[8388608]{0:T(1024)(128)(4,1)} %bitcast.131), calls=%async_computation.4 | async-start | bytes 8388608 | tf_op jit(solution)/shard_map/while
  210.5 6.3 %copy-start.5 = (f32[4,8,64]{2,1,0:T(8,128)S(1)}, f32[4,8,64]{2,1,0:T(8,128)}, u32[]{:S(2)}) copy-start(f32[4,8,64]{2,1,0:T(8,128)} %get-tuple-element.337) | copy-start | bytes 24580 | tf_op jit(solution)/shard_map/while
  233.7 5.0 %copy-start.4 = (s32[16,16]{1,0:T(8,128)S(1)}, s32[16,16]{1,0:T(8,128)}, u32[]{:S(2)}) copy-start(s32[16,16]{1,0:T(8,128)} %get-tuple-element.409) | copy-start | bytes 3076 | tf_op jit(solution)/shard_map/while
  238.6 6.1 %copy-start.9 = (s32[8,1,3]{2,1,0:T(1,128)S(1)}, s32[8,1,3]{2,1,0:T(1,128)}, u32[]{:S(2)}) copy-start(s32[8,1,3]{2,1,0:T(1,128)} %copy-done.8) | copy-start | bytes 292
  239.9 40.8 %all-to-all-start.2 = ((f32[8,3,64,2,128]{4,2,3,1,0:T(8,128)}), f32[8,3,64,2,128]{4,2,3,1,0:T(8,128)}, u32[]{:S(2)}, u32[]{:S(2)}) async-start(f32[8,3,64,2,128]{4,2,3,1,0:T(8,128)} %bitcast.138), calls=%async_computation.2 | async-start | bytes 3145728 | tf_op jit(solution)/shard_map/all_to_all | solution.py:138
  288.8 2.0 collective-permute-start.1
  (36 other events, 102.9 us)
where the time goes:
time: 295 us; the launch traced here: 293 us
  matrix products  85.7 us (29%)
  other arithmetic  63.7 us (22%)
  local copies, waits for them, and re-layouts  62.3 us (21%)
  waiting for transfers between devices  61.6 us (21%)
  starting transfers between devices  15.3 us (5%)
  loops' own time  3.38 us (1%)
    scatter-add x4, other arithmetic, step(): totals = totals.at[slot_sel].add(slot_grads)  35.1 us
    all_to_all x1, waiting for transfers between devices, on_device(): lax.all_to_all(send_back, 'seq', split_axis=0, concat_axis=0, tiled=True)  34.2 us
    sub x4, matrix products, attend_tiles(): raised = jnp.where(allowed, jnp.exp(masked - row_max), 0.0)  34 us
    dot_general x4, matrix products, attend_tiles(): jnp.einsum('gqhd,gnd->ghqn', dout_blk, value_sel, preferred_element_type=...  21.4 us
    all_to_all x1, waiting for transfers between devices, on_device(): lax.all_to_all(replies, 'seq', split_axis=0, concat_axis=0, tiled=True)  19.1 us
    dot_general x4, matrix products, attend_tiles(): jnp.einsum('ghqn,gnd->gqhd', dscore, key_sel, preferred_element_type=jnp....  15.1 us
    gather x4, local copies, waits for them, and re-layouts, step(): key_sel = ws_keys[slot_sel].reshape(per_step, SEL * TILE, head_dim)  11.3 us
    another operation x4, local copies, waits for them, and re-layouts, step(): jnp.stack([grad_k.reshape(per_step, SEL, TILE, head_dim), grad_v.reshape(...  9.11 us
  transfers between devices with their start and end apart: 5, of which 4 were waited for; matrix products, arithmetic and copies ran while one was open for 2% of the time, Pallas kernels for 0%

commit v1 on v0

v1 whole, which is shorter than its diff:
```python
import functools
import math

import jax
import jax.numpy as jnp
from jax import lax
from jax.experimental import pallas as pl
from jax.experimental.pallas import tpu as pltpu
from jax.sharding import PartitionSpec as P

TILE = 64
SEL = 16
CAP = 3
PACK = 4
MOST_FAR = 8
LOW = -1e30
HIGH = 1e30
NT = (((1,), (1,)), ((), ()))
TN = (((0,), (0,)), ((), ()))


def swap_pair(block):
    count = lax.axis_size("head")
    return lax.ppermute(block, "head", [(h, h ^ 1) for h in range(count)])


def tile_rows(index):
    return pl.ds(pl.multiple_of(index * TILE, TILE), TILE)


def take_tiles(ref, half, picks):
    return jnp.concatenate([ref[half, tile_rows(t), :] for t in picks], axis=0)


def dot(a, b, dims=(((1,), (0,)), ((), ()))):
    return lax.dot_general(a, b, dims, preferred_element_type=jnp.float32)


def fold(x, op):
    parts = [x[8 * i : 8 * i + 8] for i in range(TILE // 8)]
    while len(parts) > 1:
        parts = [op(parts[i], parts[i + 1]) for i in range(0, len(parts), 2)]
    return parts[0]


def mask_diagonal(x, is_first, group):
    key = lax.broadcasted_iota(jnp.int32, (TILE, x.shape[1]), 0)
    query = lax.broadcasted_iota(jnp.int32, (TILE, x.shape[1]), 1) // group
    return jnp.where((key <= query) | jnp.logical_not(is_first), x, LOW)


def lay_halves(par_ref, mine_ref, theirs_ref, kv_ref):
    par = par_ref[0]
    kv_ref[par] = mine_ref[...]
    kv_ref[1 - par] = theirs_ref[...]


def own_stats(scale, group, list_ref, par_ref, q_ref, do_ref, mine_ref, theirs_ref, st_ref, kv_ref):
    b = pl.program_id(0)

    @pl.when(b == 0)
    def _():
        lay_halves(par_ref, mine_ref, theirs_ref, kv_ref)

    count = list_ref[b, SEL]
    q = q_ref[...]
    do = do_ref[...]
    rows = q.shape[0]

    def chunk(c, carry):
        top, total, dotted = carry
        picks = [list_ref[b, c * PACK + i] for i in range(PACK)]
        real = [c * PACK + i < count for i in range(PACK)]
        x = dot(take_tiles(kv_ref, 0, picks), q, NT) * scale
        xs = [x[i * TILE : (i + 1) * TILE] for i in range(PACK)]
        xs[0] = mask_diagonal(xs[0], c == 0, group)
        new = top
        for i in range(PACK):
            new = jnp.maximum(new, jnp.where(real[i], fold(xs[i], jnp.maximum), LOW))
        new = jnp.broadcast_to(jnp.max(new, axis=0, keepdims=True), new.shape)
        fade = jnp.exp2(top - new)
        total, dotted = total * fade, dotted * fade
        dp = dot(take_tiles(kv_ref, 1, picks), do, NT)
        for i in range(PACK):
            base = jnp.where(real[i], new, HIGH)[0:1]
            e = jnp.exp2(xs[i] - base)
            total = total + fold(e, jnp.add)
            dotted = dotted + fold(e * dp[i * TILE : (i + 1) * TILE], jnp.add)
        return new, total, dotted

    zero = jnp.zeros((8, rows), jnp.float32)
    top, total, dotted = lax.fori_loop(
        0, pl.cdiv(count, PACK), chunk, (jnp.full((8, rows), LOW, jnp.float32), zero, zero)
    )
    st_ref[0] = top
    st_ref[1] = total
    st_ref[2] = dotted


def add_grads(acc_ref, picks, gk, gv):
    for i, t in enumerate(picks):
        acc_ref[0, tile_rows(t), :] += gk[i * TILE : (i + 1) * TILE]
        acc_ref[1, tile_rows(t), :] += gv[i * TILE : (i + 1) * TILE]


def far_grads(
    scale, inv_root, list_ref, par_ref, st_ref, q_ref, do_ref, mine_ref, theirs_ref,
    fin_ref, dq_ref, keep_ref, send_ref, kv_ref, acc_ref, x_ref, dp_ref,
):
    b = pl.program_id(0)

    @pl.when(b == 0)
    def _():
        lay_halves(par_ref, mine_ref, theirs_ref, kv_ref)
        acc_ref[...] = jnp.zeros_like(acc_ref)

    count = list_ref[b, SEL]
    chunks = pl.cdiv(count, PACK)
    q = q_ref[...]
    do = do_ref[...]
    span = PACK * TILE

    def chosen(c):
        return (
            [list_ref[b, c * PACK + i] for i in range(PACK)],
            [c * PACK + i < count for i in range(PACK)],
        )

    def score(c, top):
        picks, real = chosen(c)
        x = dot(take_tiles(kv_ref, 0, picks), q, NT) * scale
        x_ref[pl.ds(pl.multiple_of(c * span, span), span), :] = x
        dp_ref[pl.ds(pl.multiple_of(c * span, span), span), :] = dot(
            take_tiles(kv_ref, 1, picks), do, NT
        )
        for i in range(PACK):
            part = fold(x[i * TILE : (i + 1) * TILE], jnp.maximum)
            top = jnp.maximum(top, jnp.where(real[i], part, LOW))
        return top

    old = st_ref[0]
    top = lax.fori_loop(0, chunks, score, old)
    top = jnp.broadcast_to(jnp.max(top, axis=0, keepdims=True), top.shape)
    fade = jnp.exp2(old - top)

    def gather(c, carry):
        total, dotted = carry
        _, real = chosen(c)
        for i in range(PACK):
            at = pl.ds(pl.multiple_of(c * span + i * TILE, TILE), TILE)
            base = jnp.where(real[i], top, HIGH)[0:1]
            e = jnp.exp2(x_ref[at, :] - base)
            total = total + fold(e, jnp.add)
            dotted = dotted + fold(e * dp_ref[at, :], jnp.add)
        return total, dotted

    total, dotted = lax.fori_loop(0, chunks, gather, (st_ref[1] * fade, st_ref[2] * fade))
    total = jnp.sum(total, axis=0, keepdims=True)
    dotted = jnp.sum(dotted, axis=0, keepdims=True)
    level = top[0:1] + jnp.log2(total)
    delta = dotted / total
    fin_ref[0] = jnp.broadcast_to(level, top.shape)
    fin_ref[1] = jnp.broadcast_to(delta, top.shape)
    dq_ref[...] = jnp.zeros_like(dq_ref)

    def spread(c, _):
        picks, real = chosen(c)
        ps, dss = [], []
        for i in range(PACK):
            at = pl.ds(pl.multiple_of(c * span + i * TILE, TILE), TILE)
            p = jnp.exp2(x_ref[at, :] - jnp.where(real[i], level, HIGH))
            ps.append(p.astype(jnp.bfloat16))
            dss.append((p * (dp_ref[at, :] - delta)).astype(jnp.bfloat16))
        p, ds = jnp.concatenate(ps, axis=0), jnp.concatenate(dss, axis=0)
        add_grads(acc_ref, picks, dot(ds, q), dot(p, do))
        dq_ref[...] += dot(take_tiles(kv_ref, 0, picks), ds, TN)
        return 0

    lax.fori_loop(0, chunks, spread, 0)

    @pl.when(b == pl.num_programs(0) - 1)
    def _():
        par = par_ref[0]
        keep_ref[...] = acc_ref[par] * jnp.where(par == 0, inv_root, 1.0)
        send_ref[...] = acc_ref[1 - par] * jnp.where(par == 0, 1.0, inv_root)


def own_grads(
    scale, inv_root, group, list_ref, par_ref, fin_ref, part_ref, q_ref, do_ref, mine_ref, theirs_ref,
    out_ref, keep_ref, send_ref, kv_ref, acc_ref, dq_ref,
):
    b = pl.program_id(0)

    @pl.when(b == 0)
    def _():
        lay_halves(par_ref, mine_ref, theirs_ref, kv_ref)
        acc_ref[...] = jnp.zeros_like(acc_ref)

    count = list_ref[b, SEL]
    q = q_ref[...]
    do = do_ref[...]
    dq_ref[...] = part_ref[...]
    level = fin_ref[0][0:1]
    delta = fin_ref[1][0:1]

    def spread(c, _):
        picks = [list_ref[b, c * PACK + i] for i in range(PACK)]
        keys = take_tiles(kv_ref, 0, picks)
        x = dot(keys, q, NT) * scale
        dp = dot(take_tiles(kv_ref, 1, picks), do, NT)
        ps, dss = [], []
        for i in range(PACK):
            xi = x[i * TILE : (i + 1) * TILE]
            if i == 0:
                xi = mask_diagonal(xi, c == 0, group)
            p = jnp.exp2(xi - jnp.where(c * PACK + i < count, level, HIGH))
            ps.append(p.astype(jnp.bfloat16))
            dss.append((p * (dp[i * TILE : (i + 1) * TILE] - delta)).astype(jnp.bfloat16))
        p, ds = jnp.concatenate(ps, axis=0), jnp.concatenate(dss, axis=0)
        add_grads(acc_ref, picks, dot(ds, q), dot(p, do))
        dq_ref[...] += dot(keys, ds, TN)
        return 0

    lax.fori_loop(0, pl.cdiv(count, PACK), spread, 0)
    out_ref[...] = (dq_ref[...].T * inv_root).astype(out_ref.dtype)

    @pl.when(b == pl.num_programs(0) - 1)
    def _():
        par = par_ref[0]
        keep_ref[...] = acc_ref[par] * jnp.where(par == 0, inv_root, 1.0)
        send_ref[...] = acc_ref[1 - par] * jnp.where(par == 0, 1.0, inv_root)


def join_grads(home_ref, keep_ref, other_ref, came_ref, out_ref, acc_ref):
    acc_ref[...] = keep_ref[...] + other_ref[...]
    for i in range(home_ref.shape[0]):
        t = home_ref[i]

        @pl.when(t >= 0)
        def _():
            acc_ref[tile_rows(t), :] += came_ref[pl.ds(i * TILE, TILE), :].astype(jnp.float32)

    out_ref[...] = acc_ref[...].astype(out_ref.dtype)


def before(flags):
    n = flags.shape[1]
    earlier = jnp.arange(n)[None, :] < jnp.arange(n)[:, None]
    return jnp.sum((flags[:, None, :] & earlier[None]).astype(jnp.int32), axis=2)


def packed_list(flags, values):
    place = before(flags)
    slots = jnp.arange(SEL)
    hit = flags[:, :, None] & (place[:, :, None] == slots[None, None, :])
    packed = jnp.sum(jnp.where(hit, values[:, :, None], 0), axis=1)
    return jnp.concatenate([packed, jnp.sum(flags.astype(jnp.int32), axis=1, keepdims=True)], axis=1)


def whole(shape):
    return pl.BlockSpec(shape, lambda b, *_: (0,) * len(shape), pipeline_mode=pl.Buffered(1))


def on_device(queries, keyvals, selected, d_out):
    tok_rows, heads, dim = queries.shape
    blocks = tok_rows // TILE
    shards = lax.axis_size("seq")
    me = lax.axis_index("seq")
    par = (lax.axis_index("head") % 2).astype(jnp.int32).reshape(1)
    inv_root = dim**-0.5
    scale = inv_root / math.log(2.0)
    rows = TILE * heads
    far = shards * CAP
    f32 = jnp.float32

    mine = keyvals[:, 0, :]
    theirs = swap_pair(mine)

    owner = selected // blocks
    matches = selected[:, :, None] == jnp.arange(shards * blocks)[None, None, :]
    wanted = jnp.any(matches, axis=(0, 1)).reshape(shards, blocks)
    wanted = wanted & (jnp.arange(shards) != me)[:, None]
    rank = before(wanted)
    spots = jnp.arange(CAP)
    placed = wanted[:, :, None] & (rank[:, :, None] == spots[None, None, :])
    asked = jnp.sum(jnp.where(placed, jnp.arange(1, blocks + 1)[None, :, None], 0), axis=1) - 1
    home = lax.all_to_all(asked, "seq", split_axis=0, concat_axis=0, tiled=True).reshape(far)
    reply = mine.reshape(blocks, TILE, dim)[jnp.clip(home, 0, blocks - 1)].reshape(far * TILE, dim)
    far_mine = lax.all_to_all(reply, "seq", split_axis=0, concat_axis=0, tiled=True)
    far_theirs = swap_pair(far_mine)

    sel = jnp.concatenate([selected[:, 1:2], selected[:, :1], selected[:, 2:]], axis=1)
    slots = jnp.arange(SEL)
    repeats = (sel[:, :, None] == sel[:, None, :]) & (slots[None, :] < slots[:, None])[None]
    live = jnp.logical_not(jnp.any(repeats, axis=2))
    sel_owner = sel // blocks
    hits = sel[:, :, None] == jnp.arange(shards * blocks)[None, None, :]
    rank_of = jnp.sum(jnp.where(hits, rank.reshape(-1)[None, None, :], 0), axis=2)
    own_list = packed_list(live & (sel_owner == me), sel % blocks)
    far_list = packed_list(live & (sel_owner != me), sel_owner * CAP + rank_of)

    q2 = queries.reshape(blocks * rows, dim)
    do2 = d_out.reshape(blocks * rows, dim)
    blk = pl.BlockSpec((rows, dim), lambda b, *_: (b, 0))
    stat = pl.BlockSpec((None, 3, 8, rows), lambda b, *_: (b, 0, 0, 0))
    fin = pl.BlockSpec((None, 2, 8, rows), lambda b, *_: (b, 0, 0, 0))
    part = pl.BlockSpec((None, dim, rows), lambda b, *_: (b, 0, 0))
    params = pltpu.CompilerParams(
        dimension_semantics=("arbitrary",), vmem_limit_bytes=40 * 1024 * 1024
    )
    one = 2 * rows * TILE * dim

    stats = pl.pallas_call(
        functools.partial(own_stats, scale, heads),
        out_shape=jax.ShapeDtypeStruct((blocks, 3, 8, rows), f32),
        grid_spec=pltpu.PrefetchScalarGridSpec(
            num_scalar_prefetch=2,
            grid=(blocks,),
            in_specs=[blk, blk, whole((tok_rows, dim)), whole((tok_rows, dim))],
            out_specs=stat,
            scratch_shapes=[pltpu.VMEM((2, tok_rows, dim), jnp.bfloat16)],
        ),
        compiler_params=params,
        cost_estimate=pl.CostEstimate(
            flops=2 * one * blocks * 8, bytes_accessed=2 * tok_rows * heads * dim * 2, transcendentals=0
        ),
        name="own_stats",
    )(own_list, par, q2, do2, mine, theirs)

    final, dq_part, far_keep, far_send = pl.pallas_call(
        functools.partial(far_grads, scale, inv_root),
        out_shape=(
            jax.ShapeDtypeStruct((blocks, 2, 8, rows), f32),
            jax.ShapeDtypeStruct((blocks, dim, rows), f32),
            jax.ShapeDtypeStruct((far * TILE, dim), f32),
            jax.ShapeDtypeStruct((far * TILE, dim), f32),
        ),
        grid_spec=pltpu.PrefetchScalarGridSpec(
            num_scalar_prefetch=2,
            grid=(blocks,),
            in_specs=[stat, blk, blk, whole((far * TILE, dim)), whole((far * TILE, dim))],
            out_specs=(fin, part, whole((far * TILE, dim)), whole((far * TILE, dim))),
            scratch_shapes=[
                pltpu.VMEM((2, far * TILE, dim), jnp.bfloat16),
                pltpu.VMEM((2, far * TILE, dim), f32),
                pltpu.VMEM((MOST_FAR * TILE, rows), f32),
                pltpu.VMEM((MOST_FAR * TILE, rows), f32),
            ],
        ),
        compiler_params=params,
        cost_estimate=pl.CostEstimate(
            flops=5 * one * blocks * 6, bytes_accessed=4 * tok_rows * heads * dim * 2, transcendentals=0
        ),
        name="far_grads",
    )(far_list, par, stats, q2, do2, far_mine, far_theirs)

    back = (far_keep + swap_pair(far_send)).astype(jnp.bfloat16)
    came = lax.all_to_all(back, "seq", split_axis=0, concat_axis=0, tiled=True)

    grad_q, own_keep, own_send = pl.pallas_call(
        functools.partial(own_grads, scale, inv_root, heads),
        out_shape=(
            jax.ShapeDtypeStruct((blocks * rows, dim), jnp.bfloat16),
            jax.ShapeDtypeStruct((tok_rows, dim), f32),
            jax.ShapeDtypeStruct((tok_rows, dim), f32),
        ),
        grid_spec=pltpu.PrefetchScalarGridSpec(
            num_scalar_prefetch=2,
            grid=(blocks,),
            in_specs=[fin, part, blk, blk, whole((tok_rows, dim)), whole((tok_rows, dim))],
            out_specs=(blk, whole((tok_rows, dim)), whole((tok_rows, dim))),
            scratch_shapes=[
                pltpu.VMEM((2, tok_rows, dim), jnp.bfloat16),
                pltpu.VMEM((2, tok_rows, dim), f32),
                pltpu.VMEM((dim, rows), f32),
            ],
        ),
        compiler_params=params,
        cost_estimate=pl.CostEstimate(
            flops=5 * one * blocks * 8, bytes_accessed=5 * tok_rows * heads * dim * 2, transcendentals=0
        ),
        name="own_grads",
    )(own_list, par, final, dq_part, q2, do2, mine, theirs)

    other = swap_pair(own_send)
    grad_kv = pl.pallas_call(
        join_grads,
        out_shape=jax.ShapeDtypeStruct((tok_rows, dim), jnp.bfloat16),
        in_specs=[pl.BlockSpec(memory_space=pltpu.SMEM)] + [pl.BlockSpec(memory_space=pltpu.VMEM)] * 3,
        out_specs=pl.BlockSpec(memory_space=pltpu.VMEM),
        scratch_shapes=[pltpu.VMEM((tok_rows, dim), f32)],
        name="join_grads",
    )(home, own_keep, other, came)
    return (grad_q.reshape(tok_rows, heads, dim), grad_kv.reshape(tok_rows, 1, dim))


def solution(mesh):
    in_specs = (
        P("seq", "head", None),
        P("seq", "head", None),
        P("seq", None),
        P("seq", "head", None),
    )
    out_specs = (P("seq", "head", None), P("seq", "head", None))
    return jax.shard_map(
        on_device, mesh=mesh, in_specs=in_specs, out_specs=out_specs, check_vma=False
    )
```

time: 295 us -> 121 us (0.41)
  matrix products: 85.7 us -> 0 us
  other arithmetic: 63.7 us -> 4.93 us
  waiting for transfers between devices: 61.6 us -> 16.7 us
  local copies, waits for them, and re-layouts: 62.3 us -> 18.7 us
  Pallas kernels: 0 us -> 42.1 us
  starting transfers between devices: 15.3 us -> 36.8 us
  loops' own time: 3.38 us -> 0 us
    dot_general x16 -> x0, matrix products: 51.7 us -> none  [the longest x4 21.4 us: attend_tiles(): jnp.einsum('gqhd,gnd->ghqn', dout_blk, value_sel, preferred_element_type=...]
    all_to_all x3, waiting for transfers between devices: 59.7 us -> 13.7 us  [the longest x1 9.04 us: on_device(): lax.all_to_all(reply, 'seq', split_axis=0, concat_axis=0, tiled=True)]
    pallas_call x0 -> x4, Pallas kernels: none -> 42.1 us  [the longest x1 23.2 us: on_device(): pl.pallas_call(functools.partial(own_grads, scale, inv_root, heads), out_...]
    scatter-add x5 -> x0, other arithmetic: 41.9 us -> none  [the longest x4 35.1 us: step(): totals = totals.at[slot_sel].add(slot_grads)]
    sub x4 -> x0, matrix products: 34 us -> none  [attend_tiles(): raised = jnp.where(allowed, jnp.exp(masked - row_max), 0.0)]
    all_to_all x3, starting transfers between devices: 14.7 us -> 35.7 us  [the longest x1 25.3 us: on_device(): came = lax.all_to_all(back, 'seq', split_axis=0, concat_axis=0, tiled=True)]
    gather x9 -> x1, local copies, waits for them, and re-layouts: 18.7 us -> 2.3 us  [on_device(): mine.reshape(blocks, TILE, dim)[jnp.clip(home, 0, blocks - 1)]]
    unnamed x6 -> x26, local copies, waits for them, and re-layouts: 0.01 us -> 12.5 us
  transfers between devices with their start and end apart: 5 -> 7, of which waited for: 4 -> 4; matrix products, arithmetic and copies ran while one was open for 2% -> 9% of each run, Pallas kernels for 0% -> 31%
where the time goes in v1:
time: 121 us; the launch traced here: 120 us
  Pallas kernels  42.1 us (35%)
  starting transfers between devices  36.8 us (30%)
  local copies, waits for them, and re-layouts  18.7 us (15%)
  waiting for transfers between devices  16.7 us (14%)
  other arithmetic  4.93 us (4%)
    all_to_all x1, starting transfers between devices, on_device(): came = lax.all_to_all(back, 'seq', split_axis=0, concat_axis=0, tiled=True)  25.3 us
    pallas_call x1, Pallas kernels, on_device(): pl.pallas_call(functools.partial(own_grads, scale, inv_root, heads), out_...  23.2 us
    pallas_call x1, Pallas kernels, on_device(): pl.pallas_call(functools.partial(own_stats, scale, heads), out_shape=jax....  14.1 us
    unnamed x26, local copies, waits for them, and re-layouts  12.5 us
    all_to_all x1, waiting for transfers between devices, on_device(): lax.all_to_all(reply, 'seq', split_axis=0, concat_axis=0, tiled=True)  9.04 us
    all_to_all x1, starting transfers between devices, on_device(): lax.all_to_all(asked, 'seq', split_axis=0, concat_axis=0, tiled=True)  6.86 us
    all_to_all x1, waiting for transfers between devices, on_device(): lax.all_to_all(asked, 'seq', split_axis=0, concat_axis=0, tiled=True)  4.61 us
    all_to_all x1, starting transfers between devices, on_device(): lax.all_to_all(reply, 'seq', split_axis=0, concat_axis=0, tiled=True)  3.45 us
  transfers between devices with their start and end apart: 7, of which 4 were waited for; matrix products, arithmetic and copies ran while one was open for 9% of the time, Pallas kernels for 31%

profile of v1, /device:TPU:0, one launch (start us, length us, event | category | flops | bytes accessed | tf_op | source)
XLA Modules:
  0.0 120.0 jit_solution(1793266779218257733)
XLA Ops:
  1.2 0.8 fusion.2
  3.2 6.9 %all-to-all-start = ((s32[8,1,3]{2,1,0:T(1,128)}), s32[8,1,3]{2,1,0:T(1,128)S(1)}, u32[]{:S(2)}, u32[]{:S(2)}) async-start(s32[8,1,3]{2,1,0:T(1,128)} %copy.19), calls=%async_computation | async-start | bytes 8192 | tf_op jit(solution)/shard_map/all_to_all | solution.py:287
  10.1 0.8 fusion.8
  11.9 4.6 %all-to-all-done = s32[8,1,3]{2,1,0:T(1,128)S(1)} async-done(((s32[8,1,3]{2,1,0:T(1,128)}), s32[8,1,3]{2,1,0:T(1,128)S(1)}, u32[]{:S(2)}, u32[]{:S(2)}) %all-to-all-start) | async-done | bytes 128 | tf_op jit(solution)/shard_map/all_to_all | solution.py:287
  17.8 2.3 %gather_fusion = bf16[24,64,128]{2,1,0:T(8,128)(2,1)} fusion(bf16[16,64,128]{2,1,0:T(8,128)(2,1)} %bitcast.18, s32[1024]{0:T(1024)S(1)} %pad_clamp_fusion), kind=kCustom, calls=%fused_computation | custom fusion | bytes 786528 | tf_op jit(solution)/shard_map/gather | solution.py:288
  20.1 3.5 %all-to-all-start.1 = ((bf16[8,192,128]{2,1,0:T(8,128)(2,1)}), bf16[8,192,128]{2,1,0:T(8,128)(2,1)S(1)}, u32[]{:S(2)}, u32[]{:S(2)}) async-start(bf16[8,192,128]{2,1,0:T(8,128)(2,1)} %bitcast.9), calls=%async_computation.1 | async-start | bytes 786432 | tf_op jit(solution)/shard_map/all_to_all | solution.py:289
  25.6 9.0 %all-to-all-done.1 = bf16[8,192,128]{2,1,0:T(8,128)(2,1)S(1)} async-done(((bf16[8,192,128]{2,1,0:T(8,128)(2,1)}), bf16[8,192,128]{2,1,0:T(8,128)(2,1)S(1)}, u32[]{:S(2)}, u32[]{:S(2)}) %all-to-all-start.1) | async-done | bytes 393248 | tf_op jit(solution)/shard_map/all_to_all | solution.py:289
  34.8 1.0 copy-done
  35.8 1.6 %copy-done.3 = bf16[1024,8,128]{2,1,0:T(8,128)(2,1)S(1)} copy-done((bf16[1024,8,128]{2,1,0:T(8,128)(2,1)S(1)}, bf16[1024,8,128]{2,1,0:T(8,128)(2,1)}, u32[]{:S(2)}) %copy-start.3) | copy-done | bytes 2097176
  37.4 1.6 %copy-done.5 = bf16[1024,8,128]{2,1,0:T(8,128)(2,1)S(1)} copy-done((bf16[1024,8,128]{2,1,0:T(8,128)(2,1)S(1)}, bf16[1024,8,128]{2,1,0:T(8,128)(2,1)}, u32[]{:S(2)}) %copy-start.5) | copy-done | bytes 2097176
  39.0 14.1 %own_stats.1.st_ref = f32[16,3,8,512]{3,2,1,0:T(8,128)S(1)} custom-call(s32[16,17]{1,0:T(8,128)S(1)} %pad_add_fusion.1.list_ref, s32[1]{0:T(128)} %bitcast.1.par_ref, bf16[8192,128]{1,0:T(8,128)(2,1)S(1)} %bitcast.23, bf16[8192,128]{1,0:T(8,128)(2,1)S(1)} %bitcast.26, bf16[1024,128]{1,0:T(8,128)(2,1)S(1)} %bitcast.19, ...), custom_call_target="tpu_custom_call" | custom-call | flops 2147483648 | bytes 4194304 | tf_op jit(solution)/shard_map/own_stats/pallas_call | solution.py:313
  53.1 2.5 %far_grads.1 = (f32[16,2,8,512]{3,2,1,0:T(8,128)S(1)}, f32[16,128,512]{2,1,0:T(8,128)S(1)}, f32[1536,128]{1,0:T(8,128)S(1)}, f32[1536,128]{1,0:T(8,128)S(1)}) custom-call(s32[16,17]{1,0:T(8,128)S(1)} %pad_add_fusion.2.list_ref, s32[1]{0:T(128)} %bitcast.1.par_ref, f32[16,3,8,512]{3,2,1,0:T(8,128)S(1)} %own_stats.1.st_ref, bf16[8192,128]{1,0:T(8,128)(2,1)S(1)} %bitcast.24, ...), custom_call_target="tpu_custom_call" | custom-call | flops 4026531840 | bytes 8388608 | tf_op jit(solution)/shard_map/far_grads/pallas_call | solution.py:330
  55.6 1.9 %copy-done.8 = f32[16,128,512]{2,1,0:T(8,128)} copy-done((f32[16,128,512]{2,1,0:T(8,128)}, f32[16,128,512]{2,1,0:T(8,128)S(1)}, u32[]{:S(2)}) %copy-start.8) | copy-done | bytes 4194328
  58.1 1.9 %collective-permute-done.3 = f32[1536,128]{1,0:T(8,128)S(1)} collective-permute-done((f32[1536,128]{1,0:T(8,128)S(1)}, f32[1536,128]{1,0:T(8,128)S(1)}, u32[]{:S(2)}, u32[]{:S(2)}) %collective-permute-start.3) | collective-permute-done | bytes 786464 | tf_op jit(solution)/shard_map/ppermute | solution.py:24
  60.0 0.8 add_convert_fusion
  60.8 25.3 %all-to-all-start.2 = ((bf16[8,192,128]{2,1,0:T(8,128)(2,1)}), bf16[8,192,128]{2,1,0:T(8,128)(2,1)}, u32[]{:S(2)}, u32[]{:S(2)}) async-start(bf16[8,192,128]{2,1,0:T(8,128)(2,1)} %bitcast.29), calls=%async_computation.2 | async-start | bytes 786432 | tf_op jit(solution)/shard_map/all_to_all | solution.py:358
  86.2 1.6 %copy-done.7 = bf16[1024,8,128]{2,1,0:T(8,128)(2,1)S(1)} copy-done((bf16[1024,8,128]{2,1,0:T(8,128)(2,1)S(1)}, bf16[1024,8,128]{2,1,0:T(8,128)(2,1)}, u32[]{:S(2)}) %copy-start.7) | copy-done | bytes 2097176
  87.8 2.2 %copy-done.9 = f32[16,128,512]{2,1,0:T(8,128)S(1)} copy-done((f32[16,128,512]{2,1,0:T(8,128)S(1)}, f32[16,128,512]{2,1,0:T(8,128)}, u32[]{:S(2)}) %copy-start.9) | copy-done | bytes 4194328
  89.9 1.0 copy-done.11
  91.0 23.2 %own_grads.1 = (bf16[8192,128]{1,0:T(8,128)(2,1)}, f32[1024,128]{1,0:T(8,128)S(1)}, f32[1024,128]{1,0:T(8,128)S(1)}) custom-call(s32[16,17]{1,0:T(8,128)S(1)} %pad_add_fusion.1.list_ref, s32[1]{0:T(128)} %bitcast.1.par_ref, f32[16,2,8,512]{3,2,1,0:T(8,128)S(1)} %copy-done.11, f32[16,128,512]{2,1,0:T(8,128)S(1)} %copy-done.9, bf16[8192,128]{1,0:T(8,128)(2,1)S(1)} %bitcast.25, ...), custom_call_target="tpu_custom_call" | custom-call | flops 5368709120 | bytes 10485760 | tf_op jit(solution)/shard_map/own_grads/pallas_call | solution.py:360
  114.1 0.8 copy-done.2
  115.7 1.2 collective-permute-done.2.other_ref
  116.8 0.8 copy-done.12
  117.7 2.3 %join_grads.1 = bf16[1024,128]{1,0:T(8,128)(2,1)} custom-call(s32[24]{0:T(128)} %reshape.520.home_ref, f32[1024,128]{1,0:T(8,128)} %copy-done.2, f32[1024,128]{1,0:T(8,128)} %copy-done.12, bf16[1536,128]{1,0:T(8,128)(2,1)} %bitcast.13.came_ref), custom_call_target="tpu_custom_call" | custom-call | tf_op jit(solution)/shard_map/join_grads/pallas_call | solution.py:386
  (51 shorter events, 7.5 us)
Async XLA Ops:
  0.6 34.2 %collective-permute-start = (bf16[1024,128]{1,0:T(8,128)(2,1)}, bf16[1024,128]{1,0:T(8,128)(2,1)S(1)}, u32[]{:S(2)}, u32[]{:S(2)}) collective-permute-start(bf16[1024,128]{1,0:T(8,128)(2,1)} %bitcast.17), channel_id=1, source_target_pairs={{0,1},{1,0},{2,3},{3,2},{4,5},{5,4},{6,7},{7,6},{8,9},{9,8},{10,11... | collective-permute-start | bytes 786440 | tf_op jit(solution)/shard_map/ppermute | solution.py:24
  3.2 13.2 %all-to-all-start = ((s32[8,1,3]{2,1,0:T(1,128)}), s32[8,1,3]{2,1,0:T(1,128)S(1)}, u32[]{:S(2)}, u32[]{:S(2)}) async-start(s32[8,1,3]{2,1,0:T(1,128)} %copy.19), calls=%async_computation | async-start | bytes 8192 | tf_op jit(solution)/shard_map/all_to_all | solution.py:287
  20.1 14.6 %all-to-all-start.1 = ((bf16[8,192,128]{2,1,0:T(8,128)(2,1)}), bf16[8,192,128]{2,1,0:T(8,128)(2,1)S(1)}, u32[]{:S(2)}, u32[]{:S(2)}) async-start(bf16[8,192,128]{2,1,0:T(8,128)(2,1)} %bitcast.9), calls=%async_computation.1 | async-start | bytes 786432 | tf_op jit(solution)/shard_map/all_to_all | solution.py:289
  34.7 18.4 %collective-permute-start.1 = (bf16[1536,128]{1,0:T(8,128)(2,1)S(1)}, bf16[1536,128]{1,0:T(8,128)(2,1)S(1)}, u32[]{:S(2)}, u32[]{:S(2)}) collective-permute-start(bf16[1536,128]{1,0:T(8,128)(2,1)S(1)} %bitcast.21), channel_id=1, source_target_pairs={{0,1},{1,0},{2,3},{3,2},{4,5},{5,4},{6,7},{7,6},{8,9},{9,8},{10,11... | collective-permute-start | bytes 1179656 | tf_op jit(solution)/shard_map/ppermute | solution.py:24
  34.8 1.0 copy-start
  35.8 1.6 %copy-start.3 = (bf16[1024,8,128]{2,1,0:T(8,128)(2,1)S(1)}, bf16[1024,8,128]{2,1,0:T(8,128)(2,1)}, u32[]{:S(2)}) copy-start(bf16[1024,8,128]{2,1,0:T(8,128)(2,1)} %param.4) | copy-start | bytes 6291460
  37.4 1.6 %copy-start.5 = (bf16[1024,8,128]{2,1,0:T(8,128)(2,1)S(1)}, bf16[1024,8,128]{2,1,0:T(8,128)(2,1)}, u32[]{:S(2)}) copy-start(bf16[1024,8,128]{2,1,0:T(8,128)(2,1)} %param.7) | copy-start | bytes 6291460
  39.0 14.1 %copy-start.4 = (bf16[1024,8,128]{2,1,0:T(8,128)(2,1)S(1)}, bf16[1024,8,128]{2,1,0:T(8,128)(2,1)}, u32[]{:S(2)}) copy-start(bf16[1024,8,128]{2,1,0:T(8,128)(2,1)} %param.4) | copy-start | bytes 6291460
  39.0 14.1 %copy-start.6 = (bf16[1024,8,128]{2,1,0:T(8,128)(2,1)S(1)}, bf16[1024,8,128]{2,1,0:T(8,128)(2,1)}, u32[]{:S(2)}) copy-start(bf16[1024,8,128]{2,1,0:T(8,128)(2,1)} %param.7) | copy-start | bytes 6291460
  55.6 1.9 %copy-start.8 = (f32[16,128,512]{2,1,0:T(8,128)}, f32[16,128,512]{2,1,0:T(8,128)S(1)}, u32[]{:S(2)}) copy-start(f32[16,128,512]{2,1,0:T(8,128)S(1)} %get-tuple-element.10.part_ref) | copy-start | bytes 12582916
  57.5 28.6 %copy-start.10 = (f32[16,2,8,512]{3,2,1,0:T(8,128)}, f32[16,2,8,512]{3,2,1,0:T(8,128)S(1)}, u32[]{:S(2)}) copy-start(f32[16,2,8,512]{3,2,1,0:T(8,128)S(1)} %get-tuple-element.9.fin_ref) | copy-start | bytes 1572868
  57.5 28.6 %copy-start.1 = (bf16[1024,1,128]{2,0,1:T(8,128)(2,1)S(1)}, bf16[1024,1,128]{2,0,1:T(8,128)(2,1)}, u32[]{:S(2)}) copy-start(bf16[1024,1,128]{2,0,1:T(8,128)(2,1)} %param.5) | copy-start | bytes 786436
  57.6 2.4 %collective-permute-start.3 = (f32[1536,128]{1,0:T(8,128)S(1)}, f32[1536,128]{1,0:T(8,128)S(1)}, u32[]{:S(2)}, u32[]{:S(2)}) collective-permute-start(f32[1536,128]{1,0:T(8,128)S(1)} %get-tuple-element.15), channel_id=1, source_target_pairs={{0,1},{1,0},{2,3},{3,2},{4,5},{5,4},{6,7},{7,6},{8,9},{9,8},{10,11... | collective-permute-start | bytes 2359304 | tf_op jit(solution)/shard_map/ppermute | solution.py:24
  60.8 56.0 %all-to-all-start.2 = ((bf16[8,192,128]{2,1,0:T(8,128)(2,1)}), bf16[8,192,128]{2,1,0:T(8,128)(2,1)}, u32[]{:S(2)}, u32[]{:S(2)}) async-start(bf16[8,192,128]{2,1,0:T(8,128)(2,1)} %bitcast.29), calls=%async_computation.2 | async-start | bytes 786432 | tf_op jit(solution)/shard_map/all_to_all | solution.py:358
  86.2 1.6 %copy-start.7 = (bf16[1024,8,128]{2,1,0:T(8,128)(2,1)S(1)}, bf16[1024,8,128]{2,1,0:T(8,128)(2,1)}, u32[]{:S(2)}) copy-start(bf16[1024,8,128]{2,1,0:T(8,128)(2,1)} %param.7) | copy-start | bytes 6291460
  87.7 2.2 %copy-start.9 = (f32[16,128,512]{2,1,0:T(8,128)S(1)}, f32[16,128,512]{2,1,0:T(8,128)}, u32[]{:S(2)}) copy-start(f32[16,128,512]{2,1,0:T(8,128)} %copy-done.8) | copy-start | bytes 12582916
  89.9 1.0 copy-start.11
  114.1 0.8 copy-start.2
  114.9 1.9 %collective-permute-start.2 = (f32[1024,128]{1,0:T(8,128)S(1)}, f32[1024,128]{1,0:T(8,128)S(1)}, u32[]{:S(2)}, u32[]{:S(2)}) collective-permute-start(f32[1024,128]{1,0:T(8,128)S(1)} %get-tuple-element.13), channel_id=1, source_target_pairs={{0,1},{1,0},{2,3},{3,2},{4,5},{5,4},{6,7},{7,6},{8,9},{9,8},{10,11... | collective-permute-start | bytes 1572872 | tf_op jit(solution)/shard_map/ppermute | solution.py:24
  116.8 0.8 copy-start.12

commit v2 on v1

v2 whole, which is shorter than its diff:
```python
import functools
import math

import jax
import jax.numpy as jnp
from jax import lax
from jax.experimental import pallas as pl
from jax.experimental.pallas import tpu as pltpu
from jax.sharding import PartitionSpec as P

TILE = 64
SEL = 16
CAP = 3
WIDE = 8
OWN_SIZES = (2, 4, 6)
FAR_SIZES = (4, 7, 8)
STEP = 2
LOW = -1e30
HIGH = 1e30
RISE = 64.0
NT = (((1,), (1,)), ((), ()))
TN = (((0,), (0,)), ((), ()))


def swap_pair(block):
    count = lax.axis_size("head")
    return lax.ppermute(block, "head", [(h, h ^ 1) for h in range(count)])


def tile_rows(index):
    return pl.ds(pl.multiple_of(index * TILE, TILE), TILE)


def span(index, size):
    return pl.ds(pl.multiple_of(index * size, size), size)


def dot(a, b, dims=(((1,), (0,)), ((), ()))):
    return lax.dot_general(a, b, dims, preferred_element_type=jnp.float32)


def fold(x, op):
    parts = [x[8 * i : 8 * i + 8] for i in range(TILE // 8)]
    while len(parts) > 1:
        parts = [op(parts[i], parts[i + 1]) for i in range(0, len(parts), 2)]
    return parts[0]


def mask_diagonal(x, is_first, group):
    key = lax.broadcasted_iota(jnp.int32, (TILE, x.shape[1]), 0)
    query = lax.broadcasted_iota(jnp.int32, (TILE, x.shape[1]), 1) // group
    return jnp.where((key <= query) | jnp.logical_not(is_first), x, LOW)


def lay_halves(par_ref, mine_ref, theirs_ref, kv_ref):
    par = par_ref[0]
    kv_ref[par] = mine_ref[...]
    kv_ref[1 - par] = theirs_ref[...]


def each_block(body):
    def run(j, _):
        body(pl.program_id(0) * STEP + j, j)
        return 0

    lax.fori_loop(0, STEP, run, 0)


def pick(list_ref, b, start, size):
    count = list_ref[b, SEL]
    return (
        [list_ref[b, start + i] for i in range(size)],
        [start + i < count for i in range(size)],
    )


def part(i):
    return slice(i * TILE, (i + 1) * TILE)


def load_tiles(kv_ref, k_ref, v_ref, picks):
    for i, t in enumerate(picks):
        k_ref[part(i)] = kv_ref[0, tile_rows(t), :]
        v_ref[part(i)] = kv_ref[1, tile_rows(t), :]


def by_size(left, sizes, run):
    for low, size in zip((0,) + sizes[:-1], sizes, strict=True):

        @pl.when((left > low) & (left <= size))
        def _():
            run(size)


def in_parts(count, run):
    wide = (count + 1) // WIDE

    def full(c, _):
        run(c * WIDE, WIDE)
        return 0

    lax.fori_loop(0, wide, full, 0)
    by_size(count - wide * WIDE, OWN_SIZES, lambda size: run(wide * WIDE, size))


def own_stats(
    scale, group, list_ref, par_ref, q_ref, do_ref, mine_ref, theirs_ref, st_ref, kv_ref, k_ref, v_ref
):
    rows = q_ref.shape[0] // STEP

    @pl.when(pl.program_id(0) == 0)
    def _():
        lay_halves(par_ref, mine_ref, theirs_ref, kv_ref)

    def block(b, j):
        zero = jnp.zeros((8, rows), jnp.float32)
        st_ref[j, 0] = jnp.full((8, rows), LOW, jnp.float32)
        st_ref[j, 1] = zero
        st_ref[j, 2] = zero

        def run(start, size):
            picks, real = pick(list_ref, b, start, size)
            load_tiles(kv_ref, k_ref, v_ref, picks)
            x = dot(k_ref[: size * TILE], q_ref[span(j, rows), :], NT) * scale
            xs = [x[part(i)] for i in range(size)]
            xs[0] = mask_diagonal(xs[0], start == 0, group)
            top = st_ref[j, 0]
            new = top
            for i in range(size):
                new = jnp.maximum(new, jnp.where(real[i], fold(xs[i], jnp.maximum), LOW))
            new = jnp.broadcast_to(jnp.max(new, axis=0, keepdims=True), new.shape)
            fade = jnp.exp2(top - new)
            total, dotted = st_ref[j, 1] * fade, st_ref[j, 2] * fade
            dp = dot(v_ref[: size * TILE], do_ref[span(j, rows), :], NT)
            for i in range(size):
                base = jnp.where(real[i], new, HIGH)[0:1]
                e = jnp.exp2(xs[i] - base)
                total = total + fold(e, jnp.add)
                dotted = dotted + fold(e * dp[part(i)], jnp.add)
            st_ref[j, 0] = new
            st_ref[j, 1] = total
            st_ref[j, 2] = dotted

        in_parts(list_ref[b, SEL], run)

    each_block(block)


def add_grads(acc_ref, picks, gk, gv):
    for i, t in enumerate(picks):
        acc_ref[0, tile_rows(t), :] += gk[part(i)]
        acc_ref[1, tile_rows(t), :] += gv[part(i)]


def leave_grads(inv_root, par_ref, acc_ref, keep_ref, send_ref):
    @pl.when(pl.program_id(0) == pl.num_programs(0) - 1)
    def _():
        par = par_ref[0]
        keep = acc_ref[par] * jnp.where(par == 0, inv_root, 1.0)
        send = acc_ref[1 - par] * jnp.where(par == 0, 1.0, inv_root)
        keep_ref[...] = keep.astype(keep_ref.dtype)
        send_ref[...] = send.astype(send_ref.dtype)


def far_grads(
    scale, inv_root, list_ref, par_ref, st_ref, q_ref, do_ref, mine_ref, theirs_ref,
    fin_ref, dq_ref, keep_ref, send_ref,
    kv_ref, acc_ref, e_ref, dp_ref, sum_ref, k_ref, v_ref, p_ref, ds_ref,
):
    rows = q_ref.shape[0] // STEP

    @pl.when(pl.program_id(0) == 0)
    def _():
        lay_halves(par_ref, mine_ref, theirs_ref, kv_ref)
        acc_ref[...] = jnp.zeros_like(acc_ref)

    def block(b, j):
        count = list_ref[b, SEL]
        q_at = span(j, rows)

        def read(start, size):
            picks, real = pick(list_ref, b, start, size)
            load_tiles(kv_ref, k_ref, v_ref, picks)
            x = dot(k_ref[: size * TILE], q_ref[q_at, :], NT) * scale
            dp = dot(v_ref[: size * TILE], do_ref[q_at, :], NT)
            base, total, dotted, top = sum_ref[0], sum_ref[1], sum_ref[2], sum_ref[3]
            for i in range(size):
                to = tile_rows(start + i)
                top = jnp.maximum(top, jnp.where(real[i], fold(x[part(i)], jnp.maximum), LOW))
                e = jnp.exp2(x[part(i)] - jnp.where(real[i], base, HIGH)[0:1])
                e_ref[to, :] = e
                dp_ref[to, :] = dp[part(i)]
                total = total + fold(e, jnp.add)
                dotted = dotted + fold(e * dp[part(i)], jnp.add)
            sum_ref[1], sum_ref[2], sum_ref[3] = total, dotted, top

        old = st_ref[j, 0]
        sum_ref[0] = old
        sum_ref[1] = st_ref[j, 1]
        sum_ref[2] = st_ref[j, 2]
        sum_ref[3] = old
        by_size(count, FAR_SIZES, lambda size: read(0, size))

        @pl.when(jnp.max(sum_ref[3] - old) > RISE)
        def _():
            best = jnp.broadcast_to(jnp.max(sum_ref[3], axis=0, keepdims=True), old.shape)
            fade = jnp.exp2(old - best)
            sum_ref[0] = best
            sum_ref[1] = st_ref[j, 1] * fade
            sum_ref[2] = st_ref[j, 2] * fade

            def again(c, _):
                read(c * FAR_SIZES[0], FAR_SIZES[0])
                return 0

            lax.fori_loop(0, pl.cdiv(count, FAR_SIZES[0]), again, 0)

        total = jnp.sum(sum_ref[1], axis=0, keepdims=True)
        dotted = jnp.sum(sum_ref[2], axis=0, keepdims=True)
        delta = dotted / total
        ratio = 1.0 / total
        fin_ref[j, 0] = sum_ref[0] + jnp.log2(total)
        fin_ref[j, 1] = jnp.broadcast_to(delta, old.shape)

        @pl.when(count == 0)
        def _():
            dq_ref[j] = jnp.zeros(dq_ref.shape[1:], dq_ref.dtype)

        def spread(size):
            picks, _ = pick(list_ref, b, 0, size)
            n = size * TILE
            for i, t in enumerate(picks):
                k_ref[part(i)] = kv_ref[0, tile_rows(t), :]
                p = e_ref[part(i)] * ratio
                p_ref[part(i)] = p.astype(jnp.bfloat16)
                ds_ref[part(i)] = (p * (dp_ref[part(i)] - delta)).astype(jnp.bfloat16)
            add_grads(acc_ref, picks, dot(ds_ref[:n], q_ref[q_at, :]), dot(p_ref[:n], do_ref[q_at, :]))
            dq_ref[j] = dot(k_ref[:n], ds_ref[:n], TN)

        by_size(count, FAR_SIZES, spread)

    each_block(block)
    leave_grads(inv_root, par_ref, acc_ref, keep_ref, send_ref)


def own_grads(
    scale, inv_root, group, list_ref, par_ref, fin_ref, part_ref, q_ref, do_ref, mine_ref, theirs_ref,
    out_ref, keep_ref, send_ref, kv_ref, acc_ref, dq_ref, k_ref, v_ref, p_ref, ds_ref,
):
    rows = q_ref.shape[0] // STEP

    @pl.when(pl.program_id(0) == 0)
    def _():
        lay_halves(par_ref, mine_ref, theirs_ref, kv_ref)
        acc_ref[...] = jnp.zeros_like(acc_ref)

    def block(b, j):
        q_at = span(j, rows)
        dq_ref[...] = part_ref[j]

        def spread(start, size):
            picks, real = pick(list_ref, b, start, size)
            n = size * TILE
            load_tiles(kv_ref, k_ref, v_ref, picks)
            level = fin_ref[j, 0, 0:1]
            delta = fin_ref[j, 1, 0:1]
            x = dot(k_ref[:n], q_ref[q_at, :], NT) * scale
            dp = dot(v_ref[:n], do_ref[q_at, :], NT)
            for i in range(size):
                xi = mask_diagonal(x[part(i)], start == 0, group) if i == 0 else x[part(i)]
                p = jnp.exp2(xi - jnp.where(real[i], level, HIGH))
                p_ref[part(i)] = p.astype(jnp.bfloat16)
                ds_ref[part(i)] = (p * (dp[part(i)] - delta)).astype(jnp.bfloat16)
            add_grads(acc_ref, picks, dot(ds_ref[:n], q_ref[q_at, :]), dot(p_ref[:n], do_ref[q_at, :]))
            dq_ref[...] += dot(k_ref[:n], ds_ref[:n], TN)

        in_parts(list_ref[b, SEL], spread)
        out_ref[q_at, :] = (dq_ref[...] * inv_root).astype(out_ref.dtype).T

    each_block(block)
    leave_grads(inv_root, par_ref, acc_ref, keep_ref, send_ref)


def fill_reply(home_ref, mine_ref, reply_ref):
    cap = home_ref.shape[2]
    for i in range(home_ref.shape[0] * cap):
        t = jnp.maximum(home_ref[i // cap, 0, i % cap], 0)
        reply_ref[i * TILE : (i + 1) * TILE] = mine_ref[tile_rows(t), :]


def join_grads(home_ref, keep_ref, other_ref, came_ref, out_ref, acc_ref):
    cap = home_ref.shape[2]
    acc_ref[...] = keep_ref[...] + other_ref[...]
    for i in range(home_ref.shape[0] * cap):
        t = home_ref[i // cap, 0, i % cap]

        @pl.when(t >= 0)
        def _():
            acc_ref[tile_rows(t), :] += came_ref[i * TILE : (i + 1) * TILE].astype(jnp.float32)

    out_ref[...] = acc_ref[...].astype(out_ref.dtype)


def before(flags):
    n = flags.shape[1]
    earlier = jnp.arange(n)[None, :] < jnp.arange(n)[:, None]
    return jnp.sum((flags[:, None, :] & earlier[None]).astype(jnp.int32), axis=2)


def packed_list(flags, values):
    place = before(flags)
    slots = jnp.arange(SEL)
    hit = flags[:, :, None] & (place[:, :, None] == slots[None, None, :])
    packed = jnp.sum(jnp.where(hit, values[:, :, None], 0), axis=1)
    return jnp.concatenate([packed, jnp.sum(flags.astype(jnp.int32), axis=1, keepdims=True)], axis=1)


def whole(shape):
    return pl.BlockSpec(shape, lambda b, *_: (0,) * len(shape), pipeline_mode=pl.Buffered(1))


def on_device(queries, keyvals, selected, d_out):
    tok_rows, heads, dim = queries.shape
    blocks = tok_rows // TILE
    shards = lax.axis_size("seq")
    me = lax.axis_index("seq")
    par = (lax.axis_index("head") % 2).astype(jnp.int32).reshape(1)
    inv_root = dim**-0.5
    scale = inv_root / math.log(2.0)
    rows = TILE * heads
    far = shards * CAP
    f32 = jnp.float32

    mine = keyvals[:, 0, :]
    theirs = swap_pair(mine)

    owner = selected // blocks
    matches = selected[:, :, None] == jnp.arange(shards * blocks)[None, None, :]
    wanted = jnp.any(matches, axis=(0, 1)).reshape(shards, blocks)
    wanted = wanted & (jnp.arange(shards) != me)[:, None]
    rank = before(wanted)
    spots = jnp.arange(CAP)
    placed = wanted[:, :, None] & (rank[:, :, None] == spots[None, None, :])
    asked = jnp.sum(jnp.where(placed, jnp.arange(1, blocks + 1)[None, :, None], 0), axis=1) - 1
    home = lax.all_to_all(asked[:, None, :], "seq", split_axis=0, concat_axis=0, tiled=True)
    in_smem = pl.BlockSpec(memory_space=pltpu.SMEM)
    in_vmem = pl.BlockSpec(memory_space=pltpu.VMEM)
    reply = pl.pallas_call(
        fill_reply,
        out_shape=jax.ShapeDtypeStruct((far * TILE, dim), jnp.bfloat16),
        in_specs=[in_smem, in_vmem],
        out_specs=in_vmem,
        compiler_params=pltpu.CompilerParams(vmem_limit_bytes=60 * 1024 * 1024),
        name="fill_reply",
    )(home, mine)
    far_mine = lax.all_to_all(reply, "seq", split_axis=0, concat_axis=0, tiled=True)

    sel = jnp.concatenate([selected[:, 1:2], selected[:, :1], selected[:, 2:]], axis=1)
    slots = jnp.arange(SEL)
    repeats = (sel[:, :, None] == sel[:, None, :]) & (slots[None, :] < slots[:, None])[None]
    live = jnp.logical_not(jnp.any(repeats, axis=2))
    sel_owner = sel // blocks
    hits = sel[:, :, None] == jnp.arange(shards * blocks)[None, None, :]
    rank_of = jnp.sum(jnp.where(hits, rank.reshape(-1)[None, None, :], 0), axis=2)
    own_list = packed_list(live & (sel_owner == me), sel % blocks)
    far_list = packed_list(live & (sel_owner != me), sel_owner * CAP + rank_of)

    q2 = queries.reshape(blocks * rows, dim)
    do2 = d_out.reshape(blocks * rows, dim)
    blk = pl.BlockSpec((STEP * rows, dim), lambda b, *_: (b, 0))
    stat = pl.BlockSpec((STEP, 3, 8, rows), lambda b, *_: (b, 0, 0, 0))
    fin = pl.BlockSpec((STEP, 2, 8, rows), lambda b, *_: (b, 0, 0, 0))
    part_dq = pl.BlockSpec((STEP, dim, rows), lambda b, *_: (b, 0, 0))
    params = pltpu.CompilerParams(
        dimension_semantics=("arbitrary",), vmem_limit_bytes=60 * 1024 * 1024
    )
    one = 2 * rows * TILE * dim
    bf16 = jnp.bfloat16
    own_rows, far_rows = (tok_rows, dim), (far * TILE, dim)
    some_keys = [pltpu.VMEM((WIDE * TILE, dim), bf16)] * 2
    some_probs = [pltpu.VMEM((WIDE * TILE, rows), bf16)] * 2

    stats = pl.pallas_call(
        functools.partial(own_stats, scale, heads),
        out_shape=jax.ShapeDtypeStruct((blocks, 3, 8, rows), f32),
        grid_spec=pltpu.PrefetchScalarGridSpec(
            num_scalar_prefetch=2,
            grid=(blocks // STEP,),
            in_specs=[blk, blk, whole(own_rows), whole(own_rows)],
            out_specs=stat,
            scratch_shapes=[pltpu.VMEM((2,) + own_rows, bf16)] + some_keys,
        ),
        compiler_params=params,
        cost_estimate=pl.CostEstimate(
            flops=2 * one * blocks * 8, bytes_accessed=2 * tok_rows * heads * dim * 2, transcendentals=0
        ),
        name="own_stats",
    )(own_list, par, q2, do2, mine, theirs)

    far_mine, stats = lax.optimization_barrier((far_mine, stats))
    far_theirs = swap_pair(far_mine)

    final, dq_part, far_keep, far_send = pl.pallas_call(
        functools.partial(far_grads, scale, inv_root),
        out_shape=(
            jax.ShapeDtypeStruct((blocks, 2, 8, rows), f32),
            jax.ShapeDtypeStruct((blocks, dim, rows), f32),
            jax.ShapeDtypeStruct(far_rows, f32),
            jax.ShapeDtypeStruct(far_rows, bf16),
        ),
        grid_spec=pltpu.PrefetchScalarGridSpec(
            num_scalar_prefetch=2,
            grid=(blocks // STEP,),
            in_specs=[stat, blk, blk, whole(far_rows), whole(far_rows)],
            out_specs=(fin, part_dq, whole(far_rows), whole(far_rows)),
            scratch_shapes=[
                pltpu.VMEM((2,) + far_rows, bf16),
                pltpu.VMEM((2,) + far_rows, f32),
                pltpu.VMEM((WIDE * TILE, rows), f32),
                pltpu.VMEM((WIDE * TILE, rows), f32),
                pltpu.VMEM((4, 8, rows), f32),
            ]
            + some_keys
            + some_probs,
        ),
        compiler_params=params,
        cost_estimate=pl.CostEstimate(
            flops=5 * one * blocks * 6, bytes_accessed=4 * tok_rows * heads * dim * 2, transcendentals=0
        ),
        name="far_grads",
    )(far_list, par, stats, q2, do2, far_mine, far_theirs)

    back = (far_keep + swap_pair(far_send).astype(f32)).astype(bf16)
    came = lax.all_to_all(back, "seq", split_axis=0, concat_axis=0, tiled=True)

    grad_q, own_keep, own_send = pl.pallas_call(
        functools.partial(own_grads, scale, inv_root, heads),
        out_shape=(
            jax.ShapeDtypeStruct((blocks * rows, dim), bf16),
            jax.ShapeDtypeStruct(own_rows, f32),
            jax.ShapeDtypeStruct(own_rows, f32),
        ),
        grid_spec=pltpu.PrefetchScalarGridSpec(
            num_scalar_prefetch=2,
            grid=(blocks // STEP,),
            in_specs=[fin, part_dq, blk, blk, whole(own_rows), whole(own_rows)],
            out_specs=(blk, whole(own_rows), whole(own_rows)),
            scratch_shapes=[
                pltpu.VMEM((2,) + own_rows, bf16),
                pltpu.VMEM((2,) + own_rows, f32),
                pltpu.VMEM((dim, rows), f32),
            ]
            + some_keys
            + some_probs,
        ),
        compiler_params=params,
        cost_estimate=pl.CostEstimate(
            flops=5 * one * blocks * 8, bytes_accessed=5 * tok_rows * heads * dim * 2, transcendentals=0
        ),
        name="own_grads",
    )(own_list, par, final, dq_part, q2, do2, mine, theirs)

    other = swap_pair(own_send)
    grad_kv = pl.pallas_call(
        join_grads,
        out_shape=jax.ShapeDtypeStruct(own_rows, bf16),
        in_specs=[in_smem, in_vmem, in_vmem, in_vmem],
        out_specs=in_vmem,
        scratch_shapes=[pltpu.VMEM(own_rows, f32)],
        compiler_params=pltpu.CompilerParams(vmem_limit_bytes=60 * 1024 * 1024),
        name="join_grads",
    )(home, own_keep, other, came)
    return (grad_q.reshape(tok_rows, heads, dim), grad_kv.reshape(tok_rows, 1, dim))


def solution(mesh):
    in_specs = (
        P("seq", "head", None),
        P("seq", "head", None),
        P("seq", None),
        P("seq", "head", None),
    )
    out_specs = (P("seq", "head", None), P("seq", "head", None))
    return jax.shard_map(
        on_device, mesh=mesh, in_specs=in_specs, out_specs=out_specs, check_vma=False
    )
```

time: 121 us -> 95.5 us (0.79)
  local copies, waits for them, and re-layouts: 18.7 us -> 5.6 us
  starting transfers between devices: 36.8 us -> 26.4 us
  waiting for transfers between devices: 16.7 us -> 8.42 us
  Pallas kernels: 42.1 us -> 47.2 us
  other arithmetic: 4.93 us -> 6.62 us
    all_to_all x1, starting transfers between devices: 25.3 us -> 15.2 us  [on_device(): came = lax.all_to_all(back, 'seq', split_axis=0, concat_axis=0, tiled=True)]
    unnamed x26 -> x12, local copies, waits for them, and re-layouts: 12.5 us -> 2.96 us
    all_to_all x1, waiting for transfers between devices: 9.04 us -> 0.01 us  [on_device(): lax.all_to_all(reply, 'seq', split_axis=0, concat_axis=0, tiled=True)]
    pallas_call x1, Pallas kernels: 2.55 us -> 9.81 us  [on_device(): pl.pallas_call(functools.partial(far_grads, scale, inv_root), out_shape=(...]
    pallas_call x1, Pallas kernels: 23.2 us -> 20 us  [on_device(): pl.pallas_call(functools.partial(own_grads, scale, inv_root, heads), out_...]
    gather x1 -> x0, local copies, waits for them, and re-layouts: 2.3 us -> none  [on_device(): mine.reshape(blocks, TILE, dim)[jnp.clip(home, 0, blocks - 1)]]
    pallas_call x1 -> x2, Pallas kernels: 2.31 us -> 4.05 us  [the longest x1 2.31 us: on_device(): pl.pallas_call(join_grads, out_shape=jax.ShapeDtypeStruct(own_rows, bf16)...]
    ppermute x4, waiting for transfers between devices: 3.08 us -> 4.68 us  [swap_pair(): return lax.ppermute(block, 'head', [(h, h ^ 1) for h in range(count)])]
  transfers between devices with their start and end apart: 7 -> 7, of which waited for: 4 -> 4; matrix products, arithmetic and copies ran while one was open for 9% -> 8% of each run, Pallas kernels for 31% -> 37%
where the time goes in v2:
time: 95.5 us; the launch traced here: 95 us
  Pallas kernels  47.2 us (49%)
  starting transfers between devices  26.4 us (28%)
  waiting for transfers between devices  8.42 us (9%)
  other arithmetic  6.62 us (7%)
  local copies, waits for them, and re-layouts  5.6 us (6%)
    pallas_call x1, Pallas kernels, on_device(): pl.pallas_call(functools.partial(own_grads, scale, inv_root, heads), out_...  20 us
    all_to_all x1, starting transfers between devices, on_device(): came = lax.all_to_all(back, 'seq', split_axis=0, concat_axis=0, tiled=True)  15.2 us
    pallas_call x1, Pallas kernels, on_device(): pl.pallas_call(functools.partial(own_stats, scale, heads), out_shape=jax....  13.3 us
    pallas_call x1, Pallas kernels, on_device(): pl.pallas_call(functools.partial(far_grads, scale, inv_root), out_shape=(...  9.81 us
    all_to_all x1, starting transfers between devices, on_device(): lax.all_to_all(asked[:, None, :], 'seq', split_axis=0, concat_axis=0, til...  6.86 us
    ppermute x4, waiting for transfers between devices, swap_pair(): return lax.ppermute(block, 'head', [(h, h ^ 1) for h in range(count)])  4.68 us
    all_to_all x1, waiting for transfers between devices, on_device(): lax.all_to_all(asked[:, None, :], 'seq', split_axis=0, concat_axis=0, til...  3.74 us
    all_to_all x1, starting transfers between devices, on_device(): lax.all_to_all(reply, 'seq', split_axis=0, concat_axis=0, tiled=True)  3.45 us
  transfers between devices with their start and end apart: 7, of which 4 were waited for; matrix products, arithmetic and copies ran while one was open for 8% of the time, Pallas kernels for 37%

profile of v2, /device:TPU:0, one launch (start us, length us, event | category | flops | bytes accessed | tf_op | source)
XLA Modules:
  0.0 95.0 jit_solution(6827519502944604808)
XLA Ops:
  1.2 0.8 fusion.2
  2.5 0.7 copy.11
  3.2 6.9 %all-to-all-start = ((s32[8,1,3]{2,1,0:T(1,128)}), s32[8,1,3]{2,1,0:T(1,128)S(1)}, u32[]{:S(2)}, u32[]{:S(2)}) async-start(s32[8,1,3]{2,1,0:T(1,128)} %copy.11), calls=%async_computation | async-start | bytes 8192 | tf_op jit(solution)/shard_map/all_to_all | solution.py:345
  10.2 0.8 fusion.6
  11.0 0.8 slice.11
  12.7 3.7 %all-to-all-done.home_ref = s32[8,1,3]{2,1,0:T(1,128)S(1)} async-done(((s32[8,1,3]{2,1,0:T(1,128)}), s32[8,1,3]{2,1,0:T(1,128)S(1)}, u32[]{:S(2)}, u32[]{:S(2)}) %all-to-all-start) | async-done | bytes 128 | tf_op jit(solution)/shard_map/all_to_all | solution.py:345
  16.5 0.6 copy-done.3
  17.1 1.7 %fill_reply.1 = bf16[1536,128]{1,0:T(8,128)(2,1)} custom-call(s32[8,1,3]{2,1,0:T(1,128)} %copy-done.3, bf16[1024,128]{1,0:T(8,128)(2,1)} %bitcast.19), custom_call_target="tpu_custom_call" | custom-call | tf_op jit(solution)/shard_map/fill_reply/pallas_call | solution.py:348
  18.8 3.5 %all-to-all-start.1 = ((bf16[8,192,128]{2,1,0:T(8,128)(2,1)}), bf16[8,192,128]{2,1,0:T(8,128)(2,1)S(1)}, u32[]{:S(2)}, u32[]{:S(2)}) async-start(bf16[8,192,128]{2,1,0:T(8,128)(2,1)} %bitcast.14), calls=%async_computation.1 | async-start | bytes 786432 | tf_op jit(solution)/shard_map/all_to_all | solution.py:356
  22.4 0.6 convert_reduce_fusion
  23.3 0.7 pad_add_fusion.1.list_ref
  24.0 0.7 copy-done.5
  24.7 13.3 %own_stats.1.st_ref = f32[16,3,8,512]{3,2,1,0:T(8,128)} custom-call(s32[16,17]{1,0:T(8,128)} %pad_add_fusion.1.list_ref, s32[1]{0:T(128)} %bitcast.1.par_ref, bf16[8192,128]{1,0:T(8,128)(2,1)} %bitcast.25, bf16[8192,128]{1,0:T(8,128)(2,1)} %bitcast.28, bf16[1024,128]{1,0:T(8,128)(2,1)} %bitcast.20, bf16[1024,128]{1,0:T(8,128)(2,1)} %copy-done.5), custom_call_target="tpu_custom_call" | custom-call | flops 2147483648 | bytes 4194304 | tf_op jit(solution)/shard_map/own_stats/pallas_call | solution.py:383
  38.4 0.7 pad_add_fusion.2.list_ref
  39.0 0.8 collective-permute-done.1.theirs_ref
  39.8 0.8 copy-done.4
  40.6 9.8 %far_grads.1 = (f32[16,2,8,512]{3,2,1,0:T(8,128)}, f32[16,128,512]{2,1,0:T(8,128)}, f32[1536,128]{1,0:T(8,128)}, bf16[1536,128]{1,0:T(8,128)(2,1)}) custom-call(s32[16,17]{1,0:T(8,128)} %pad_add_fusion.2.list_ref, s32[1]{0:T(128)} %bitcast.1.par_ref, f32[16,3,8,512]{3,2,1,0:T(8,128)} %own_stats.1.st_ref, bf16[8192,128]{1,0:T(8,128)(2,1)} %bitcast.26, ...), custom_call_target="tpu_custom_call" | custom-call | flops 4026531840 | bytes 8388608 | tf_op jit(solution)/shard_map/far_grads/pallas_call | solution.py:403
  50.6 1.8 %collective-permute-done.3 = bf16[1536,128]{1,0:T(8,128)(2,1)S(1)} collective-permute-done((bf16[1536,128]{1,0:T(8,128)(2,1)}, bf16[1536,128]{1,0:T(8,128)(2,1)S(1)}, u32[]{:S(2)}, u32[]{:S(2)}) %collective-permute-start.3) | collective-permute-done | bytes 393248 | tf_op jit(solution)/shard_map/ppermute | solution.py:27
  52.4 2.0 %add_convert_fusion = bf16[1536,128]{1,0:T(8,128)(2,1)} fusion(f32[1536,128]{1,0:T(8,128)} %get-tuple-element.18, bf16[1536,128]{1,0:T(8,128)(2,1)S(1)} %collective-permute-done.3), kind=kLoop, calls=%fused_computation | loop fusion | flops 589824 | bytes 1572864 | tf_op jit(solution)/shard_map/convert_element_type | solution.py:433
  54.3 15.2 %all-to-all-start.2 = ((bf16[8,192,128]{2,1,0:T(8,128)(2,1)}), bf16[8,192,128]{2,1,0:T(8,128)(2,1)S(1)}, u32[]{:S(2)}, u32[]{:S(2)}) async-start(bf16[8,192,128]{2,1,0:T(8,128)(2,1)} %bitcast.10), calls=%async_computation.2 | async-start | bytes 786432 | tf_op jit(solution)/shard_map/all_to_all | solution.py:434
  69.6 20.0 %own_grads.1 = (bf16[8192,128]{1,0:T(8,128)(2,1)}, f32[1024,128]{1,0:T(8,128)}, f32[1024,128]{1,0:T(8,128)}) custom-call(s32[16,17]{1,0:T(8,128)} %pad_add_fusion.1.list_ref, s32[1]{0:T(128)} %bitcast.1.par_ref, f32[16,2,8,512]{3,2,1,0:T(8,128)} %get-tuple-element.13.fin_ref, f32[16,128,512]{2,1,0:T(8,128)} %get-tuple-element.14.part_ref, ...), custom_call_target="tpu_custom_call" | custom-call | flops 5368709120 | bytes 10485760 | tf_op jit(solution)/shard_map/own_grads/pallas_call | solution.py:436
  89.7 2.1 %collective-permute-done.2.other_ref = f32[1024,128]{1,0:T(8,128)S(1)} collective-permute-done((f32[1024,128]{1,0:T(8,128)}, f32[1024,128]{1,0:T(8,128)S(1)}, u32[]{:S(2)}, u32[]{:S(2)}) %collective-permute-start.2) | collective-permute-done | bytes 524320 | tf_op jit(solution)/shard_map/ppermute | solution.py:27
  91.8 0.8 copy-done.1
  92.7 2.3 %join_grads.1 = bf16[1024,128]{1,0:T(8,128)(2,1)} custom-call(s32[8,1,3]{2,1,0:T(1,128)} %copy-done.3, f32[1024,128]{1,0:T(8,128)} %get-tuple-element.16.keep_ref, f32[1024,128]{1,0:T(8,128)} %copy-done.1, bf16[1536,128]{1,0:T(8,128)(2,1)} %bitcast.15), custom_call_target="tpu_custom_call" | custom-call | tf_op jit(solution)/shard_map/join_grads/pallas_call | solution.py:464
  (32 shorter events, 3.2 us)
Async XLA Ops:
  0.6 23.3 %collective-permute-start = (bf16[1024,128]{1,0:T(8,128)(2,1)}, bf16[1024,128]{1,0:T(8,128)(2,1)S(1)}, u32[]{:S(2)}, u32[]{:S(2)}) collective-permute-start(bf16[1024,128]{1,0:T(8,128)(2,1)} %bitcast.18), channel_id=1, source_target_pairs={{0,1},{1,0},{2,3},{3,2},{4,5},{5,4},{6,7},{7,6},{8,9},{9,8},{10,11... | collective-permute-start | bytes 786440 | tf_op jit(solution)/shard_map/ppermute | solution.py:27
  3.2 13.2 %all-to-all-start = ((s32[8,1,3]{2,1,0:T(1,128)}), s32[8,1,3]{2,1,0:T(1,128)S(1)}, u32[]{:S(2)}, u32[]{:S(2)}) async-start(s32[8,1,3]{2,1,0:T(1,128)} %copy.11), calls=%async_computation | async-start | bytes 8192 | tf_op jit(solution)/shard_map/all_to_all | solution.py:345
  16.5 0.6 copy-start.3
  18.8 19.2 %all-to-all-start.1 = ((bf16[8,192,128]{2,1,0:T(8,128)(2,1)}), bf16[8,192,128]{2,1,0:T(8,128)(2,1)S(1)}, u32[]{:S(2)}, u32[]{:S(2)}) async-start(bf16[8,192,128]{2,1,0:T(8,128)(2,1)} %bitcast.14), calls=%async_computation.1 | async-start | bytes 786432 | tf_op jit(solution)/shard_map/all_to_all | solution.py:356
  24.0 0.7 copy-start.5
  38.0 1.8 %copy-start.2 = (bf16[8,192,128]{2,1,0:T(8,128)(2,1)}, bf16[8,192,128]{2,1,0:T(8,128)(2,1)S(1)}, u32[]{:S(2)}) copy-start(bf16[8,192,128]{2,1,0:T(8,128)(2,1)S(1)} %all-to-all-done.1) | copy-start | bytes 1179652
  38.0 1.8 %collective-permute-start.1 = (bf16[1536,128]{1,0:T(8,128)(2,1)S(1)}, bf16[1536,128]{1,0:T(8,128)(2,1)S(1)}, u32[]{:S(2)}, u32[]{:S(2)}) collective-permute-start(bf16[1536,128]{1,0:T(8,128)(2,1)S(1)} %bitcast.16), channel_id=1, source_target_pairs={{0,1},{1,0},{2,3},{3,2},{4,5},{5,4},{6,7},{7,6},{8,9},{9,8},{10,11... | collective-permute-start | bytes 1179656 | tf_op jit(solution)/shard_map/ppermute | solution.py:27
  39.8 0.8 copy-start.4
  50.4 2.0 %collective-permute-start.3 = (bf16[1536,128]{1,0:T(8,128)(2,1)}, bf16[1536,128]{1,0:T(8,128)(2,1)S(1)}, u32[]{:S(2)}, u32[]{:S(2)}) collective-permute-start(bf16[1536,128]{1,0:T(8,128)(2,1)} %get-tuple-element.19), channel_id=1, source_target_pairs={{0,1},{1,0},{2,3},{3,2},{4,5},{5,4},{6,7},{7,6},{8,9},{9,8},{10,11... | collective-permute-start | bytes 1179656 | tf_op jit(solution)/shard_map/ppermute | solution.py:27
  54.3 37.5 %all-to-all-start.2 = ((bf16[8,192,128]{2,1,0:T(8,128)(2,1)}), bf16[8,192,128]{2,1,0:T(8,128)(2,1)S(1)}, u32[]{:S(2)}, u32[]{:S(2)}) async-start(bf16[8,192,128]{2,1,0:T(8,128)(2,1)} %bitcast.10), calls=%async_computation.2 | async-start | bytes 786432 | tf_op jit(solution)/shard_map/all_to_all | solution.py:434
  89.6 2.2 %collective-permute-start.2 = (f32[1024,128]{1,0:T(8,128)}, f32[1024,128]{1,0:T(8,128)S(1)}, u32[]{:S(2)}, u32[]{:S(2)}) collective-permute-start(f32[1024,128]{1,0:T(8,128)} %get-tuple-element.17), channel_id=1, source_target_pairs={{0,1},{1,0},{2,3},{3,2},{4,5},{5,4},{6,7},{7,6},{8,9},{9,8},{10,11... | collective-permute-start | bytes 1572872 | tf_op jit(solution)/shard_map/ppermute | solution.py:27
  91.8 0.8 copy-start.1
  91.8 0.9 copy-start

commit v3 on v2

v3 whole, which is shorter than its diff:
```python
import functools
import math

import jax
import jax.numpy as jnp
from jax import lax
from jax.experimental import pallas as pl
from jax.experimental.pallas import tpu as pltpu
from jax.sharding import PartitionSpec as P

TILE = 64
SEL = 16
CAP = 3
WIDE = 8
OWN_SIZES = (2, 4, 6)
FAR_SIZES = (4, 7, 8)
VMEM_LIMIT = 40 * 1024 * 1024
SMALL_LIMIT = 8 * 1024 * 1024
STEP = 4
LOW = -1e30
HIGH = 1e30
TOO_LARGE = 2.0**64
NT = (((1,), (1,)), ((), ()))
TN = (((0,), (0,)), ((), ()))


def swap_pair(block):
    count = lax.axis_size("head")
    return lax.ppermute(block, "head", [(h, h ^ 1) for h in range(count)])


def keep_in_hbm(array):
    return pltpu.with_memory_space_constraint(array, pltpu.HBM)


def tile_rows(index):
    return pl.ds(pl.multiple_of(index * TILE, TILE), TILE)


def span(index, size):
    return pl.ds(pl.multiple_of(index * size, size), size)


def dot(a, b, dims=(((1,), (0,)), ((), ()))):
    return lax.dot_general(a, b, dims, preferred_element_type=jnp.float32)


def fold(x, op):
    parts = [x[8 * i : 8 * i + 8] for i in range(TILE // 8)]
    while len(parts) > 1:
        parts = [op(parts[i], parts[i + 1]) for i in range(0, len(parts), 2)]
    return parts[0]


def places(rows, group):
    key = lax.broadcasted_iota(jnp.int32, (TILE, rows), 0)
    query = lax.broadcasted_iota(jnp.int32, (TILE, rows), 1) // group
    return key, query


def mask_diagonal(x, is_first, group):
    key, query = places(x.shape[1], group)
    return jnp.where((key <= query) | jnp.logical_not(is_first), x, LOW)


def pick_diagonal(x, group):
    key, query = places(x.shape[1], group)
    return jnp.sum(fold(jnp.where(key == query, x, 0.0), jnp.add), axis=0, keepdims=True)


def lay_halves(par_ref, mine_ref, theirs_ref, kv_ref):
    par = par_ref[0]
    kv_ref[par] = mine_ref[...]
    kv_ref[1 - par] = theirs_ref[...]


def each_block(body):
    def run(j, _):
        body(pl.program_id(0) * STEP + j, j)
        return 0

    lax.fori_loop(0, STEP, run, 0)


def pick(list_ref, b, start, size):
    count = list_ref[b, SEL]
    return (
        [list_ref[b, start + i] for i in range(size)],
        [start + i < count for i in range(size)],
    )


def part(i):
    return slice(i * TILE, (i + 1) * TILE)


def load_tiles(kv_ref, k_ref, v_ref, picks):
    for i, t in enumerate(picks):
        k_ref[part(i)] = kv_ref[0, tile_rows(t), :]
        v_ref[part(i)] = kv_ref[1, tile_rows(t), :]


def by_size(left, sizes, run):
    for low, size in zip((0,) + sizes[:-1], sizes, strict=True):

        @pl.when((left > low) & (left <= size))
        def _():
            run(size)


def in_parts(count, run):
    wide = (count + 1) // WIDE

    def full(c, _):
        run(c * WIDE, WIDE)
        return 0

    lax.fori_loop(0, wide, full, 0)
    by_size(count - wide * WIDE, OWN_SIZES, lambda size: run(wide * WIDE, size))


def sum_up(x):
    return jnp.sum(x, axis=0, keepdims=True)


def own_stats(
    scale, group, list_ref, par_ref, q_ref, do_ref, mine_ref, theirs_ref, st_ref,
    kv_ref, k_ref, v_ref, sum_ref,
):
    rows = q_ref.shape[0] // STEP

    @pl.when(pl.program_id(0) == 0)
    def _():
        lay_halves(par_ref, mine_ref, theirs_ref, kv_ref)

    def block(b, j, again=False):
        count = list_ref[b, SEL]
        q_at = span(j, rows)
        sums = sum_ref.at[j]

        def scores(start, size):
            picks, real = pick(list_ref, b, start, size)
            load_tiles(kv_ref, k_ref, v_ref, picks)
            return dot(k_ref[: size * TILE], q_ref[q_at, :], NT) * scale, real

        def run(start, size):
            x, real = scores(start, size)
            dp = dot(v_ref[: size * TILE], do_ref[q_at, :], NT)
            base = sums[0]
            if not again:
                base = jnp.where(start == 0, pick_diagonal(x[part(0)], group), base)
                sums[0] = base
            base = base[0:1]
            total, dotted = sums[1], sums[2]
            for i in range(size):
                xi = mask_diagonal(x[part(i)], start == 0, group) if i == 0 else x[part(i)]
                e = jnp.exp2(xi - jnp.where(real[i], base, HIGH))
                total = total + fold(e, jnp.add)
                dotted = dotted + fold(e * dp[part(i)], jnp.add)
            sums[1] = total
            sums[2] = dotted

        if not again:
            sums[...] = jnp.zeros_like(sums)
            in_parts(count, run)
            return

        size = OWN_SIZES[0]
        sums[0] = jnp.full(sums.shape[1:], LOW, jnp.float32)

        def look(c, _):
            x, real = scores(c * size, size)
            top = sums[0]
            for i in range(size):
                xi = mask_diagonal(x[part(i)], c == 0, group) if i == 0 else x[part(i)]
                top = jnp.maximum(top, jnp.where(real[i], fold(xi, jnp.maximum), LOW))
            sums[0] = top
            return 0

        def anew(c, _):
            run(c * size, size)
            return 0

        lax.fori_loop(0, pl.cdiv(count, size), look, 0)
        sums[0] = jnp.broadcast_to(jnp.max(sums[0], axis=0, keepdims=True), sums.shape[1:])
        sums[1] = jnp.zeros(sums.shape[1:], jnp.float32)
        sums[2] = jnp.zeros(sums.shape[1:], jnp.float32)
        lax.fori_loop(0, pl.cdiv(count, size), anew, 0)

    each_block(block)

    @pl.when(jnp.max(sum_ref[:, 1]) > TOO_LARGE)
    def _():
        each_block(functools.partial(block, again=True))

    for j in range(STEP):
        st_ref[j, 0:1] = sum_ref[j, 0, 0:1]
        st_ref[j, 1:2] = sum_up(sum_ref[j, 1])
        st_ref[j, 2:3] = sum_up(sum_ref[j, 2])


def add_grads(acc_ref, picks, gk, gv):
    for i, t in enumerate(picks):
        acc_ref[0, tile_rows(t), :] += gk[part(i)]
        acc_ref[1, tile_rows(t), :] += gv[part(i)]


def leave_grads(inv_root, par_ref, acc_ref, keep_ref, send_ref):
    @pl.when(pl.program_id(0) == pl.num_programs(0) - 1)
    def _():
        par = par_ref[0]
        keep = acc_ref[par] * jnp.where(par == 0, inv_root, 1.0)
        send = acc_ref[1 - par] * jnp.where(par == 0, 1.0, inv_root)
        keep_ref[...] = keep.astype(keep_ref.dtype)
        send_ref[...] = send.astype(send_ref.dtype)


def far_grads(
    scale, inv_root, list_ref, par_ref, st_ref, q_ref, do_ref, mine_ref, theirs_ref,
    fin_ref, dq_ref, keep_ref, send_ref,
    kv_ref, acc_ref, e_ref, dp_ref, sum_ref, k_ref, v_ref, p_ref, ds_ref,
):
    rows = q_ref.shape[0] // STEP

    @pl.when(pl.program_id(0) == 0)
    def _():
        lay_halves(par_ref, mine_ref, theirs_ref, kv_ref)
        acc_ref[...] = jnp.zeros_like(acc_ref)

    def first(b, j, again=False):
        count = list_ref[b, SEL]
        q_at = span(j, rows)
        sums = sum_ref.at[j]

        def scores(start, size):
            picks, real = pick(list_ref, b, start, size)
            load_tiles(kv_ref, k_ref, v_ref, picks)
            return dot(k_ref[: size * TILE], q_ref[q_at, :], NT) * scale, real

        def read(start, size):
            x, real = scores(start, size)
            dp = dot(v_ref[: size * TILE], do_ref[q_at, :], NT)
            base, total, dotted = sums[0, 0:1], sums[1], sums[2]
            for i in range(size):
                to = tile_rows(start + i)
                e = jnp.exp2(x[part(i)] - jnp.where(real[i], base, HIGH))
                e_ref[j, to, :] = e
                dp_ref[j, to, :] = dp[part(i)]
                total = total + fold(e, jnp.add)
                dotted = dotted + fold(e * dp[part(i)], jnp.add)
            sums[1] = total
            sums[2] = dotted

        def begin(base):
            fade = jnp.exp2(st_ref[j, 0:1] - base)
            at_top = lax.broadcasted_iota(jnp.int32, sums.shape[1:], 0) == 0
            sums[0] = jnp.broadcast_to(base, sums.shape[1:])
            sums[1] = jnp.where(at_top, st_ref[j, 1:2] * fade, 0.0)
            sums[2] = jnp.where(at_top, st_ref[j, 2:3] * fade, 0.0)

        if not again:
            begin(st_ref[j, 0:1])
            by_size(count, FAR_SIZES, lambda size: read(0, size))
            return

        size = FAR_SIZES[0]
        sums[0] = jnp.broadcast_to(st_ref[j, 0:1], sums.shape[1:])

        def look(c, _):
            x, real = scores(c * size, size)
            top = sums[0]
            for i in range(size):
                top = jnp.maximum(top, jnp.where(real[i], fold(x[part(i)], jnp.maximum), LOW))
            sums[0] = top
            return 0

        def anew(c, _):
            read(c * size, size)
            return 0

        lax.fori_loop(0, pl.cdiv(count, size), look, 0)
        begin(jnp.max(sums[0], axis=0, keepdims=True))
        lax.fori_loop(0, pl.cdiv(count, size), anew, 0)

    def second(b, j):
        count = list_ref[b, SEL]
        q_at = span(j, rows)
        total, dotted = sum_up(sum_ref[j, 1]), sum_up(sum_ref[j, 2])
        delta = dotted / total
        ratio = 1.0 / total
        fin_ref[j, 0:1] = sum_ref[j, 0, 0:1] + jnp.log2(total)
        fin_ref[j, 1:2] = delta

        @pl.when(count == 0)
        def _():
            dq_ref[j] = jnp.zeros(dq_ref.shape[1:], dq_ref.dtype)

        def spread(size):
            picks, _ = pick(list_ref, b, 0, size)
            n = size * TILE
            for i, t in enumerate(picks):
                k_ref[part(i)] = kv_ref[0, tile_rows(t), :]
                p = e_ref[j, part(i)] * ratio
                p_ref[part(i)] = p.astype(jnp.bfloat16)
                ds_ref[part(i)] = (p * (dp_ref[j, part(i)] - delta)).astype(jnp.bfloat16)
            add_grads(acc_ref, picks, dot(ds_ref[:n], q_ref[q_at, :]), dot(p_ref[:n], do_ref[q_at, :]))
            dq_ref[j] = dot(k_ref[:n], ds_ref[:n], TN).astype(dq_ref.dtype)

        by_size(count, FAR_SIZES, spread)

    each_block(first)

    @pl.when(jnp.max(sum_ref[:, 1]) > TOO_LARGE)
    def _():
        each_block(functools.partial(first, again=True))

    each_block(second)
    leave_grads(inv_root, par_ref, acc_ref, keep_ref, send_ref)


def own_grads(
    scale, inv_root, group, list_ref, par_ref, fin_ref, part_ref, q_ref, do_ref, mine_ref, theirs_ref,
    out_ref, keep_ref, send_ref, kv_ref, acc_ref, dq_ref, k_ref, v_ref, p_ref, ds_ref,
):
    rows = q_ref.shape[0] // STEP

    @pl.when(pl.program_id(0) == 0)
    def _():
        lay_halves(par_ref, mine_ref, theirs_ref, kv_ref)
        acc_ref[...] = jnp.zeros_like(acc_ref)

    def block(b, j):
        q_at = span(j, rows)
        dq_ref[...] = part_ref[j].astype(jnp.float32)

        def spread(start, size):
            picks, real = pick(list_ref, b, start, size)
            n = size * TILE
            load_tiles(kv_ref, k_ref, v_ref, picks)
            level = fin_ref[j, 0:1]
            delta = fin_ref[j, 1:2]
            x = dot(k_ref[:n], q_ref[q_at, :], NT) * scale
            dp = dot(v_ref[:n], do_ref[q_at, :], NT)
            for i in range(size):
                xi = mask_diagonal(x[part(i)], start == 0, group) if i == 0 else x[part(i)]
                p = jnp.exp2(xi - jnp.where(real[i], level, HIGH))
                p_ref[part(i)] = p.astype(jnp.bfloat16)
                ds_ref[part(i)] = (p * (dp[part(i)] - delta)).astype(jnp.bfloat16)
            add_grads(acc_ref, picks, dot(ds_ref[:n], q_ref[q_at, :]), dot(p_ref[:n], do_ref[q_at, :]))
            dq_ref[...] += dot(k_ref[:n], ds_ref[:n], TN)

        in_parts(list_ref[b, SEL], spread)
        out_ref[q_at, :] = (dq_ref[...] * inv_root).astype(out_ref.dtype).T

    each_block(block)
    leave_grads(inv_root, par_ref, acc_ref, keep_ref, send_ref)


def fill_reply(home_ref, mine_ref, reply_ref):
    cap = home_ref.shape[2]
    for i in range(home_ref.shape[0] * cap):
        t = jnp.maximum(home_ref[i // cap, 0, i % cap], 0)
        reply_ref[i * TILE : (i + 1) * TILE] = mine_ref[tile_rows(t), :]


def join_grads(home_ref, keep_ref, other_ref, came_ref, out_ref, acc_ref):
    cap = home_ref.shape[2]
    acc_ref[...] = keep_ref[...] + other_ref[...]
    for i in range(home_ref.shape[0] * cap):
        t = home_ref[i // cap, 0, i % cap]

        @pl.when(t >= 0)
        def _():
            acc_ref[tile_rows(t), :] += came_ref[i * TILE : (i + 1) * TILE].astype(jnp.float32)

    out_ref[...] = acc_ref[...].astype(out_ref.dtype)


def plan(blocks, me_ref, sel_ref, ask_ref, own_ref, far_ref):
    shards = ask_ref.shape[0]
    tiles = shards * blocks
    f32, bf16 = jnp.float32, jnp.bfloat16
    me = me_ref[0]
    sel = sel_ref[...]
    rows = sel.shape[0]
    tile = lax.broadcasted_iota(jnp.int32, (rows, tiles), 1)
    named = sel[:, 0:1] == tile
    for s in range(1, SEL):
        named = named | (sel[:, s : s + 1] == tile)
    is_own = tile // blocks == me
    own = jnp.where(named & is_own, 1.0, 0.0)
    far = jnp.where(named & jnp.logical_not(is_own), 1.0, 0.0)
    wanted = jnp.max(far, axis=0, keepdims=True)

    a = lax.broadcasted_iota(jnp.int32, (tiles, tiles), 0)
    b = lax.broadcasted_iota(jnp.int32, (tiles, tiles), 1)
    lower = jnp.where(a < b, 1.0, 0.0).astype(bf16)
    higher = jnp.where(a > b, 1.0, 0.0).astype(bf16)
    same = jnp.where((a < b) & (a // blocks == b // blocks), 1.0, 0.0).astype(bf16)
    own_place = dot(own.astype(bf16), higher)
    far_place = dot(far.astype(bf16), lower)
    rank = dot(jnp.broadcast_to(wanted, (rows, tiles)).astype(bf16), same)

    local = (tile % blocks).astype(f32)
    far_index = (tile // blocks * CAP).astype(f32) + rank
    column = lax.broadcasted_iota(jnp.int32, (rows, 128), 1)

    def packed(flags, place, values, most):
        out = jnp.where(column == SEL, jnp.sum(flags, axis=1, keepdims=True), 0.0)
        for p in range(most):
            here = jnp.sum(jnp.where(place == p, flags * values, 0.0), axis=1, keepdims=True)
            out = jnp.where(column == p, here, out)
        return out.astype(jnp.int32)[:, : SEL + 1]

    own_ref[...] = packed(own, own_place, local, SEL)
    far_ref[...] = packed(far, far_place, far_index, FAR_SIZES[-1])

    spot = lax.broadcasted_iota(jnp.int32, (rows, tiles), 0).astype(f32)
    asked = jnp.where((rank == spot) & (wanted > 0.0), local + 1.0, 0.0).astype(bf16)
    shard = lax.broadcasted_iota(jnp.int32, (shards, tiles), 0)
    owned = lax.broadcasted_iota(jnp.int32, (shards, tiles), 1) // blocks == shard
    asked = dot(jnp.where(owned, 1.0, 0.0).astype(bf16), asked, NT).astype(jnp.int32) - 1
    for e in range(shards):
        ask_ref[e] = asked[e : e + 1, :CAP]


def whole(shape):
    return pl.BlockSpec(shape, lambda b, *_: (0,) * len(shape), pipeline_mode=pl.Buffered(1))


def on_device(queries, keyvals, selected, d_out):
    tok_rows, heads, dim = queries.shape
    blocks = tok_rows // TILE
    shards = lax.axis_size("seq")
    me = lax.axis_index("seq")
    par = (lax.axis_index("head") % 2).astype(jnp.int32).reshape(1)
    inv_root = dim**-0.5
    scale = inv_root / math.log(2.0)
    rows = TILE * heads
    far = shards * CAP
    f32 = jnp.float32

    mine = keyvals[:, 0, :]
    theirs = swap_pair(mine)
    still = keep_in_hbm(mine)

    in_smem = pl.BlockSpec(memory_space=pltpu.SMEM)
    in_vmem = pl.BlockSpec(memory_space=pltpu.VMEM)
    asked, own_list, far_list = pl.pallas_call(
        functools.partial(plan, blocks),
        out_shape=(
            jax.ShapeDtypeStruct((shards, 1, CAP), jnp.int32),
            jax.ShapeDtypeStruct((blocks, SEL + 1), jnp.int32),
            jax.ShapeDtypeStruct((blocks, SEL + 1), jnp.int32),
        ),
        in_specs=[in_smem, in_vmem],
        out_specs=(in_vmem, in_vmem, in_vmem),
        compiler_params=pltpu.CompilerParams(vmem_limit_bytes=SMALL_LIMIT),
        name="plan",
    )(me.astype(jnp.int32).reshape(1), keep_in_hbm(selected))
    home = lax.all_to_all(asked, "seq", split_axis=0, concat_axis=0, tiled=True)
    home, theirs = lax.optimization_barrier((home, theirs))
    theirs = keep_in_hbm(theirs)
    reply = pl.pallas_call(
        fill_reply,
        out_shape=jax.ShapeDtypeStruct((far * TILE, dim), jnp.bfloat16),
        in_specs=[in_smem, in_vmem],
        out_specs=in_vmem,
        compiler_params=pltpu.CompilerParams(vmem_limit_bytes=SMALL_LIMIT),
        name="fill_reply",
    )(home, still)
    far_mine = lax.all_to_all(reply, "seq", split_axis=0, concat_axis=0, tiled=True)

    q2 = keep_in_hbm(queries.reshape(blocks * rows, dim))
    do2 = keep_in_hbm(d_out.reshape(blocks * rows, dim))
    blk = pl.BlockSpec((STEP * rows, dim), lambda b, *_: (b, 0))
    stat = pl.BlockSpec((STEP, 8, rows), lambda b, *_: (b, 0, 0))
    part_dq = pl.BlockSpec((STEP, dim, rows), lambda b, *_: (b, 0, 0))
    params = pltpu.CompilerParams(
        dimension_semantics=("arbitrary",), vmem_limit_bytes=VMEM_LIMIT
    )
    one = 2 * rows * TILE * dim
    bf16 = jnp.bfloat16
    own_rows, far_rows = (tok_rows, dim), (far * TILE, dim)
    some_keys = [pltpu.VMEM((WIDE * TILE, dim), bf16)] * 2
    some_probs = [pltpu.VMEM((WIDE * TILE, rows), bf16)] * 2

    stats = pl.pallas_call(
        functools.partial(own_stats, scale, heads),
        out_shape=jax.ShapeDtypeStruct((blocks, 8, rows), f32),
        grid_spec=pltpu.PrefetchScalarGridSpec(
            num_scalar_prefetch=2,
            grid=(blocks // STEP,),
            in_specs=[blk, blk, whole(own_rows), whole(own_rows)],
            out_specs=stat,
            scratch_shapes=[pltpu.VMEM((2,) + own_rows, bf16)] + some_keys + [pltpu.VMEM((STEP, 3, 8, rows), f32)],
        ),
        compiler_params=params,
        cost_estimate=pl.CostEstimate(
            flops=2 * one * blocks * 8, bytes_accessed=2 * tok_rows * heads * dim * 2, transcendentals=0
        ),
        name="own_stats",
    )(own_list, par, q2, do2, still, theirs)

    far_mine, stats = lax.optimization_barrier((far_mine, stats))
    far_theirs = swap_pair(far_mine)

    final, dq_part, far_keep, far_send = pl.pallas_call(
        functools.partial(far_grads, scale, inv_root),
        out_shape=(
            pltpu.HBM((blocks, 8, rows), f32),
            pltpu.HBM((blocks, dim, rows), f32),
            jax.ShapeDtypeStruct(far_rows, f32),
            jax.ShapeDtypeStruct(far_rows, bf16),
        ),
        grid_spec=pltpu.PrefetchScalarGridSpec(
            num_scalar_prefetch=2,
            grid=(blocks // STEP,),
            in_specs=[stat, blk, blk, whole(far_rows), whole(far_rows)],
            out_specs=(stat, part_dq, whole(far_rows), whole(far_rows)),
            scratch_shapes=[
                pltpu.VMEM((2,) + far_rows, bf16),
                pltpu.VMEM((2,) + far_rows, f32),
                pltpu.VMEM((STEP, WIDE * TILE, rows), f32),
                pltpu.VMEM((STEP, WIDE * TILE, rows), f32),
                pltpu.VMEM((STEP, 3, 8, rows), f32),
            ]
            + some_keys
            + some_probs,
        ),
        compiler_params=params,
        cost_estimate=pl.CostEstimate(
            flops=5 * one * blocks * 6, bytes_accessed=4 * tok_rows * heads * dim * 2, transcendentals=0
        ),
        name="far_grads",
    )(far_list, par, stats, q2, do2, far_mine, far_theirs)

    back = (far_keep + swap_pair(far_send).astype(f32)).astype(bf16)
    came = lax.all_to_all(back, "seq", split_axis=0, concat_axis=0, tiled=True)

    grad_q, own_keep, own_send = pl.pallas_call(
        functools.partial(own_grads, scale, inv_root, heads),
        out_shape=(
            jax.ShapeDtypeStruct((blocks * rows, dim), bf16),
            jax.ShapeDtypeStruct(own_rows, f32),
            jax.ShapeDtypeStruct(own_rows, f32),
        ),
        grid_spec=pltpu.PrefetchScalarGridSpec(
            num_scalar_prefetch=2,
            grid=(blocks // STEP,),
            in_specs=[stat, part_dq, blk, blk, whole(own_rows), whole(own_rows)],
            out_specs=(blk, whole(own_rows), whole(own_rows)),
            scratch_shapes=[
                pltpu.VMEM((2,) + own_rows, bf16),
                pltpu.VMEM((2,) + own_rows, f32),
                pltpu.VMEM((dim, rows), f32),
            ]
            + some_keys
            + some_probs,
        ),
        compiler_params=params,
        cost_estimate=pl.CostEstimate(
            flops=5 * one * blocks * 8, bytes_accessed=5 * tok_rows * heads * dim * 2, transcendentals=0
        ),
        name="own_grads",
    )(own_list, par, keep_in_hbm(final), keep_in_hbm(dq_part), q2, do2, still, theirs)

    other = swap_pair(own_send)
    grad_kv = pl.pallas_call(
        join_grads,
        out_shape=jax.ShapeDtypeStruct(own_rows, bf16),
        in_specs=[in_smem, in_vmem, in_vmem, in_vmem],
        out_specs=in_vmem,
        scratch_shapes=[pltpu.VMEM(own_rows, f32)],
        compiler_params=pltpu.CompilerParams(vmem_limit_bytes=SMALL_LIMIT),
        name="join_grads",
    )(home, own_keep, other, came)
    return (grad_q.reshape(tok_rows, heads, dim), grad_kv.reshape(tok_rows, 1, dim))


def solution(mesh):
    in_specs = (
        P("seq", "head", None),
        P("seq", "head", None),
        P("seq", None),
        P("seq", "head", None),
    )
    out_specs = (P("seq", "head", None), P("seq", "head", None))
    return jax.shard_map(
        on_device, mesh=mesh, in_specs=in_specs, out_specs=out_specs, check_vma=False
    )
```

time: 95.5 us -> 83.8 us (0.88)
  blocking collectives: 0 us -> 13.1 us
  starting transfers between devices: 26.4 us -> 20.6 us
  other arithmetic: 6.62 us -> 0.87 us
  local copies, waits for them, and re-layouts: 5.6 us -> 0.01 us
  Pallas kernels: 47.2 us -> 43.3 us
  waiting for transfers between devices: 8.42 us -> 5.21 us
    all_to_all x0 -> x1, blocking collectives: none -> 13.1 us  [on_device(): home = lax.all_to_all(asked, 'seq', split_axis=0, concat_axis=0, tiled=True)]
    all_to_all x1 -> x0, starting transfers between devices: 6.86 us -> none  [on_device(): lax.all_to_all(asked[:, None, :], 'seq', split_axis=0, concat_axis=0, til...]
    all_to_all x1 -> x0, waiting for transfers between devices: 3.74 us -> none  [on_device(): lax.all_to_all(asked[:, None, :], 'seq', split_axis=0, concat_axis=0, til...]
    pallas_call x1, Pallas kernels: 9.81 us -> 6.57 us  [on_device(): pl.pallas_call(functools.partial(far_grads, scale, inv_root), out_shape=(...]
    unnamed x12 -> x2, local copies, waits for them, and re-layouts: 2.96 us -> 0.01 us
    reduce_sum x7 -> x0, other arithmetic: 1.89 us -> none  [the longest x2 0.85 us: before(): jnp.sum((flags[:, None, :] & earlier[None]).astype(jnp.int32), axis=2)]
    pallas_call x1, Pallas kernels: 13.3 us -> 11.7 us  [on_device(): pl.pallas_call(functools.partial(own_stats, scale, heads), out_shape=jax....]
    slice x2 -> x0, local copies, waits for them, and re-layouts: 1.62 us -> none  [the longest x1 0.85 us: on_device(): selected[:, 1:2]]
  transfers between devices with their start and end apart: 7 -> 6, of which waited for: 4 -> 3; matrix products, arithmetic and copies ran while one was open for 8% -> 0% of each run, Pallas kernels for 37% -> 40%
where the time goes in v3:
time: 83.8 us
  Pallas kernels  43.3 us (52%)
  starting transfers between devices  20.6 us (25%)
  blocking collectives  13.1 us (16%)
  waiting for transfers between devices  5.21 us (6%)
  other arithmetic  0.87 us (1%)
    pallas_call x1, Pallas kernels, on_device(): pl.pallas_call(functools.partial(own_grads, scale, inv_root, heads), out_...  20.5 us
    all_to_all x1, starting transfers between devices, on_device(): came = lax.all_to_all(back, 'seq', split_axis=0, concat_axis=0, tiled=True)  16.5 us
    all_to_all x1, blocking collectives, on_device(): home = lax.all_to_all(asked, 'seq', split_axis=0, concat_axis=0, tiled=True)  13.1 us
    pallas_call x1, Pallas kernels, on_device(): pl.pallas_call(functools.partial(own_stats, scale, heads), out_shape=jax....  11.7 us
    pallas_call x1, Pallas kernels, on_device(): pl.pallas_call(functools.partial(far_grads, scale, inv_root), out_shape=(...  6.57 us
    ppermute x4, waiting for transfers between devices, swap_pair(): return lax.ppermute(block, 'head', [(h, h ^ 1) for h in range(count)])  5.21 us
    all_to_all x1, starting transfers between devices, on_device(): lax.all_to_all(reply, 'seq', split_axis=0, concat_axis=0, tiled=True)  3.45 us
    pallas_call x1, Pallas kernels, on_device(): pl.pallas_call(fill_reply, out_shape=jax.ShapeDtypeStruct((far * TILE, di...  1.85 us
  transfers between devices with their start and end apart: 6, of which 3 were waited for; matrix products, arithmetic and copies ran while one was open for 0% of the time, Pallas kernels for 40%

profile of v3, /device:TPU:0, one launch (start us, length us, event | category | flops | bytes accessed | tf_op | source)
XLA Modules:
  0.0 83.8 jit_solution(7113555327094755958)
XLA Ops:
  0.6 0.5 collective-permute-start
  1.1 1.1 %plan.1 = (s32[8,1,3]{2,1,0:T(1,128)S(1)}, s32[16,17]{1,0:T(8,128)S(1)}, s32[16,17]{1,0:T(8,128)S(1)}) custom-call(s32[1]{0:T(128)} %bitcast.me_ref, s32[16,16]{1,0:T(8,128)} %sel_ref.1), custom_call_target="tpu_custom_call" | custom-call | tf_op jit(solution)/shard_map/plan/pallas_call | solution.py:449
  2.2 13.1 %all_to_all.28.home_ref = s32[8,1,3]{2,1,0:T(1,128)S(1)} all-to-all(s32[8,1,3]{2,1,0:T(1,128)S(1)} %get-tuple-element.18), channel_id=1, replica_groups=mesh['seq'=8,'head'=4] {'seq'}, dimensions={0} | all-to-all | bytes 192 | tf_op jit(solution)/shard_map/all_to_all | solution.py:461
  15.3 0.0 collective-permute-done.theirs_ref
  15.3 0.0 copy-start
  15.3 1.8 %fill_reply.1 = bf16[1536,128]{1,0:T(8,128)(2,1)} custom-call(s32[8,1,3]{2,1,0:T(1,128)S(1)} %all_to_all.28.home_ref, bf16[1024,128]{1,0:T(8,128)(2,1)} %bitcast.15), custom_call_target="tpu_custom_call" | custom-call | tf_op jit(solution)/shard_map/fill_reply/pallas_call | solution.py:464
  17.2 3.5 %all-to-all-start.1 = ((bf16[8,192,128]{2,1,0:T(8,128)(2,1)}), bf16[8,192,128]{2,1,0:T(8,128)(2,1)S(1)}, u32[]{:S(2)}, u32[]{:S(2)}) async-start(bf16[8,192,128]{2,1,0:T(8,128)(2,1)} %bitcast.3), calls=%async_computation.1 | async-start | bytes 786432 | tf_op jit(solution)/shard_map/all_to_all | solution.py:472
  20.6 0.0 copy-done
  20.7 11.7 %own_stats.1.st_ref = f32[16,8,512]{2,1,0:T(8,128)S(1)} custom-call(s32[16,17]{1,0:T(8,128)S(1)} %get-tuple-element.16.list_ref, s32[1]{0:T(128)} %bitcast.1.par_ref, bf16[8192,128]{1,0:T(8,128)(2,1)} %bitcast.19, bf16[8192,128]{1,0:T(8,128)(2,1)} %bitcast.22, bf16[1024,128]{1,0:T(8,128)(2,1)} %bitcast.16, bf16[1024,128]{1,0:T(8,128)(2,1)} %copy-done), custom_call_target="tpu_custom_call" | custom-call | flops 2147483648 | bytes 4194304 | tf_op jit(solution)/shard_map/own_stats/pallas_call | solution.py:488
  32.4 0.0 all-to-all-done.1
  32.4 0.1 collective-permute-start.1
  32.5 1.7 %collective-permute-done.1.theirs_ref = bf16[1536,128]{1,0:T(8,128)(2,1)S(1)} collective-permute-done((bf16[1536,128]{1,0:T(8,128)(2,1)S(1)}, bf16[1536,128]{1,0:T(8,128)(2,1)S(1)}, u32[]{:S(2)}, u32[]{:S(2)}) %collective-permute-start.1) | collective-permute-done | bytes 393248 | tf_op jit(solution)/shard_map/ppermute | solution.py:29
  34.2 6.6 %far_grads.1 = (f32[16,8,512]{2,1,0:T(8,128)}, f32[16,128,512]{2,1,0:T(8,128)}, f32[1536,128]{1,0:T(8,128)S(1)}, bf16[1536,128]{1,0:T(8,128)(2,1)S(1)}) custom-call(s32[16,17]{1,0:T(8,128)S(1)} %get-tuple-element.17.list_ref, s32[1]{0:T(128)} %bitcast.1.par_ref, f32[16,8,512]{2,1,0:T(8,128)S(1)} %own_stats.1.st_ref, bf16[8192,128]{1,0:T(8,128)(2,1)} %bitcast.20, ...), custom_call_target="tpu_custom_call" | custom-call | flops 4026531840 | bytes 8388608 | tf_op jit(solution)/shard_map/far_grads/pallas_call | solution.py:508
  40.7 0.1 collective-permute-start.3
  40.9 1.6 %collective-permute-done.3 = bf16[1536,128]{1,0:T(8,128)(2,1)S(1)} collective-permute-done((bf16[1536,128]{1,0:T(8,128)(2,1)S(1)}, bf16[1536,128]{1,0:T(8,128)(2,1)S(1)}, u32[]{:S(2)}, u32[]{:S(2)}) %collective-permute-start.3) | collective-permute-done | bytes 393248 | tf_op jit(solution)/shard_map/ppermute | solution.py:29
  42.5 0.9 %add_convert_fusion = bf16[1536,128]{1,0:T(8,128)(2,1)} fusion(f32[1536,128]{1,0:T(8,128)S(1)} %get-tuple-element.28, bf16[1536,128]{1,0:T(8,128)(2,1)S(1)} %collective-permute-done.3), kind=kLoop, calls=%fused_computation | loop fusion | flops 589824 | bytes 1572864 | tf_op jit(solution)/shard_map/convert_element_type | solution.py:538
  43.3 16.5 %all-to-all-start.2 = ((bf16[8,192,128]{2,1,0:T(8,128)(2,1)}), bf16[8,192,128]{2,1,0:T(8,128)(2,1)S(1)}, u32[]{:S(2)}, u32[]{:S(2)}) async-start(bf16[8,192,128]{2,1,0:T(8,128)(2,1)} %bitcast.8), calls=%async_computation.2 | async-start | bytes 786432 | tf_op jit(solution)/shard_map/all_to_all | solution.py:539
  59.8 20.5 %own_grads.1 = (bf16[8192,128]{1,0:T(8,128)(2,1)}, f32[1024,128]{1,0:T(8,128)S(1)}, f32[1024,128]{1,0:T(8,128)S(1)}) custom-call(s32[16,17]{1,0:T(8,128)S(1)} %get-tuple-element.16.list_ref, s32[1]{0:T(128)} %bitcast.1.par_ref, f32[16,8,512]{2,1,0:T(8,128)} %get-tuple-element.23.fin_ref, f32[16,128,512]{2,1,0:T(8,128)} %get-tuple-element.24.part_ref, ...), custom_call_target="tpu_custom_call" | custom-call | flops 5368709120 | bytes 10485760 | tf_op jit(solution)/shard_map/own_grads/pallas_call | solution.py:541
  80.3 0.0 collective-permute-start.2
  80.3 1.9 %collective-permute-done.2.other_ref = f32[1024,128]{1,0:T(8,128)S(1)} collective-permute-done((f32[1024,128]{1,0:T(8,128)S(1)}, f32[1024,128]{1,0:T(8,128)S(1)}, u32[]{:S(2)}, u32[]{:S(2)}) %collective-permute-start.2) | collective-permute-done | bytes 524320 | tf_op jit(solution)/shard_map/ppermute | solution.py:29
  82.2 0.0 all-to-all-done.2
  82.2 1.6 %join_grads.1 = bf16[1024,128]{1,0:T(8,128)(2,1)} custom-call(s32[8,1,3]{2,1,0:T(1,128)S(1)} %all_to_all.28.home_ref, f32[1024,128]{1,0:T(8,128)S(1)} %get-tuple-element.26.keep_ref, f32[1024,128]{1,0:T(8,128)S(1)} %collective-permute-done.2.other_ref, bf16[1536,128]{1,0:T(8,128)(2,1)S(1)} %bitcast.11), custom_call_target="tpu_custom_call" | custom-call | tf_op jit(solution)/shard_map/join_grads/pallas_call | solution.py:569
Async XLA Ops:
  0.6 14.7 %collective-permute-start = (bf16[1024,128]{1,0:T(8,128)(2,1)}, bf16[1024,128]{1,0:T(8,128)(2,1)S(1)}, u32[]{:S(2)}, u32[]{:S(2)}) collective-permute-start(bf16[1024,128]{1,0:T(8,128)(2,1)} %bitcast.14), channel_id=1, source_target_pairs={{0,1},{1,0},{2,3},{3,2},{4,5},{5,4},{6,7},{7,6},{8,9},{9,8},{10,11... | collective-permute-start | bytes 786440 | tf_op jit(solution)/shard_map/ppermute | solution.py:29
  15.3 5.3 %copy-start = (bf16[1024,128]{1,0:T(8,128)(2,1)}, bf16[1024,128]{1,0:T(8,128)(2,1)S(1)}, u32[]{:S(2)}) copy-start(bf16[1024,128]{1,0:T(8,128)(2,1)S(1)} %collective-permute-done.theirs_ref) | copy-start | bytes 786436
  17.2 15.2 %all-to-all-start.1 = ((bf16[8,192,128]{2,1,0:T(8,128)(2,1)}), bf16[8,192,128]{2,1,0:T(8,128)(2,1)S(1)}, u32[]{:S(2)}, u32[]{:S(2)}) async-start(bf16[8,192,128]{2,1,0:T(8,128)(2,1)} %bitcast.3), calls=%async_computation.1 | async-start | bytes 786432 | tf_op jit(solution)/shard_map/all_to_all | solution.py:472
  32.4 1.8 %collective-permute-start.1 = (bf16[1536,128]{1,0:T(8,128)(2,1)S(1)}, bf16[1536,128]{1,0:T(8,128)(2,1)S(1)}, u32[]{:S(2)}, u32[]{:S(2)}) collective-permute-start(bf16[1536,128]{1,0:T(8,128)(2,1)S(1)} %bitcast.12), channel_id=1, source_target_pairs={{0,1},{1,0},{2,3},{3,2},{4,5},{5,4},{6,7},{7,6},{8,9},{9,8},{10,11... | collective-permute-start | bytes 1179656 | tf_op jit(solution)/shard_map/ppermute | solution.py:29
  40.7 1.7 %collective-permute-start.3 = (bf16[1536,128]{1,0:T(8,128)(2,1)S(1)}, bf16[1536,128]{1,0:T(8,128)(2,1)S(1)}, u32[]{:S(2)}, u32[]{:S(2)}) collective-permute-start(bf16[1536,128]{1,0:T(8,128)(2,1)S(1)} %get-tuple-element.29), channel_id=1, source_target_pairs={{0,1},{1,0},{2,3},{3,2},{4,5},{5,4},{6,7},{7,6},{8,9},{9,8},{10,11... | collective-permute-start | bytes 1179656 | tf_op jit(solution)/shard_map/ppermute | solution.py:29
  43.3 38.9 %all-to-all-start.2 = ((bf16[8,192,128]{2,1,0:T(8,128)(2,1)}), bf16[8,192,128]{2,1,0:T(8,128)(2,1)S(1)}, u32[]{:S(2)}, u32[]{:S(2)}) async-start(bf16[8,192,128]{2,1,0:T(8,128)(2,1)} %bitcast.8), calls=%async_computation.2 | async-start | bytes 786432 | tf_op jit(solution)/shard_map/all_to_all | solution.py:539
  80.3 1.9 %collective-permute-start.2 = (f32[1024,128]{1,0:T(8,128)S(1)}, f32[1024,128]{1,0:T(8,128)S(1)}, u32[]{:S(2)}, u32[]{:S(2)}) collective-permute-start(f32[1024,128]{1,0:T(8,128)S(1)} %get-tuple-element.27), channel_id=1, source_target_pairs={{0,1},{1,0},{2,3},{3,2},{4,5},{5,4},{6,7},{7,6},{8,9},{9,8},{10,11... | collective-permute-start | bytes 1572872 | tf_op jit(solution)/shard_map/ppermute | solution.py:29

commit v4 on v3

--- a/solution.py
+++ b/solution.py
@@ -227,94 +227,115 @@
         lay_halves(par_ref, mine_ref, theirs_ref, kv_ref)
         acc_ref[...] = jnp.zeros_like(acc_ref)
 
-    def first(b, j, again=False):
+    def begin(j, base):
+        fade = jnp.exp2(st_ref[j, 0:1] - base)
+        at_top = lax.broadcasted_iota(jnp.int32, sum_ref.shape[2:], 0) == 0
+        sum_ref[j, 0] = jnp.broadcast_to(base, sum_ref.shape[2:])
+        sum_ref[j, 1] = jnp.where(at_top, st_ref[j, 1:2] * fade, 0.0)
+        sum_ref[j, 2] = jnp.where(at_top, st_ref[j, 2:3] * fade, 0.0)
+
+    def scores(b, j, half, start, size):
+        picks, real = pick(list_ref, b, start, size)
+        load_tiles(kv_ref, k_ref.at[half], v_ref.at[half], picks)
+        return dot(k_ref[half, : size * TILE], q_ref[span(j, rows), :], NT) * scale, real
+
+    def read(b, j, half, start, size):
+        x, real = scores(b, j, half, start, size)
+        dp = dot(v_ref[half, : size * TILE], do_ref[span(j, rows), :], NT)
+        base, total, dotted = sum_ref[j, 0, 0:1], sum_ref[j, 1], sum_ref[j, 2]
+        for i in range(size):
+            to = tile_rows(start + i)
+            e = jnp.exp2(x[part(i)] - jnp.where(real[i], base, HIGH))
+            e_ref[j, to, :] = e
+            dp_ref[j, to, :] = dp[part(i)]
+            total = total + fold(e, jnp.add)
+            dotted = dotted + fold(e * dp[part(i)], jnp.add)
+        sum_ref[j, 1] = total
+        sum_ref[j, 2] = dotted
+
+    def anew(b, j):
         count = list_ref[b, SEL]
-        q_at = span(j, rows)
-        sums = sum_ref.at[j]
-
-        def scores(start, size):
-            picks, real = pick(list_ref, b, start, size)
-            load_tiles(kv_ref, k_ref, v_ref, picks)
-            return dot(k_ref[: size * TILE], q_ref[q_at, :], NT) * scale, real
-
-        def read(start, size):
-            x, real = scores(start, size)
-            dp = dot(v_ref[: size * TILE], do_ref[q_at, :], NT)
-            base, total, dotted = sums[0, 0:1], sums[1], sums[2]
-            for i in range(size):
-                to = tile_rows(start + i)
-                e = jnp.exp2(x[part(i)] - jnp.where(real[i], base, HIGH))
-                e_ref[j, to, :] = e
-                dp_ref[j, to, :] = dp[part(i)]
-                total = total + fold(e, jnp.add)
-                dotted = dotted + fold(e * dp[part(i)], jnp.add)
-            sums[1] = total
-            sums[2] = dotted
-
-        def begin(base):
-            fade = jnp.exp2(st_ref[j, 0:1] - base)
-            at_top = lax.broadcasted_iota(jnp.int32, sums.shape[1:], 0) == 0
-            sums[0] = jnp.broadcast_to(base, sums.shape[1:])
-            sums[1] = jnp.where(at_top, st_ref[j, 1:2] * fade, 0.0)
-            sums[2] = jnp.where(at_top, st_ref[j, 2:3] * fade, 0.0)
-
-        if not again:
-            begin(st_ref[j, 0:1])
-            by_size(count, FAR_SIZES, lambda size: read(0, size))
-            return
-
         size = FAR_SIZES[0]
-        sums[0] = jnp.broadcast_to(st_ref[j, 0:1], sums.shape[1:])
+        sum_ref[j, 0] = jnp.broadcast_to(st_ref[j, 0:1], sum_ref.shape[2:])
 
         def look(c, _):
-            x, real = scores(c * size, size)
-            top = sums[0]
+            x, real = scores(b, j, 0, c * size, size)
+            top = sum_ref[j, 0]
             for i in range(size):
                 top = jnp.maximum(top, jnp.where(real[i], fold(x[part(i)], jnp.maximum), LOW))
-            sums[0] = top
+            sum_ref[j, 0] = top
             return 0
 
-        def anew(c, _):
-            read(c * size, size)
+        def once_more(c, _):
+            read(b, j, 0, c * size, size)
             return 0
 
         lax.fori_loop(0, pl.cdiv(count, size), look, 0)
-        begin(jnp.max(sums[0], axis=0, keepdims=True))
-        lax.fori_loop(0, pl.cdiv(count, size), anew, 0)
-
-    def second(b, j):
-        count = list_ref[b, SEL]
-        q_at = span(j, rows)
+        begin(j, jnp.max(sum_ref[j, 0], axis=0, keepdims=True))
+        lax.fori_loop(0, pl.cdiv(count, size), once_more, 0)
+
+    def finish(j):
         total, dotted = sum_up(sum_ref[j, 1]), sum_up(sum_ref[j, 2])
         delta = dotted / total
-        ratio = 1.0 / total
         fin_ref[j, 0:1] = sum_ref[j, 0, 0:1] + jnp.log2(total)
         fin_ref[j, 1:2] = delta
+        fin_ref[j, 2:3] = 1.0 / total
+
+    def spread(b, j, half, size):
+        picks, _ = pick(list_ref, b, 0, size)
+        delta, ratio = fin_ref[j, 1:2], fin_ref[j, 2:3]
+        n = size * TILE
+        q_at = span(j, rows)
+        for i, t in enumerate(picks):
+            k_ref[half, part(i)] = kv_ref[0, tile_rows(t), :]
+            p = e_ref[j, part(i)] * ratio
+            p_ref[half, part(i)] = p.astype(jnp.bfloat16)
+            ds_ref[half, part(i)] = (p * (dp_ref[j, part(i)] - delta)).astype(jnp.bfloat16)
+        ds = ds_ref[half, :n]
+        add_grads(acc_ref, picks, dot(ds, q_ref[q_at, :]), dot(p_ref[half, :n], do_ref[q_at, :]))
+        dq_ref[j] = dot(k_ref[half, :n], ds, TN)
+
+    def each_pair(body):
+        def run(i, _):
+            places = [2 * i, 2 * i + 1]
+            pair = [(pl.program_id(0) * STEP + j, j) for j in places]
+            body(pair, jnp.maximum(list_ref[pair[0][0], SEL], list_ref[pair[1][0], SEL]))
+            return 0
+
+        lax.fori_loop(0, STEP // 2, run, 0)
+
+    def first(pair, count):
+        for _, j in pair:
+            begin(j, st_ref[j, 0:1])
+
+        def both(size):
+            for half, (b, j) in enumerate(pair):
+                read(b, j, half, 0, size)
+
+        by_size(count, FAR_SIZES, both)
+
+    def second(pair, count):
+        for _, j in pair:
+            finish(j)
 
         @pl.when(count == 0)
         def _():
-            dq_ref[j] = jnp.zeros(dq_ref.shape[1:], dq_ref.dtype)
-
-        def spread(size):
-            picks, _ = pick(list_ref, b, 0, size)
-            n = size * TILE
-            for i, t in enumerate(picks):
-                k_ref[part(i)] = kv_ref[0, tile_rows(t), :]
-                p = e_ref[j, part(i)] * ratio
-                p_ref[part(i)] = p.astype(jnp.bfloat16)
-                ds_ref[part(i)] = (p * (dp_ref[j, part(i)] - delta)).astype(jnp.bfloat16)
-            add_grads(acc_ref, picks, dot(ds_ref[:n], q_ref[q_at, :]), dot(p_ref[:n], do_ref[q_at, :]))
-            dq_ref[j] = dot(k_ref[:n], ds_ref[:n], TN).astype(dq_ref.dtype)
-
-        by_size(count, FAR_SIZES, spread)
-
-    each_block(first)
+            for _, j in pair:
+                dq_ref[j] = jnp.zeros(dq_ref.shape[1:], dq_ref.dtype)
+
+        def both(size):
+            for half, (b, j) in enumerate(pair):
+                spread(b, j, half, size)
+
+        by_size(count, FAR_SIZES, both)
+
+    each_pair(first)
 
     @pl.when(jnp.max(sum_ref[:, 1]) > TOO_LARGE)
     def _():
-        each_block(functools.partial(first, again=True))
-
-    each_block(second)
+        each_block(anew)
+
+    each_pair(second)
     leave_grads(inv_root, par_ref, acc_ref, keep_ref, send_ref)
 
 
@@ -329,9 +350,12 @@
         lay_halves(par_ref, mine_ref, theirs_ref, kv_ref)
         acc_ref[...] = jnp.zeros_like(acc_ref)
 
+    def write(j):
+        out_ref[span(j, rows), :] = (dq_ref[j] * inv_root).astype(out_ref.dtype).T
+
     def block(b, j):
         q_at = span(j, rows)
-        dq_ref[...] = part_ref[j].astype(jnp.float32)
+        dq_ref[j] = part_ref[j]
 
         def spread(start, size):
             picks, real = pick(list_ref, b, start, size)
@@ -346,13 +370,14 @@
                 p = jnp.exp2(xi - jnp.where(real[i], level, HIGH))
                 p_ref[part(i)] = p.astype(jnp.bfloat16)
                 ds_ref[part(i)] = (p * (dp[part(i)] - delta)).astype(jnp.bfloat16)
+            write(jnp.maximum(j - 1, 0))
             add_grads(acc_ref, picks, dot(ds_ref[:n], q_ref[q_at, :]), dot(p_ref[:n], do_ref[q_at, :]))
-            dq_ref[...] += dot(k_ref[:n], ds_ref[:n], TN)
+            dq_ref[j] += dot(k_ref[:n], ds_ref[:n], TN)
 
         in_parts(list_ref[b, SEL], spread)
-        out_ref[q_at, :] = (dq_ref[...] * inv_root).astype(out_ref.dtype).T
 
     each_block(block)
+    write(STEP - 1)
     leave_grads(inv_root, par_ref, acc_ref, keep_ref, send_ref)
 
 
@@ -525,8 +550,8 @@
                 pltpu.VMEM((STEP, WIDE * TILE, rows), f32),
                 pltpu.VMEM((STEP, 3, 8, rows), f32),
             ]
-            + some_keys
-            + some_probs,
+            + [pltpu.VMEM((2, WIDE * TILE, dim), bf16)] * 2
+            + [pltpu.VMEM((2, WIDE * TILE, rows), bf16)] * 2,
         ),
         compiler_params=params,
         cost_estimate=pl.CostEstimate(
@@ -553,7 +578,7 @@
             scratch_shapes=[
                 pltpu.VMEM((2,) + own_rows, bf16),
                 pltpu.VMEM((2,) + own_rows, f32),
-                pltpu.VMEM((dim, rows), f32),
+                pltpu.VMEM((STEP, dim, rows), f32),
             ]
             + some_keys
             + some_probs,

time: 83.8 us -> 79.4 us (0.947)
  starting transfers between devices: 20.6 us -> 18.2 us
  Pallas kernels: 43.3 us -> 41.2 us
    all_to_all x1, starting transfers between devices: 16.5 us -> 14 us  [on_device(): came = lax.all_to_all(back, 'seq', split_axis=0, concat_axis=0, tiled=True)]
    pallas_call x1, Pallas kernels: 20.5 us -> 19 us  [on_device(): pl.pallas_call(functools.partial(own_grads, scale, inv_root, heads), out_...]
where the time goes in v4:
time: 79.4 us; the launch traced here: 79.3 us
  Pallas kernels  41.2 us (52%)
  starting transfers between devices  18.2 us (23%)
  blocking collectives  13.1 us (16%)
  waiting for transfers between devices  5.21 us (7%)
  other arithmetic  0.87 us (1%)
    pallas_call x1, Pallas kernels, on_device(): pl.pallas_call(functools.partial(own_grads, scale, inv_root, heads), out_...  19 us
    all_to_all x1, starting transfers between devices, on_device(): came = lax.all_to_all(back, 'seq', split_axis=0, concat_axis=0, tiled=True)  14 us
    all_to_all x1, blocking collectives, on_device(): home = lax.all_to_all(asked, 'seq', split_axis=0, concat_axis=0, tiled=True)  13.1 us
    pallas_call x1, Pallas kernels, on_device(): pl.pallas_call(functools.partial(own_stats, scale, heads), out_shape=jax....  11.4 us
    pallas_call x1, Pallas kernels, on_device(): pl.pallas_call(functools.partial(far_grads, scale, inv_root), out_shape=(...  6.33 us
    ppermute x4, waiting for transfers between devices, swap_pair(): return lax.ppermute(block, 'head', [(h, h ^ 1) for h in range(count)])  5.21 us
    all_to_all x1, starting transfers between devices, on_device(): lax.all_to_all(reply, 'seq', split_axis=0, concat_axis=0, tiled=True)  3.45 us
    pallas_call x1, Pallas kernels, on_device(): pl.pallas_call(fill_reply, out_shape=jax.ShapeDtypeStruct((far * TILE, di...  1.85 us
  transfers between devices with their start and end apart: 6, of which 3 were waited for; matrix products, arithmetic and copies ran while one was open for 0% of the time, Pallas kernels for 40%

profile of v4, /device:TPU:0, one launch (start us, length us, event | category | flops | bytes accessed | tf_op | source)
XLA Modules:
  0.0 79.3 jit_solution(2604160022021130716)
XLA Ops:
  0.6 0.5 collective-permute-start
  1.1 1.1 %plan.1 = (s32[8,1,3]{2,1,0:T(1,128)S(1)}, s32[16,17]{1,0:T(8,128)S(1)}, s32[16,17]{1,0:T(8,128)S(1)}) custom-call(s32[1]{0:T(128)} %bitcast.me_ref, s32[16,16]{1,0:T(8,128)} %sel_ref.1), custom_call_target="tpu_custom_call" | custom-call | tf_op jit(solution)/shard_map/plan/pallas_call | solution.py:474
  2.2 13.1 %all_to_all.28.home_ref = s32[8,1,3]{2,1,0:T(1,128)S(1)} all-to-all(s32[8,1,3]{2,1,0:T(1,128)S(1)} %get-tuple-element.18), channel_id=1, replica_groups=mesh['seq'=8,'head'=4] {'seq'}, dimensions={0} | all-to-all | bytes 192 | tf_op jit(solution)/shard_map/all_to_all | solution.py:486
  15.3 0.0 collective-permute-done.theirs_ref
  15.3 0.0 copy-start
  15.3 1.8 %fill_reply.1 = bf16[1536,128]{1,0:T(8,128)(2,1)} custom-call(s32[8,1,3]{2,1,0:T(1,128)S(1)} %all_to_all.28.home_ref, bf16[1024,128]{1,0:T(8,128)(2,1)} %bitcast.15), custom_call_target="tpu_custom_call" | custom-call | tf_op jit(solution)/shard_map/fill_reply/pallas_call | solution.py:489
  17.2 3.5 %all-to-all-start.1 = ((bf16[8,192,128]{2,1,0:T(8,128)(2,1)}), bf16[8,192,128]{2,1,0:T(8,128)(2,1)S(1)}, u32[]{:S(2)}, u32[]{:S(2)}) async-start(bf16[8,192,128]{2,1,0:T(8,128)(2,1)} %bitcast.3), calls=%async_computation.1 | async-start | bytes 786432 | tf_op jit(solution)/shard_map/all_to_all | solution.py:497
  20.6 0.0 copy-done
  20.7 11.4 %own_stats.1.st_ref = f32[16,8,512]{2,1,0:T(8,128)S(1)} custom-call(s32[16,17]{1,0:T(8,128)S(1)} %get-tuple-element.16.list_ref, s32[1]{0:T(128)} %bitcast.1.par_ref, bf16[8192,128]{1,0:T(8,128)(2,1)} %bitcast.19, bf16[8192,128]{1,0:T(8,128)(2,1)} %bitcast.22, bf16[1024,128]{1,0:T(8,128)(2,1)} %bitcast.16, bf16[1024,128]{1,0:T(8,128)(2,1)} %copy-done), custom_call_target="tpu_custom_call" | custom-call | flops 2147483648 | bytes 4194304 | tf_op jit(solution)/shard_map/own_stats/pallas_call | solution.py:513
  32.1 0.0 all-to-all-done.1
  32.1 0.1 collective-permute-start.1
  32.2 1.7 %collective-permute-done.1.theirs_ref = bf16[1536,128]{1,0:T(8,128)(2,1)S(1)} collective-permute-done((bf16[1536,128]{1,0:T(8,128)(2,1)S(1)}, bf16[1536,128]{1,0:T(8,128)(2,1)S(1)}, u32[]{:S(2)}, u32[]{:S(2)}) %collective-permute-start.1) | collective-permute-done | bytes 393248 | tf_op jit(solution)/shard_map/ppermute | solution.py:29
  33.9 6.3 %far_grads.1 = (f32[16,8,512]{2,1,0:T(8,128)}, f32[16,128,512]{2,1,0:T(8,128)}, f32[1536,128]{1,0:T(8,128)S(1)}, bf16[1536,128]{1,0:T(8,128)(2,1)S(1)}) custom-call(s32[16,17]{1,0:T(8,128)S(1)} %get-tuple-element.17.list_ref, s32[1]{0:T(128)} %bitcast.1.par_ref, f32[16,8,512]{2,1,0:T(8,128)S(1)} %own_stats.1.st_ref, bf16[8192,128]{1,0:T(8,128)(2,1)} %bitcast.20, ...), custom_call_target="tpu_custom_call" | custom-call | flops 4026531840 | bytes 8388608 | tf_op jit(solution)/shard_map/far_grads/pallas_call | solution.py:533
  40.2 0.1 collective-permute-start.3
  40.3 1.6 %collective-permute-done.3 = bf16[1536,128]{1,0:T(8,128)(2,1)S(1)} collective-permute-done((bf16[1536,128]{1,0:T(8,128)(2,1)S(1)}, bf16[1536,128]{1,0:T(8,128)(2,1)S(1)}, u32[]{:S(2)}, u32[]{:S(2)}) %collective-permute-start.3) | collective-permute-done | bytes 393248 | tf_op jit(solution)/shard_map/ppermute | solution.py:29
  41.9 0.9 %add_convert_fusion = bf16[1536,128]{1,0:T(8,128)(2,1)} fusion(f32[1536,128]{1,0:T(8,128)S(1)} %get-tuple-element.28, bf16[1536,128]{1,0:T(8,128)(2,1)S(1)} %collective-permute-done.3), kind=kLoop, calls=%fused_computation | loop fusion | flops 589824 | bytes 1572864 | tf_op jit(solution)/shard_map/convert_element_type | solution.py:563
  42.8 14.0 %all-to-all-start.2 = ((bf16[8,192,128]{2,1,0:T(8,128)(2,1)}), bf16[8,192,128]{2,1,0:T(8,128)(2,1)S(1)}, u32[]{:S(2)}, u32[]{:S(2)}) async-start(bf16[8,192,128]{2,1,0:T(8,128)(2,1)} %bitcast.8), calls=%async_computation.2 | async-start | bytes 786432 | tf_op jit(solution)/shard_map/all_to_all | solution.py:564
  56.8 19.0 %own_grads.1 = (bf16[8192,128]{1,0:T(8,128)(2,1)}, f32[1024,128]{1,0:T(8,128)S(1)}, f32[1024,128]{1,0:T(8,128)S(1)}) custom-call(s32[16,17]{1,0:T(8,128)S(1)} %get-tuple-element.16.list_ref, s32[1]{0:T(128)} %bitcast.1.par_ref, f32[16,8,512]{2,1,0:T(8,128)} %get-tuple-element.23.fin_ref, f32[16,128,512]{2,1,0:T(8,128)} %get-tuple-element.24.part_ref, ...), custom_call_target="tpu_custom_call" | custom-call | flops 5368709120 | bytes 10485760 | tf_op jit(solution)/shard_map/own_grads/pallas_call | solution.py:566
  75.8 0.0 collective-permute-start.2
  75.8 1.9 %collective-permute-done.2.other_ref = f32[1024,128]{1,0:T(8,128)S(1)} collective-permute-done((f32[1024,128]{1,0:T(8,128)S(1)}, f32[1024,128]{1,0:T(8,128)S(1)}, u32[]{:S(2)}, u32[]{:S(2)}) %collective-permute-start.2) | collective-permute-done | bytes 524320 | tf_op jit(solution)/shard_map/ppermute | solution.py:29
  77.7 0.0 all-to-all-done.2
  77.7 1.6 %join_grads.1 = bf16[1024,128]{1,0:T(8,128)(2,1)} custom-call(s32[8,1,3]{2,1,0:T(1,128)S(1)} %all_to_all.28.home_ref, f32[1024,128]{1,0:T(8,128)S(1)} %get-tuple-element.26.keep_ref, f32[1024,128]{1,0:T(8,128)S(1)} %collective-permute-done.2.other_ref, bf16[1536,128]{1,0:T(8,128)(2,1)S(1)} %bitcast.11), custom_call_target="tpu_custom_call" | custom-call | tf_op jit(solution)/shard_map/join_grads/pallas_call | solution.py:594
Async XLA Ops:
  0.6 14.7 %collective-permute-start = (bf16[1024,128]{1,0:T(8,128)(2,1)}, bf16[1024,128]{1,0:T(8,128)(2,1)S(1)}, u32[]{:S(2)}, u32[]{:S(2)}) collective-permute-start(bf16[1024,128]{1,0:T(8,128)(2,1)} %bitcast.14), channel_id=1, source_target_pairs={{0,1},{1,0},{2,3},{3,2},{4,5},{5,4},{6,7},{7,6},{8,9},{9,8},{10,11... | collective-permute-start | bytes 786440 | tf_op jit(solution)/shard_map/ppermute | solution.py:29
  15.3 5.3 %copy-start = (bf16[1024,128]{1,0:T(8,128)(2,1)}, bf16[1024,128]{1,0:T(8,128)(2,1)S(1)}, u32[]{:S(2)}) copy-start(bf16[1024,128]{1,0:T(8,128)(2,1)S(1)} %collective-permute-done.theirs_ref) | copy-start | bytes 786436
  17.2 14.9 %all-to-all-start.1 = ((bf16[8,192,128]{2,1,0:T(8,128)(2,1)}), bf16[8,192,128]{2,1,0:T(8,128)(2,1)S(1)}, u32[]{:S(2)}, u32[]{:S(2)}) async-start(bf16[8,192,128]{2,1,0:T(8,128)(2,1)} %bitcast.3), calls=%async_computation.1 | async-start | bytes 786432 | tf_op jit(solution)/shard_map/all_to_all | solution.py:497
  32.1 1.8 %collective-permute-start.1 = (bf16[1536,128]{1,0:T(8,128)(2,1)S(1)}, bf16[1536,128]{1,0:T(8,128)(2,1)S(1)}, u32[]{:S(2)}, u32[]{:S(2)}) collective-permute-start(bf16[1536,128]{1,0:T(8,128)(2,1)S(1)} %bitcast.12), channel_id=1, source_target_pairs={{0,1},{1,0},{2,3},{3,2},{4,5},{5,4},{6,7},{7,6},{8,9},{9,8},{10,11... | collective-permute-start | bytes 1179656 | tf_op jit(solution)/shard_map/ppermute | solution.py:29
  40.2 1.7 %collective-permute-start.3 = (bf16[1536,128]{1,0:T(8,128)(2,1)S(1)}, bf16[1536,128]{1,0:T(8,128)(2,1)S(1)}, u32[]{:S(2)}, u32[]{:S(2)}) collective-permute-start(bf16[1536,128]{1,0:T(8,128)(2,1)S(1)} %get-tuple-element.29), channel_id=1, source_target_pairs={{0,1},{1,0},{2,3},{3,2},{4,5},{5,4},{6,7},{7,6},{8,9},{9,8},{10,11... | collective-permute-start | bytes 1179656 | tf_op jit(solution)/shard_map/ppermute | solution.py:29
  42.8 34.9 %all-to-all-start.2 = ((bf16[8,192,128]{2,1,0:T(8,128)(2,1)}), bf16[8,192,128]{2,1,0:T(8,128)(2,1)S(1)}, u32[]{:S(2)}, u32[]{:S(2)}) async-start(bf16[8,192,128]{2,1,0:T(8,128)(2,1)} %bitcast.8), calls=%async_computation.2 | async-start | bytes 786432 | tf_op jit(solution)/shard_map/all_to_all | solution.py:564
  75.8 1.9 %collective-permute-start.2 = (f32[1024,128]{1,0:T(8,128)S(1)}, f32[1024,128]{1,0:T(8,128)S(1)}, u32[]{:S(2)}, u32[]{:S(2)}) collective-permute-start(f32[1024,128]{1,0:T(8,128)S(1)} %get-tuple-element.27), channel_id=1, source_target_pairs={{0,1},{1,0},{2,3},{3,2},{4,5},{5,4},{6,7},{7,6},{8,9},{9,8},{10,11... | collective-permute-start | bytes 1572872 | tf_op jit(solution)/shard_map/ppermute | solution.py:29

commit v5 on v4

--- a/solution.py
+++ b/solution.py
@@ -12,7 +12,7 @@
 SEL = 16
 CAP = 3
 WIDE = 8
-OWN_SIZES = (2, 4, 6)
+OWN_SIZES = (2, 4, 5, 6, 7)
 FAR_SIZES = (4, 7, 8)
 VMEM_LIMIT = 40 * 1024 * 1024
 SMALL_LIMIT = 8 * 1024 * 1024
@@ -82,6 +82,15 @@
     lax.fori_loop(0, STEP, run, 0)
 
 
+def each_pair(list_ref, body):
+    def run(i, _):
+        pair = [(pl.program_id(0) * STEP + j, j) for j in (2 * i, 2 * i + 1)]
+        body(i, pair, jnp.maximum(list_ref[pair[0][0], SEL], list_ref[pair[1][0], SEL]))
+        return 0
+
+    lax.fori_loop(0, STEP // 2, run, 0)
+
+
 def pick(list_ref, b, start, size):
     count = list_ref[b, SEL]
     return (
@@ -109,7 +118,7 @@
 
 
 def in_parts(count, run):
-    wide = (count + 1) // WIDE
+    wide = count // WIDE
 
     def full(c, _):
         run(c * WIDE, WIDE)
@@ -133,65 +142,66 @@
     def _():
         lay_halves(par_ref, mine_ref, theirs_ref, kv_ref)
 
-    def block(b, j, again=False):
+    def scores(b, j, half, start, size):
+        picks, real = pick(list_ref, b, start, size)
+        load_tiles(kv_ref, k_ref.at[half], v_ref.at[half], picks)
+        return dot(k_ref[half, : size * TILE], q_ref[span(j, rows), :], NT) * scale, real
+
+    def run(b, j, half, start, size, fresh):
+        x, real = scores(b, j, half, start, size)
+        dp = dot(v_ref[half, : size * TILE], do_ref[span(j, rows), :], NT)
+        base = sum_ref[j, 0]
+        if fresh:
+            base = jnp.where(start == 0, pick_diagonal(x[part(0)], group), base)
+            sum_ref[j, 0] = base
+        base = base[0:1]
+        total, dotted = sum_ref[j, 1], sum_ref[j, 2]
+        for i in range(size):
+            xi = mask_diagonal(x[part(i)], start == 0, group) if i == 0 else x[part(i)]
+            e = jnp.exp2(xi - jnp.where(real[i], base, HIGH))
+            total = total + fold(e, jnp.add)
+            dotted = dotted + fold(e * dp[part(i)], jnp.add)
+        sum_ref[j, 1] = total
+        sum_ref[j, 2] = dotted
+
+    def first(_, pair, count):
+        def both(start, size):
+            for half, (b, j) in enumerate(pair):
+                run(b, j, half, start, size, True)
+
+        in_parts(count, both)
+
+    def anew(b, j):
         count = list_ref[b, SEL]
-        q_at = span(j, rows)
-        sums = sum_ref.at[j]
-
-        def scores(start, size):
-            picks, real = pick(list_ref, b, start, size)
-            load_tiles(kv_ref, k_ref, v_ref, picks)
-            return dot(k_ref[: size * TILE], q_ref[q_at, :], NT) * scale, real
-
-        def run(start, size):
-            x, real = scores(start, size)
-            dp = dot(v_ref[: size * TILE], do_ref[q_at, :], NT)
-            base = sums[0]
-            if not again:
-                base = jnp.where(start == 0, pick_diagonal(x[part(0)], group), base)
-                sums[0] = base
-            base = base[0:1]
-            total, dotted = sums[1], sums[2]
-            for i in range(size):
-                xi = mask_diagonal(x[part(i)], start == 0, group) if i == 0 else x[part(i)]
-                e = jnp.exp2(xi - jnp.where(real[i], base, HIGH))
-                total = total + fold(e, jnp.add)
-                dotted = dotted + fold(e * dp[part(i)], jnp.add)
-            sums[1] = total
-            sums[2] = dotted
-
-        if not again:
-            sums[...] = jnp.zeros_like(sums)
-            in_parts(count, run)
-            return
-
         size = OWN_SIZES[0]
-        sums[0] = jnp.full(sums.shape[1:], LOW, jnp.float32)
+        clear = jnp.zeros(sum_ref.shape[2:], jnp.float32)
+        sum_ref[j, 0] = clear + LOW
 
         def look(c, _):
-            x, real = scores(c * size, size)
-            top = sums[0]
+            x, real = scores(b, j, 0, c * size, size)
+            top = sum_ref[j, 0]
             for i in range(size):
                 xi = mask_diagonal(x[part(i)], c == 0, group) if i == 0 else x[part(i)]
                 top = jnp.maximum(top, jnp.where(real[i], fold(xi, jnp.maximum), LOW))
-            sums[0] = top
+            sum_ref[j, 0] = top
             return 0
 
-        def anew(c, _):
-            run(c * size, size)
+        def once_more(c, _):
+            run(b, j, 0, c * size, size, False)
             return 0
 
         lax.fori_loop(0, pl.cdiv(count, size), look, 0)
-        sums[0] = jnp.broadcast_to(jnp.max(sums[0], axis=0, keepdims=True), sums.shape[1:])
-        sums[1] = jnp.zeros(sums.shape[1:], jnp.float32)
-        sums[2] = jnp.zeros(sums.shape[1:], jnp.float32)
-        lax.fori_loop(0, pl.cdiv(count, size), anew, 0)
-
-    each_block(block)
+        sum_ref[j, 0] = clear + jnp.max(sum_ref[j, 0], axis=0, keepdims=True)
+        sum_ref[j, 1] = clear
+        sum_ref[j, 2] = clear
+        lax.fori_loop(0, pl.cdiv(count, size), once_more, 0)
+
+    sum_ref[...] = jnp.zeros_like(sum_ref)
+    each_pair(list_ref, first)
 
     @pl.when(jnp.max(sum_ref[:, 1]) > TOO_LARGE)
     def _():
-        each_block(functools.partial(block, again=True))
+        each_block(anew)
 
     for j in range(STEP):
         st_ref[j, 0:1] = sum_ref[j, 0, 0:1]
@@ -295,16 +305,7 @@
         add_grads(acc_ref, picks, dot(ds, q_ref[q_at, :]), dot(p_ref[half, :n], do_ref[q_at, :]))
         dq_ref[j] = dot(k_ref[half, :n], ds, TN)
 
-    def each_pair(body):
-        def run(i, _):
-            places = [2 * i, 2 * i + 1]
-            pair = [(pl.program_id(0) * STEP + j, j) for j in places]
-            body(pair, jnp.maximum(list_ref[pair[0][0], SEL], list_ref[pair[1][0], SEL]))
-            return 0
-
-        lax.fori_loop(0, STEP // 2, run, 0)
-
-    def first(pair, count):
+    def first(_, pair, count):
         for _, j in pair:
             begin(j, st_ref[j, 0:1])
 
@@ -314,7 +315,7 @@
 
         by_size(count, FAR_SIZES, both)
 
-    def second(pair, count):
+    def second(_, pair, count):
         for _, j in pair:
             finish(j)
 
@@ -329,13 +330,13 @@
 
         by_size(count, FAR_SIZES, both)
 
-    each_pair(first)
+    each_pair(list_ref, first)
 
     @pl.when(jnp.max(sum_ref[:, 1]) > TOO_LARGE)
     def _():
         each_block(anew)
 
-    each_pair(second)
+    each_pair(list_ref, second)
     leave_grads(inv_root, par_ref, acc_ref, keep_ref, send_ref)
 
 
@@ -353,30 +354,38 @@
     def write(j):
         out_ref[span(j, rows), :] = (dq_ref[j] * inv_root).astype(out_ref.dtype).T
 
-    def block(b, j):
+    def spread(b, j, half, start, size):
         q_at = span(j, rows)
-        dq_ref[j] = part_ref[j]
-
-        def spread(start, size):
-            picks, real = pick(list_ref, b, start, size)
-            n = size * TILE
-            load_tiles(kv_ref, k_ref, v_ref, picks)
-            level = fin_ref[j, 0:1]
-            delta = fin_ref[j, 1:2]
-            x = dot(k_ref[:n], q_ref[q_at, :], NT) * scale
-            dp = dot(v_ref[:n], do_ref[q_at, :], NT)
-            for i in range(size):
-                xi = mask_diagonal(x[part(i)], start == 0, group) if i == 0 else x[part(i)]
-                p = jnp.exp2(xi - jnp.where(real[i], level, HIGH))
-                p_ref[part(i)] = p.astype(jnp.bfloat16)
-                ds_ref[part(i)] = (p * (dp[part(i)] - delta)).astype(jnp.bfloat16)
-            write(jnp.maximum(j - 1, 0))
-            add_grads(acc_ref, picks, dot(ds_ref[:n], q_ref[q_at, :]), dot(p_ref[:n], do_ref[q_at, :]))
-            dq_ref[j] += dot(k_ref[:n], ds_ref[:n], TN)
-
-        in_parts(list_ref[b, SEL], spread)
-
-    each_block(block)
+        picks, real = pick(list_ref, b, start, size)
+        n = size * TILE
+        load_tiles(kv_ref, k_ref.at[half], v_ref.at[half], picks)
+        level = fin_ref[j, 0:1]
+        delta = fin_ref[j, 1:2]
+        x = dot(k_ref[half, :n], q_ref[q_at, :], NT) * scale
+        dp = dot(v_ref[half, :n], do_ref[q_at, :], NT)
+        for i in range(size):
+            xi = mask_diagonal(x[part(i)], start == 0, group) if i == 0 else x[part(i)]
+            p = jnp.exp2(xi - jnp.where(real[i], level, HIGH))
+            p_ref[half, part(i)] = p.astype(jnp.bfloat16)
+            ds_ref[half, part(i)] = (p * (dp[part(i)] - delta)).astype(jnp.bfloat16)
+        ds = ds_ref[half, :n]
+        add_grads(acc_ref, picks, dot(ds, q_ref[q_at, :]), dot(p_ref[half, :n], do_ref[q_at, :]))
+        dq_ref[j] += dot(k_ref[half, :n], ds, TN)
+
+    def work(i, pair, count):
+        for _, j in pair:
+            dq_ref[j] = part_ref[j]
+        before = 2 * jnp.maximum(i - 1, 0)
+
+        def both(start, size):
+            for half, (b, j) in enumerate(pair):
+                spread(b, j, half, start, size)
+                write(before + half)
+
+        in_parts(count, both)
+
+    each_pair(list_ref, work)
+    write(STEP - 2)
     write(STEP - 1)
     leave_grads(inv_root, par_ref, acc_ref, keep_ref, send_ref)
 
@@ -412,7 +421,9 @@
     named = sel[:, 0:1] == tile
     for s in range(1, SEL):
         named = named | (sel[:, s : s + 1] == tile)
-    is_own = tile // blocks == me
+    is_own = (tile // blocks == me) & (
+        (me > 0) | (tile >= CAP) | (tile == lax.broadcasted_iota(jnp.int32, tile.shape, 0))
+    )
     own = jnp.where(named & is_own, 1.0, 0.0)
     far = jnp.where(named & jnp.logical_not(is_own), 1.0, 0.0)
     wanted = jnp.max(far, axis=0, keepdims=True)
@@ -507,8 +518,8 @@
     one = 2 * rows * TILE * dim
     bf16 = jnp.bfloat16
     own_rows, far_rows = (tok_rows, dim), (far * TILE, dim)
-    some_keys = [pltpu.VMEM((WIDE * TILE, dim), bf16)] * 2
-    some_probs = [pltpu.VMEM((WIDE * TILE, rows), bf16)] * 2
+    some_keys = [pltpu.VMEM((2, WIDE * TILE, dim), bf16)] * 2
+    some_probs = [pltpu.VMEM((2, WIDE * TILE, rows), bf16)] * 2
 
     stats = pl.pallas_call(
         functools.partial(own_stats, scale, heads),
@@ -550,8 +561,8 @@
                 pltpu.VMEM((STEP, WIDE * TILE, rows), f32),
                 pltpu.VMEM((STEP, 3, 8, rows), f32),
             ]
-            + [pltpu.VMEM((2, WIDE * TILE, dim), bf16)] * 2
-            + [pltpu.VMEM((2, WIDE * TILE, rows), bf16)] * 2,
+            + some_keys
+            + some_probs,
         ),
         compiler_params=params,
         cost_estimate=pl.CostEstimate(

time: 79.4 us -> 74.9 us (0.943); the launches traced: 79.3 us -> 73.6 us
  starting transfers between devices: 18.2 us -> 12 us
  waiting for transfers between devices: 5.21 us -> 8.87 us
  Pallas kernels: 41.2 us -> 38.1 us
    all_to_all x1, starting transfers between devices: 14 us -> 7.87 us  [on_device(): came = lax.all_to_all(back, 'seq', split_axis=0, concat_axis=0, tiled=True)]
    pallas_call x1, Pallas kernels: 6.33 us -> 12.1 us  [on_device(): pl.pallas_call(functools.partial(far_grads, scale, inv_root), out_shape=(...]
    pallas_call x1, Pallas kernels: 19 us -> 14 us  [on_device(): pl.pallas_call(functools.partial(own_grads, scale, inv_root, heads), out_...]
    pallas_call x1, Pallas kernels: 11.4 us -> 7.45 us  [on_device(): pl.pallas_call(functools.partial(own_stats, scale, heads), out_shape=jax....]
    all_to_all x1, waiting for transfers between devices: 0.01 us -> 3.66 us  [on_device(): lax.all_to_all(reply, 'seq', split_axis=0, concat_axis=0, tiled=True)]
  transfers between devices with their start and end apart: 6 -> 6, of which waited for: 3 -> 4; matrix products, arithmetic and copies ran while one was open for 0% -> 0% of each run, Pallas kernels for 40% -> 31%
where the time goes in v5:
time: 74.9 us; the launch traced here: 73.6 us
  Pallas kernels  38.1 us (51%)
  blocking collectives  13.1 us (17%)
  starting transfers between devices  12 us (16%)
  waiting for transfers between devices  8.87 us (12%)
  other arithmetic  0.87 us (1%)
    pallas_call x1, Pallas kernels, on_device(): pl.pallas_call(functools.partial(own_grads, scale, inv_root, heads), out_...  14 us
    all_to_all x1, blocking collectives, on_device(): home = lax.all_to_all(asked, 'seq', split_axis=0, concat_axis=0, tiled=True)  13.1 us
    pallas_call x1, Pallas kernels, on_device(): pl.pallas_call(functools.partial(far_grads, scale, inv_root), out_shape=(...  12.1 us
    all_to_all x1, starting transfers between devices, on_device(): came = lax.all_to_all(back, 'seq', split_axis=0, concat_axis=0, tiled=True)  7.87 us
    pallas_call x1, Pallas kernels, on_device(): pl.pallas_call(functools.partial(own_stats, scale, heads), out_shape=jax....  7.45 us
    ppermute x4, waiting for transfers between devices, swap_pair(): return lax.ppermute(block, 'head', [(h, h ^ 1) for h in range(count)])  5.21 us
    all_to_all x1, waiting for transfers between devices, on_device(): lax.all_to_all(reply, 'seq', split_axis=0, concat_axis=0, tiled=True)  3.66 us
    all_to_all x1, starting transfers between devices, on_device(): lax.all_to_all(reply, 'seq', split_axis=0, concat_axis=0, tiled=True)  3.45 us
  transfers between devices with their start and end apart: 6, of which 4 were waited for; matrix products, arithmetic and copies ran while one was open for 0% of the time, Pallas kernels for 31%

profile of v5, /device:TPU:0, one launch (start us, length us, event | category | flops | bytes accessed | tf_op | source)
XLA Modules:
  0.0 73.6 jit_solution(14793853453749762104)
XLA Ops:
  0.6 0.5 collective-permute-start
  1.1 1.1 %plan.1 = (s32[8,1,3]{2,1,0:T(1,128)S(1)}, s32[16,17]{1,0:T(8,128)S(1)}, s32[16,17]{1,0:T(8,128)S(1)}) custom-call(s32[1]{0:T(128)} %bitcast.me_ref, s32[16,16]{1,0:T(8,128)} %sel_ref.1), custom_call_target="tpu_custom_call" | custom-call | tf_op jit(solution)/shard_map/plan/pallas_call | solution.py:485
  2.2 13.1 %all_to_all.28.home_ref = s32[8,1,3]{2,1,0:T(1,128)S(1)} all-to-all(s32[8,1,3]{2,1,0:T(1,128)S(1)} %get-tuple-element.18), channel_id=1, replica_groups=mesh['seq'=8,'head'=4] {'seq'}, dimensions={0} | all-to-all | bytes 192 | tf_op jit(solution)/shard_map/all_to_all | solution.py:497
  15.3 0.0 collective-permute-done.theirs_ref
  15.3 0.0 copy-start
  15.3 1.8 %fill_reply.1 = bf16[1536,128]{1,0:T(8,128)(2,1)} custom-call(s32[8,1,3]{2,1,0:T(1,128)S(1)} %all_to_all.28.home_ref, bf16[1024,128]{1,0:T(8,128)(2,1)} %bitcast.15), custom_call_target="tpu_custom_call" | custom-call | tf_op jit(solution)/shard_map/fill_reply/pallas_call | solution.py:500
  17.2 3.5 %all-to-all-start.1 = ((bf16[8,192,128]{2,1,0:T(8,128)(2,1)}), bf16[8,192,128]{2,1,0:T(8,128)(2,1)S(1)}, u32[]{:S(2)}, u32[]{:S(2)}) async-start(bf16[8,192,128]{2,1,0:T(8,128)(2,1)} %bitcast.3), calls=%async_computation.1 | async-start | bytes 786432 | tf_op jit(solution)/shard_map/all_to_all | solution.py:508
  20.6 0.0 copy-done
  20.7 7.5 %own_stats.1.st_ref = f32[16,8,512]{2,1,0:T(8,128)S(1)} custom-call(s32[16,17]{1,0:T(8,128)S(1)} %get-tuple-element.16.list_ref, s32[1]{0:T(128)} %bitcast.1.par_ref, bf16[8192,128]{1,0:T(8,128)(2,1)} %bitcast.19, bf16[8192,128]{1,0:T(8,128)(2,1)} %bitcast.22, bf16[1024,128]{1,0:T(8,128)(2,1)} %bitcast.16, bf16[1024,128]{1,0:T(8,128)(2,1)} %copy-done), custom_call_target="tpu_custom_call" | custom-call | flops 2147483648 | bytes 4194304 | tf_op jit(solution)/shard_map/own_stats/pallas_call | solution.py:524
  28.1 3.7 %all-to-all-done.1 = bf16[8,192,128]{2,1,0:T(8,128)(2,1)S(1)} async-done(((bf16[8,192,128]{2,1,0:T(8,128)(2,1)}), bf16[8,192,128]{2,1,0:T(8,128)(2,1)S(1)}, u32[]{:S(2)}, u32[]{:S(2)}) %all-to-all-start.1) | async-done | bytes 393248 | tf_op jit(solution)/shard_map/all_to_all | solution.py:508
  31.8 0.0 collective-permute-start.1
  31.8 1.7 %collective-permute-done.1.theirs_ref = bf16[1536,128]{1,0:T(8,128)(2,1)S(1)} collective-permute-done((bf16[1536,128]{1,0:T(8,128)(2,1)S(1)}, bf16[1536,128]{1,0:T(8,128)(2,1)S(1)}, u32[]{:S(2)}, u32[]{:S(2)}) %collective-permute-start.1) | collective-permute-done | bytes 393248 | tf_op jit(solution)/shard_map/ppermute | solution.py:29
  33.5 12.1 %far_grads.1 = (f32[16,8,512]{2,1,0:T(8,128)}, f32[16,128,512]{2,1,0:T(8,128)}, f32[1536,128]{1,0:T(8,128)S(1)}, bf16[1536,128]{1,0:T(8,128)(2,1)S(1)}) custom-call(s32[16,17]{1,0:T(8,128)S(1)} %get-tuple-element.17.list_ref, s32[1]{0:T(128)} %bitcast.1.par_ref, f32[16,8,512]{2,1,0:T(8,128)S(1)} %own_stats.1.st_ref, bf16[8192,128]{1,0:T(8,128)(2,1)} %bitcast.20, ...), custom_call_target="tpu_custom_call" | custom-call | flops 4026531840 | bytes 8388608 | tf_op jit(solution)/shard_map/far_grads/pallas_call | solution.py:544
  45.6 0.1 collective-permute-start.3
  45.7 1.6 %collective-permute-done.3 = bf16[1536,128]{1,0:T(8,128)(2,1)S(1)} collective-permute-done((bf16[1536,128]{1,0:T(8,128)(2,1)S(1)}, bf16[1536,128]{1,0:T(8,128)(2,1)S(1)}, u32[]{:S(2)}, u32[]{:S(2)}) %collective-permute-start.3) | collective-permute-done | bytes 393248 | tf_op jit(solution)/shard_map/ppermute | solution.py:29
  47.3 0.9 %add_convert_fusion = bf16[1536,128]{1,0:T(8,128)(2,1)} fusion(f32[1536,128]{1,0:T(8,128)S(1)} %get-tuple-element.28, bf16[1536,128]{1,0:T(8,128)(2,1)S(1)} %collective-permute-done.3), kind=kLoop, calls=%fused_computation | loop fusion | flops 589824 | bytes 1572864 | tf_op jit(solution)/shard_map/convert_element_type | solution.py:574
  48.2 7.9 %all-to-all-start.2 = ((bf16[8,192,128]{2,1,0:T(8,128)(2,1)}), bf16[8,192,128]{2,1,0:T(8,128)(2,1)S(1)}, u32[]{:S(2)}, u32[]{:S(2)}) async-start(bf16[8,192,128]{2,1,0:T(8,128)(2,1)} %bitcast.8), calls=%async_computation.2 | async-start | bytes 786432 | tf_op jit(solution)/shard_map/all_to_all | solution.py:575
  56.0 14.0 %own_grads.1 = (bf16[8192,128]{1,0:T(8,128)(2,1)}, f32[1024,128]{1,0:T(8,128)S(1)}, f32[1024,128]{1,0:T(8,128)S(1)}) custom-call(s32[16,17]{1,0:T(8,128)S(1)} %get-tuple-element.16.list_ref, s32[1]{0:T(128)} %bitcast.1.par_ref, f32[16,8,512]{2,1,0:T(8,128)} %get-tuple-element.23.fin_ref, f32[16,128,512]{2,1,0:T(8,128)} %get-tuple-element.24.part_ref, ...), custom_call_target="tpu_custom_call" | custom-call | flops 5368709120 | bytes 10485760 | tf_op jit(solution)/shard_map/own_grads/pallas_call | solution.py:577
  70.1 0.0 collective-permute-start.2
  70.1 1.9 %collective-permute-done.2.other_ref = f32[1024,128]{1,0:T(8,128)S(1)} collective-permute-done((f32[1024,128]{1,0:T(8,128)S(1)}, f32[1024,128]{1,0:T(8,128)S(1)}, u32[]{:S(2)}, u32[]{:S(2)}) %collective-permute-start.2) | collective-permute-done | bytes 524320 | tf_op jit(solution)/shard_map/ppermute | solution.py:29
  72.0 0.0 all-to-all-done.2
  72.0 1.6 %join_grads.1 = bf16[1024,128]{1,0:T(8,128)(2,1)} custom-call(s32[8,1,3]{2,1,0:T(1,128)S(1)} %all_to_all.28.home_ref, f32[1024,128]{1,0:T(8,128)S(1)} %get-tuple-element.26.keep_ref, f32[1024,128]{1,0:T(8,128)S(1)} %collective-permute-done.2.other_ref, bf16[1536,128]{1,0:T(8,128)(2,1)S(1)} %bitcast.11), custom_call_target="tpu_custom_call" | custom-call | tf_op jit(solution)/shard_map/join_grads/pallas_call | solution.py:605
Async XLA Ops:
  0.6 14.7 %collective-permute-start = (bf16[1024,128]{1,0:T(8,128)(2,1)}, bf16[1024,128]{1,0:T(8,128)(2,1)S(1)}, u32[]{:S(2)}, u32[]{:S(2)}) collective-permute-start(bf16[1024,128]{1,0:T(8,128)(2,1)} %bitcast.14), channel_id=1, source_target_pairs={{0,1},{1,0},{2,3},{3,2},{4,5},{5,4},{6,7},{7,6},{8,9},{9,8},{10,11... | collective-permute-start | bytes 786440 | tf_op jit(solution)/shard_map/ppermute | solution.py:29
  15.3 5.3 %copy-start = (bf16[1024,128]{1,0:T(8,128)(2,1)}, bf16[1024,128]{1,0:T(8,128)(2,1)S(1)}, u32[]{:S(2)}) copy-start(bf16[1024,128]{1,0:T(8,128)(2,1)S(1)} %collective-permute-done.theirs_ref) | copy-start | bytes 786436
  17.2 14.6 %all-to-all-start.1 = ((bf16[8,192,128]{2,1,0:T(8,128)(2,1)}), bf16[8,192,128]{2,1,0:T(8,128)(2,1)S(1)}, u32[]{:S(2)}, u32[]{:S(2)}) async-start(bf16[8,192,128]{2,1,0:T(8,128)(2,1)} %bitcast.3), calls=%async_computation.1 | async-start | bytes 786432 | tf_op jit(solution)/shard_map/all_to_all | solution.py:508
  31.8 1.7 %collective-permute-start.1 = (bf16[1536,128]{1,0:T(8,128)(2,1)S(1)}, bf16[1536,128]{1,0:T(8,128)(2,1)S(1)}, u32[]{:S(2)}, u32[]{:S(2)}) collective-permute-start(bf16[1536,128]{1,0:T(8,128)(2,1)S(1)} %bitcast.12), channel_id=1, source_target_pairs={{0,1},{1,0},{2,3},{3,2},{4,5},{5,4},{6,7},{7,6},{8,9},{9,8},{10,11... | collective-permute-start | bytes 1179656 | tf_op jit(solution)/shard_map/ppermute | solution.py:29
  45.6 1.7 %collective-permute-start.3 = (bf16[1536,128]{1,0:T(8,128)(2,1)S(1)}, bf16[1536,128]{1,0:T(8,128)(2,1)S(1)}, u32[]{:S(2)}, u32[]{:S(2)}) collective-permute-start(bf16[1536,128]{1,0:T(8,128)(2,1)S(1)} %get-tuple-element.29), channel_id=1, source_target_pairs={{0,1},{1,0},{2,3},{3,2},{4,5},{5,4},{6,7},{7,6},{8,9},{9,8},{10,11... | collective-permute-start | bytes 1179656 | tf_op jit(solution)/shard_map/ppermute | solution.py:29
  48.2 23.8 %all-to-all-start.2 = ((bf16[8,192,128]{2,1,0:T(8,128)(2,1)}), bf16[8,192,128]{2,1,0:T(8,128)(2,1)S(1)}, u32[]{:S(2)}, u32[]{:S(2)}) async-start(bf16[8,192,128]{2,1,0:T(8,128)(2,1)} %bitcast.8), calls=%async_computation.2 | async-start | bytes 786432 | tf_op jit(solution)/shard_map/all_to_all | solution.py:575
  70.1 1.9 %collective-permute-start.2 = (f32[1024,128]{1,0:T(8,128)S(1)}, f32[1024,128]{1,0:T(8,128)S(1)}, u32[]{:S(2)}, u32[]{:S(2)}) collective-permute-start(f32[1024,128]{1,0:T(8,128)S(1)} %get-tuple-element.27), channel_id=1, source_target_pairs={{0,1},{1,0},{2,3},{3,2},{4,5},{5,4},{6,7},{7,6},{8,9},{9,8},{10,11... | collective-permute-start | bytes 1572872 | tf_op jit(solution)/shard_map/ppermute | solution.py:29

commit v6 on v5

--- a/solution.py
+++ b/solution.py
@@ -16,6 +16,7 @@
 FAR_SIZES = (4, 7, 8)
 VMEM_LIMIT = 40 * 1024 * 1024
 SMALL_LIMIT = 8 * 1024 * 1024
+OWN_GROUP, FAR_GROUP = 2, 4
 STEP = 4
 LOW = -1e30
 HIGH = 1e30
@@ -82,13 +83,13 @@
     lax.fori_loop(0, STEP, run, 0)
 
 
-def each_pair(list_ref, body):
+def each_group(list_ref, size, body):
     def run(i, _):
-        pair = [(pl.program_id(0) * STEP + j, j) for j in (2 * i, 2 * i + 1)]
-        body(i, pair, jnp.maximum(list_ref[pair[0][0], SEL], list_ref[pair[1][0], SEL]))
+        group = [(pl.program_id(0) * STEP + size * i + j, size * i + j) for j in range(size)]
+        body(i, group, functools.reduce(jnp.maximum, [list_ref[b, SEL] for b, _ in group]))
         return 0
 
-    lax.fori_loop(0, STEP // 2, run, 0)
+    lax.fori_loop(0, STEP // size, run, 0)
 
 
 def pick(list_ref, b, start, size):
@@ -197,7 +198,7 @@
         lax.fori_loop(0, pl.cdiv(count, size), once_more, 0)
 
     sum_ref[...] = jnp.zeros_like(sum_ref)
-    each_pair(list_ref, first)
+    each_group(list_ref, OWN_GROUP, first)
 
     @pl.when(jnp.max(sum_ref[:, 1]) > TOO_LARGE)
     def _():
@@ -330,13 +331,13 @@
 
         by_size(count, FAR_SIZES, both)
 
-    each_pair(list_ref, first)
+    each_group(list_ref, FAR_GROUP, first)
 
     @pl.when(jnp.max(sum_ref[:, 1]) > TOO_LARGE)
     def _():
         each_block(anew)
 
-    each_pair(list_ref, second)
+    each_group(list_ref, FAR_GROUP, second)
     leave_grads(inv_root, par_ref, acc_ref, keep_ref, send_ref)
 
 
@@ -384,7 +385,7 @@
 
         in_parts(count, both)
 
-    each_pair(list_ref, work)
+    each_group(list_ref, OWN_GROUP, work)
     write(STEP - 2)
     write(STEP - 1)
     leave_grads(inv_root, par_ref, acc_ref, keep_ref, send_ref)
@@ -518,8 +519,10 @@
     one = 2 * rows * TILE * dim
     bf16 = jnp.bfloat16
     own_rows, far_rows = (tok_rows, dim), (far * TILE, dim)
-    some_keys = [pltpu.VMEM((2, WIDE * TILE, dim), bf16)] * 2
-    some_probs = [pltpu.VMEM((2, WIDE * TILE, rows), bf16)] * 2
+    far_keys = [pltpu.VMEM((FAR_GROUP, WIDE * TILE, dim), bf16)] * 2
+    far_probs = [pltpu.VMEM((FAR_GROUP, WIDE * TILE, rows), bf16)] * 2
+    some_keys = [pltpu.VMEM((OWN_GROUP, WIDE * TILE, dim), bf16)] * 2
+    some_probs = [pltpu.VMEM((OWN_GROUP, WIDE * TILE, rows), bf16)] * 2
 
     stats = pl.pallas_call(
         functools.partial(own_stats, scale, heads),
@@ -561,8 +564,8 @@
                 pltpu.VMEM((STEP, WIDE * TILE, rows), f32),
                 pltpu.VMEM((STEP, 3, 8, rows), f32),
             ]
-            + some_keys
-            + some_probs,
+            + far_keys
+            + far_probs,
         ),
         compiler_params=params,
         cost_estimate=pl.CostEstimate(

time: 74.9 us -> 73.4 us (0.980); the launches traced: 73.6 us -> 73 us
    pallas_call x1, Pallas kernels: 12.1 us -> 10.5 us  [on_device(): pl.pallas_call(functools.partial(far_grads, scale, inv_root), out_shape=(...]
    pallas_call x1, Pallas kernels: 14 us -> 15.1 us  [on_device(): pl.pallas_call(functools.partial(own_grads, scale, inv_root, heads), out_...]
  transfers between devices with their start and end apart: 6 -> 6, of which waited for: 4 -> 4; matrix products, arithmetic and copies ran while one was open for 0% -> 0% of each run, Pallas kernels for 31% -> 33%
where the time goes in v6:
time: 73.4 us; the launch traced here: 73 us
  Pallas kernels  38.1 us (52%)
  blocking collectives  13.1 us (18%)
  starting transfers between devices  11.8 us (16%)
  waiting for transfers between devices  8.34 us (11%)
  other arithmetic  0.87 us (1%)
    pallas_call x1, Pallas kernels, on_device(): pl.pallas_call(functools.partial(own_grads, scale, inv_root, heads), out_...  15.1 us
    all_to_all x1, blocking collectives, on_device(): home = lax.all_to_all(asked, 'seq', split_axis=0, concat_axis=0, tiled=True)  13.1 us
    pallas_call x1, Pallas kernels, on_device(): pl.pallas_call(functools.partial(far_grads, scale, inv_root), out_shape=(...  10.5 us
    pallas_call x1, Pallas kernels, on_device(): pl.pallas_call(functools.partial(own_stats, scale, heads), out_shape=jax....  7.99 us
    all_to_all x1, starting transfers between devices, on_device(): came = lax.all_to_all(back, 'seq', split_axis=0, concat_axis=0, tiled=True)  7.73 us
    ppermute x4, waiting for transfers between devices, swap_pair(): return lax.ppermute(block, 'head', [(h, h ^ 1) for h in range(count)])  5.21 us
    all_to_all x1, starting transfers between devices, on_device(): lax.all_to_all(reply, 'seq', split_axis=0, concat_axis=0, tiled=True)  3.45 us
    all_to_all x1, waiting for transfers between devices, on_device(): lax.all_to_all(reply, 'seq', split_axis=0, concat_axis=0, tiled=True)  3.12 us
  transfers between devices with their start and end apart: 6, of which 4 were waited for; matrix products, arithmetic and copies ran while one was open for 0% of the time, Pallas kernels for 33%

profile of v6, /device:TPU:0, one launch (start us, length us, event | category | flops | bytes accessed | tf_op | source)
XLA Modules:
  0.0 73.0 jit_solution(2536769170333390735)
XLA Ops:
  0.6 0.5 collective-permute-start
  1.1 1.1 %plan.1 = (s32[8,1,3]{2,1,0:T(1,128)S(1)}, s32[16,17]{1,0:T(8,128)S(1)}, s32[16,17]{1,0:T(8,128)S(1)}) custom-call(s32[1]{0:T(128)} %bitcast.me_ref, s32[16,16]{1,0:T(8,128)} %sel_ref.1), custom_call_target="tpu_custom_call" | custom-call | tf_op jit(solution)/shard_map/plan/pallas_call | solution.py:486
  2.2 13.1 %all_to_all.28.home_ref = s32[8,1,3]{2,1,0:T(1,128)S(1)} all-to-all(s32[8,1,3]{2,1,0:T(1,128)S(1)} %get-tuple-element.18), channel_id=1, replica_groups=mesh['seq'=8,'head'=4] {'seq'}, dimensions={0} | all-to-all | bytes 192 | tf_op jit(solution)/shard_map/all_to_all | solution.py:498
  15.3 0.0 collective-permute-done.theirs_ref
  15.3 0.0 copy-start
  15.3 1.8 %fill_reply.1 = bf16[1536,128]{1,0:T(8,128)(2,1)} custom-call(s32[8,1,3]{2,1,0:T(1,128)S(1)} %all_to_all.28.home_ref, bf16[1024,128]{1,0:T(8,128)(2,1)} %bitcast.15), custom_call_target="tpu_custom_call" | custom-call | tf_op jit(solution)/shard_map/fill_reply/pallas_call | solution.py:501
  17.2 3.5 %all-to-all-start.1 = ((bf16[8,192,128]{2,1,0:T(8,128)(2,1)}), bf16[8,192,128]{2,1,0:T(8,128)(2,1)S(1)}, u32[]{:S(2)}, u32[]{:S(2)}) async-start(bf16[8,192,128]{2,1,0:T(8,128)(2,1)} %bitcast.3), calls=%async_computation.1 | async-start | bytes 786432 | tf_op jit(solution)/shard_map/all_to_all | solution.py:509
  20.6 0.0 copy-done
  20.7 8.0 %own_stats.1.st_ref = f32[16,8,512]{2,1,0:T(8,128)S(1)} custom-call(s32[16,17]{1,0:T(8,128)S(1)} %get-tuple-element.16.list_ref, s32[1]{0:T(128)} %bitcast.1.par_ref, bf16[8192,128]{1,0:T(8,128)(2,1)} %bitcast.19, bf16[8192,128]{1,0:T(8,128)(2,1)} %bitcast.22, bf16[1024,128]{1,0:T(8,128)(2,1)} %bitcast.16, bf16[1024,128]{1,0:T(8,128)(2,1)} %copy-done), custom_call_target="tpu_custom_call" | custom-call | flops 2147483648 | bytes 4194304 | tf_op jit(solution)/shard_map/own_stats/pallas_call | solution.py:527
  28.7 3.1 %all-to-all-done.1 = bf16[8,192,128]{2,1,0:T(8,128)(2,1)S(1)} async-done(((bf16[8,192,128]{2,1,0:T(8,128)(2,1)}), bf16[8,192,128]{2,1,0:T(8,128)(2,1)S(1)}, u32[]{:S(2)}, u32[]{:S(2)}) %all-to-all-start.1) | async-done | bytes 393248 | tf_op jit(solution)/shard_map/all_to_all | solution.py:509
  31.8 0.0 collective-permute-start.1
  31.8 1.7 %collective-permute-done.1.theirs_ref = bf16[1536,128]{1,0:T(8,128)(2,1)S(1)} collective-permute-done((bf16[1536,128]{1,0:T(8,128)(2,1)S(1)}, bf16[1536,128]{1,0:T(8,128)(2,1)S(1)}, u32[]{:S(2)}, u32[]{:S(2)}) %collective-permute-start.1) | collective-permute-done | bytes 393248 | tf_op jit(solution)/shard_map/ppermute | solution.py:30
  33.5 10.5 %far_grads.1 = (f32[16,8,512]{2,1,0:T(8,128)}, f32[16,128,512]{2,1,0:T(8,128)}, f32[1536,128]{1,0:T(8,128)S(1)}, bf16[1536,128]{1,0:T(8,128)(2,1)S(1)}) custom-call(s32[16,17]{1,0:T(8,128)S(1)} %get-tuple-element.17.list_ref, s32[1]{0:T(128)} %bitcast.1.par_ref, f32[16,8,512]{2,1,0:T(8,128)S(1)} %own_stats.1.st_ref, bf16[8192,128]{1,0:T(8,128)(2,1)} %bitcast.20, ...), custom_call_target="tpu_custom_call" | custom-call | flops 4026531840 | bytes 8388608 | tf_op jit(solution)/shard_map/far_grads/pallas_call | solution.py:547
  44.0 0.1 collective-permute-start.3
  44.2 1.6 %collective-permute-done.3 = bf16[1536,128]{1,0:T(8,128)(2,1)S(1)} collective-permute-done((bf16[1536,128]{1,0:T(8,128)(2,1)S(1)}, bf16[1536,128]{1,0:T(8,128)(2,1)S(1)}, u32[]{:S(2)}, u32[]{:S(2)}) %collective-permute-start.3) | collective-permute-done | bytes 393248 | tf_op jit(solution)/shard_map/ppermute | solution.py:30
  45.8 0.9 %add_convert_fusion = bf16[1536,128]{1,0:T(8,128)(2,1)} fusion(f32[1536,128]{1,0:T(8,128)S(1)} %get-tuple-element.28, bf16[1536,128]{1,0:T(8,128)(2,1)S(1)} %collective-permute-done.3), kind=kLoop, calls=%fused_computation | loop fusion | flops 589824 | bytes 1572864 | tf_op jit(solution)/shard_map/convert_element_type | solution.py:577
  46.6 7.7 %all-to-all-start.2 = ((bf16[8,192,128]{2,1,0:T(8,128)(2,1)}), bf16[8,192,128]{2,1,0:T(8,128)(2,1)S(1)}, u32[]{:S(2)}, u32[]{:S(2)}) async-start(bf16[8,192,128]{2,1,0:T(8,128)(2,1)} %bitcast.8), calls=%async_computation.2 | async-start | bytes 786432 | tf_op jit(solution)/shard_map/all_to_all | solution.py:578
  54.4 15.1 %own_grads.1 = (bf16[8192,128]{1,0:T(8,128)(2,1)}, f32[1024,128]{1,0:T(8,128)S(1)}, f32[1024,128]{1,0:T(8,128)S(1)}) custom-call(s32[16,17]{1,0:T(8,128)S(1)} %get-tuple-element.16.list_ref, s32[1]{0:T(128)} %bitcast.1.par_ref, f32[16,8,512]{2,1,0:T(8,128)} %get-tuple-element.23.fin_ref, f32[16,128,512]{2,1,0:T(8,128)} %get-tuple-element.24.part_ref, ...), custom_call_target="tpu_custom_call" | custom-call | flops 5368709120 | bytes 10485760 | tf_op jit(solution)/shard_map/own_grads/pallas_call | solution.py:580
  69.5 0.0 collective-permute-start.2
  69.5 1.9 %collective-permute-done.2.other_ref = f32[1024,128]{1,0:T(8,128)S(1)} collective-permute-done((f32[1024,128]{1,0:T(8,128)S(1)}, f32[1024,128]{1,0:T(8,128)S(1)}, u32[]{:S(2)}, u32[]{:S(2)}) %collective-permute-start.2) | collective-permute-done | bytes 524320 | tf_op jit(solution)/shard_map/ppermute | solution.py:30
  71.4 0.0 all-to-all-done.2
  71.4 1.6 %join_grads.1 = bf16[1024,128]{1,0:T(8,128)(2,1)} custom-call(s32[8,1,3]{2,1,0:T(1,128)S(1)} %all_to_all.28.home_ref, f32[1024,128]{1,0:T(8,128)S(1)} %get-tuple-element.26.keep_ref, f32[1024,128]{1,0:T(8,128)S(1)} %collective-permute-done.2.other_ref, bf16[1536,128]{1,0:T(8,128)(2,1)S(1)} %bitcast.11), custom_call_target="tpu_custom_call" | custom-call | tf_op jit(solution)/shard_map/join_grads/pallas_call | solution.py:608
Async XLA Ops:
  0.6 14.7 %collective-permute-start = (bf16[1024,128]{1,0:T(8,128)(2,1)}, bf16[1024,128]{1,0:T(8,128)(2,1)S(1)}, u32[]{:S(2)}, u32[]{:S(2)}) collective-permute-start(bf16[1024,128]{1,0:T(8,128)(2,1)} %bitcast.14), channel_id=1, source_target_pairs={{0,1},{1,0},{2,3},{3,2},{4,5},{5,4},{6,7},{7,6},{8,9},{9,8},{10,11... | collective-permute-start | bytes 786440 | tf_op jit(solution)/shard_map/ppermute | solution.py:30
  15.3 5.3 %copy-start = (bf16[1024,128]{1,0:T(8,128)(2,1)}, bf16[1024,128]{1,0:T(8,128)(2,1)S(1)}, u32[]{:S(2)}) copy-start(bf16[1024,128]{1,0:T(8,128)(2,1)S(1)} %collective-permute-done.theirs_ref) | copy-start | bytes 786436
  17.2 14.6 %all-to-all-start.1 = ((bf16[8,192,128]{2,1,0:T(8,128)(2,1)}), bf16[8,192,128]{2,1,0:T(8,128)(2,1)S(1)}, u32[]{:S(2)}, u32[]{:S(2)}) async-start(bf16[8,192,128]{2,1,0:T(8,128)(2,1)} %bitcast.3), calls=%async_computation.1 | async-start | bytes 786432 | tf_op jit(solution)/shard_map/all_to_all | solution.py:509
  31.8 1.7 %collective-permute-start.1 = (bf16[1536,128]{1,0:T(8,128)(2,1)S(1)}, bf16[1536,128]{1,0:T(8,128)(2,1)S(1)}, u32[]{:S(2)}, u32[]{:S(2)}) collective-permute-start(bf16[1536,128]{1,0:T(8,128)(2,1)S(1)} %bitcast.12), channel_id=1, source_target_pairs={{0,1},{1,0},{2,3},{3,2},{4,5},{5,4},{6,7},{7,6},{8,9},{9,8},{10,11... | collective-permute-start | bytes 1179656 | tf_op jit(solution)/shard_map/ppermute | solution.py:30
  44.0 1.7 %collective-permute-start.3 = (bf16[1536,128]{1,0:T(8,128)(2,1)S(1)}, bf16[1536,128]{1,0:T(8,128)(2,1)S(1)}, u32[]{:S(2)}, u32[]{:S(2)}) collective-permute-start(bf16[1536,128]{1,0:T(8,128)(2,1)S(1)} %get-tuple-element.29), channel_id=1, source_target_pairs={{0,1},{1,0},{2,3},{3,2},{4,5},{5,4},{6,7},{7,6},{8,9},{9,8},{10,11... | collective-permute-start | bytes 1179656 | tf_op jit(solution)/shard_map/ppermute | solution.py:30
  46.6 24.8 %all-to-all-start.2 = ((bf16[8,192,128]{2,1,0:T(8,128)(2,1)}), bf16[8,192,128]{2,1,0:T(8,128)(2,1)S(1)}, u32[]{:S(2)}, u32[]{:S(2)}) async-start(bf16[8,192,128]{2,1,0:T(8,128)(2,1)} %bitcast.8), calls=%async_computation.2 | async-start | bytes 786432 | tf_op jit(solution)/shard_map/all_to_all | solution.py:578
  69.5 1.9 %collective-permute-start.2 = (f32[1024,128]{1,0:T(8,128)S(1)}, f32[1024,128]{1,0:T(8,128)S(1)}, u32[]{:S(2)}, u32[]{:S(2)}) collective-permute-start(f32[1024,128]{1,0:T(8,128)S(1)} %get-tuple-element.27), channel_id=1, source_target_pairs={{0,1},{1,0},{2,3},{3,2},{4,5},{5,4},{6,7},{7,6},{8,9},{9,8},{10,11... | collective-permute-start | bytes 1572872 | tf_op jit(solution)/shard_map/ppermute | solution.py:30

commit v7 on v6

--- a/solution.py
+++ b/solution.py
@@ -369,6 +369,11 @@
             p = jnp.exp2(xi - jnp.where(real[i], level, HIGH))
             p_ref[half, part(i)] = p.astype(jnp.bfloat16)
             ds_ref[half, part(i)] = (p * (dp[part(i)] - delta)).astype(jnp.bfloat16)
+
+    def gather(b, j, half, start, size):
+        q_at = span(j, rows)
+        picks, _ = pick(list_ref, b, start, size)
+        n = size * TILE
         ds = ds_ref[half, :n]
         add_grads(acc_ref, picks, dot(ds, q_ref[q_at, :]), dot(p_ref[half, :n], do_ref[q_at, :]))
         dq_ref[j] += dot(k_ref[half, :n], ds, TN)
@@ -381,6 +386,8 @@
         def both(start, size):
             for half, (b, j) in enumerate(pair):
                 spread(b, j, half, start, size)
+            for half, (b, j) in enumerate(pair):
+                gather(b, j, half, start, size)
                 write(before + half)
 
         in_parts(count, both)

time: 73.4 us -> 72.7 us (level)
  the two profiles are of different devices: /device:TPU:0 before, /device:TPU:15 now
where the time goes in v7:
time: 72.7 us; the launch traced here: 71.9 us
  Pallas kernels  42.1 us (58%)
  starting transfers between devices  14.8 us (20%)
  blocking collectives  8.7 us (12%)
  waiting for transfers between devices  4.71 us (6%)
  other arithmetic  0.87 us (1%)
    pallas_call x1, Pallas kernels, on_device(): pl.pallas_call(functools.partial(own_grads, scale, inv_root, heads), out_...  14.7 us
    pallas_call x1, Pallas kernels, on_device(): pl.pallas_call(functools.partial(far_grads, scale, inv_root), out_shape=(...  14.7 us
    all_to_all x1, blocking collectives, on_device(): home = lax.all_to_all(asked, 'seq', split_axis=0, concat_axis=0, tiled=True)  8.7 us
    pallas_call x1, Pallas kernels, on_device(): pl.pallas_call(functools.partial(own_stats, scale, heads), out_shape=jax....  8.24 us
    all_to_all x1, starting transfers between devices, on_device(): came = lax.all_to_all(back, 'seq', split_axis=0, concat_axis=0, tiled=True)  5.61 us
    all_to_all x1, starting transfers between devices, on_device(): lax.all_to_all(reply, 'seq', split_axis=0, concat_axis=0, tiled=True)  5.44 us
    ppermute x4, waiting for transfers between devices, swap_pair(): return lax.ppermute(block, 'head', [(h, h ^ 1) for h in range(count)])  4.24 us
    ppermute x4, starting transfers between devices, swap_pair(): return lax.ppermute(block, 'head', [(h, h ^ 1) for h in range(count)])  3.74 us
  transfers between devices with their start and end apart: 6, of which 4 were waited for; matrix products, arithmetic and copies ran while one was open for 0% of the time, Pallas kernels for 33%

profile of v7, /device:TPU:15, one launch (start us, length us, event | category | flops | bytes accessed | tf_op | source)
XLA Modules:
  0.0 71.9 jit_solution(10938870908434928753)
XLA Ops:
  0.6 0.7 %collective-permute-start = (bf16[1024,128]{1,0:T(8,128)(2,1)}, bf16[1024,128]{1,0:T(8,128)(2,1)S(1)}, u32[]{:S(2)}, u32[]{:S(2)}) collective-permute-start(bf16[1024,128]{1,0:T(8,128)(2,1)} %bitcast.14), channel_id=1, source_target_pairs={{0,1},{1,0},{2,3},{3,2},{4,5},{5,4},{6,7},{7,6},{8,9},{9,8},{10,11... | collective-permute-start | bytes 786440 | tf_op jit(solution)/shard_map/ppermute | solution.py:30
  1.4 1.1 %plan.1 = (s32[8,1,3]{2,1,0:T(1,128)S(1)}, s32[16,17]{1,0:T(8,128)S(1)}, s32[16,17]{1,0:T(8,128)S(1)}) custom-call(s32[1]{0:T(128)} %bitcast.me_ref, s32[16,16]{1,0:T(8,128)} %sel_ref.1), custom_call_target="tpu_custom_call" | custom-call | tf_op jit(solution)/shard_map/plan/pallas_call | solution.py:493
  2.4 8.7 %all_to_all.28.home_ref = s32[8,1,3]{2,1,0:T(1,128)S(1)} all-to-all(s32[8,1,3]{2,1,0:T(1,128)S(1)} %get-tuple-element.18), channel_id=1, replica_groups=mesh['seq'=8,'head'=4] {'seq'}, dimensions={0} | all-to-all | bytes 192 | tf_op jit(solution)/shard_map/all_to_all | solution.py:505
  11.1 0.0 collective-permute-done.theirs_ref
  11.1 0.0 copy-start
  11.1 1.8 %fill_reply.1 = bf16[1536,128]{1,0:T(8,128)(2,1)} custom-call(s32[8,1,3]{2,1,0:T(1,128)S(1)} %all_to_all.28.home_ref, bf16[1024,128]{1,0:T(8,128)(2,1)} %bitcast.15), custom_call_target="tpu_custom_call" | custom-call | tf_op jit(solution)/shard_map/fill_reply/pallas_call | solution.py:508
  13.0 5.4 %all-to-all-start.1 = ((bf16[8,192,128]{2,1,0:T(8,128)(2,1)}), bf16[8,192,128]{2,1,0:T(8,128)(2,1)S(1)}, u32[]{:S(2)}, u32[]{:S(2)}) async-start(bf16[8,192,128]{2,1,0:T(8,128)(2,1)} %bitcast.3), calls=%async_computation.1 | async-start | bytes 786432 | tf_op jit(solution)/shard_map/all_to_all | solution.py:516
  18.4 0.0 copy-done
  18.4 8.2 %own_stats.1.st_ref = f32[16,8,512]{2,1,0:T(8,128)S(1)} custom-call(s32[16,17]{1,0:T(8,128)S(1)} %get-tuple-element.16.list_ref, s32[1]{0:T(128)} %bitcast.1.par_ref, bf16[8192,128]{1,0:T(8,128)(2,1)} %bitcast.19, bf16[8192,128]{1,0:T(8,128)(2,1)} %bitcast.22, bf16[1024,128]{1,0:T(8,128)(2,1)} %bitcast.16, bf16[1024,128]{1,0:T(8,128)(2,1)} %copy-done), custom_call_target="tpu_custom_call" | custom-call | flops 2147483648 | bytes 4194304 | tf_op jit(solution)/shard_map/own_stats/pallas_call | solution.py:534
  26.7 0.5 all-to-all-done.1
  27.2 1.7 %collective-permute-start.1 = (bf16[1536,128]{1,0:T(8,128)(2,1)S(1)}, bf16[1536,128]{1,0:T(8,128)(2,1)S(1)}, u32[]{:S(2)}, u32[]{:S(2)}) collective-permute-start(bf16[1536,128]{1,0:T(8,128)(2,1)S(1)} %bitcast.12), channel_id=1, source_target_pairs={{0,1},{1,0},{2,3},{3,2},{4,5},{5,4},{6,7},{7,6},{8,9},{9,8},{10,11... | collective-permute-start | bytes 1179656 | tf_op jit(solution)/shard_map/ppermute | solution.py:30
  28.9 1.3 %collective-permute-done.1.theirs_ref = bf16[1536,128]{1,0:T(8,128)(2,1)S(1)} collective-permute-done((bf16[1536,128]{1,0:T(8,128)(2,1)S(1)}, bf16[1536,128]{1,0:T(8,128)(2,1)S(1)}, u32[]{:S(2)}, u32[]{:S(2)}) %collective-permute-start.1) | collective-permute-done | bytes 393248 | tf_op jit(solution)/shard_map/ppermute | solution.py:30
  30.2 14.7 %far_grads.1 = (f32[16,8,512]{2,1,0:T(8,128)}, f32[16,128,512]{2,1,0:T(8,128)}, f32[1536,128]{1,0:T(8,128)S(1)}, bf16[1536,128]{1,0:T(8,128)(2,1)S(1)}) custom-call(s32[16,17]{1,0:T(8,128)S(1)} %get-tuple-element.17.list_ref, s32[1]{0:T(128)} %bitcast.1.par_ref, f32[16,8,512]{2,1,0:T(8,128)S(1)} %own_stats.1.st_ref, bf16[8192,128]{1,0:T(8,128)(2,1)} %bitcast.20, ...), custom_call_target="tpu_custom_call" | custom-call | flops 4026531840 | bytes 8388608 | tf_op jit(solution)/shard_map/far_grads/pallas_call | solution.py:554
  44.9 0.4 collective-permute-start.3
  45.2 1.4 %collective-permute-done.3 = bf16[1536,128]{1,0:T(8,128)(2,1)S(1)} collective-permute-done((bf16[1536,128]{1,0:T(8,128)(2,1)S(1)}, bf16[1536,128]{1,0:T(8,128)(2,1)S(1)}, u32[]{:S(2)}, u32[]{:S(2)}) %collective-permute-start.3) | collective-permute-done | bytes 393248 | tf_op jit(solution)/shard_map/ppermute | solution.py:30
  46.6 0.9 %add_convert_fusion = bf16[1536,128]{1,0:T(8,128)(2,1)} fusion(f32[1536,128]{1,0:T(8,128)S(1)} %get-tuple-element.28, bf16[1536,128]{1,0:T(8,128)(2,1)S(1)} %collective-permute-done.3), kind=kLoop, calls=%fused_computation | loop fusion | flops 589824 | bytes 1572864 | tf_op jit(solution)/shard_map/convert_element_type | solution.py:584
  47.4 5.6 %all-to-all-start.2 = ((bf16[8,192,128]{2,1,0:T(8,128)(2,1)}), bf16[8,192,128]{2,1,0:T(8,128)(2,1)S(1)}, u32[]{:S(2)}, u32[]{:S(2)}) async-start(bf16[8,192,128]{2,1,0:T(8,128)(2,1)} %bitcast.8), calls=%async_computation.2 | async-start | bytes 786432 | tf_op jit(solution)/shard_map/all_to_all | solution.py:585
  53.1 14.7 %own_grads.1 = (bf16[8192,128]{1,0:T(8,128)(2,1)}, f32[1024,128]{1,0:T(8,128)S(1)}, f32[1024,128]{1,0:T(8,128)S(1)}) custom-call(s32[16,17]{1,0:T(8,128)S(1)} %get-tuple-element.16.list_ref, s32[1]{0:T(128)} %bitcast.1.par_ref, f32[16,8,512]{2,1,0:T(8,128)} %get-tuple-element.23.fin_ref, f32[16,128,512]{2,1,0:T(8,128)} %get-tuple-element.24.part_ref, ...), custom_call_target="tpu_custom_call" | custom-call | flops 5368709120 | bytes 10485760 | tf_op jit(solution)/shard_map/own_grads/pallas_call | solution.py:587
  67.8 0.9 %collective-permute-start.2 = (f32[1024,128]{1,0:T(8,128)S(1)}, f32[1024,128]{1,0:T(8,128)S(1)}, u32[]{:S(2)}, u32[]{:S(2)}) collective-permute-start(f32[1024,128]{1,0:T(8,128)S(1)} %get-tuple-element.27), channel_id=1, source_target_pairs={{0,1},{1,0},{2,3},{3,2},{4,5},{5,4},{6,7},{7,6},{8,9},{9,8},{10,11... | collective-permute-start | bytes 1572872 | tf_op jit(solution)/shard_map/ppermute | solution.py:30
  68.7 1.5 %collective-permute-done.2.other_ref = f32[1024,128]{1,0:T(8,128)S(1)} collective-permute-done((f32[1024,128]{1,0:T(8,128)S(1)}, f32[1024,128]{1,0:T(8,128)S(1)}, u32[]{:S(2)}, u32[]{:S(2)}) %collective-permute-start.2) | collective-permute-done | bytes 524320 | tf_op jit(solution)/shard_map/ppermute | solution.py:30
  70.3 0.0 all-to-all-done.2
  70.3 1.6 %join_grads.1 = bf16[1024,128]{1,0:T(8,128)(2,1)} custom-call(s32[8,1,3]{2,1,0:T(1,128)S(1)} %all_to_all.28.home_ref, f32[1024,128]{1,0:T(8,128)S(1)} %get-tuple-element.26.keep_ref, f32[1024,128]{1,0:T(8,128)S(1)} %collective-permute-done.2.other_ref, bf16[1536,128]{1,0:T(8,128)(2,1)S(1)} %bitcast.11), custom_call_target="tpu_custom_call" | custom-call | tf_op jit(solution)/shard_map/join_grads/pallas_call | solution.py:615
Async XLA Ops:
  0.6 10.5 %collective-permute-start = (bf16[1024,128]{1,0:T(8,128)(2,1)}, bf16[1024,128]{1,0:T(8,128)(2,1)S(1)}, u32[]{:S(2)}, u32[]{:S(2)}) collective-permute-start(bf16[1024,128]{1,0:T(8,128)(2,1)} %bitcast.14), channel_id=1, source_target_pairs={{0,1},{1,0},{2,3},{3,2},{4,5},{5,4},{6,7},{7,6},{8,9},{9,8},{10,11... | collective-permute-start | bytes 786440 | tf_op jit(solution)/shard_map/ppermute | solution.py:30
  11.1 7.3 %copy-start = (bf16[1024,128]{1,0:T(8,128)(2,1)}, bf16[1024,128]{1,0:T(8,128)(2,1)S(1)}, u32[]{:S(2)}) copy-start(bf16[1024,128]{1,0:T(8,128)(2,1)S(1)} %collective-permute-done.theirs_ref) | copy-start | bytes 786436
  13.0 14.2 %all-to-all-start.1 = ((bf16[8,192,128]{2,1,0:T(8,128)(2,1)}), bf16[8,192,128]{2,1,0:T(8,128)(2,1)S(1)}, u32[]{:S(2)}, u32[]{:S(2)}) async-start(bf16[8,192,128]{2,1,0:T(8,128)(2,1)} %bitcast.3), calls=%async_computation.1 | async-start | bytes 786432 | tf_op jit(solution)/shard_map/all_to_all | solution.py:516
  27.2 3.0 %collective-permute-start.1 = (bf16[1536,128]{1,0:T(8,128)(2,1)S(1)}, bf16[1536,128]{1,0:T(8,128)(2,1)S(1)}, u32[]{:S(2)}, u32[]{:S(2)}) collective-permute-start(bf16[1536,128]{1,0:T(8,128)(2,1)S(1)} %bitcast.12), channel_id=1, source_target_pairs={{0,1},{1,0},{2,3},{3,2},{4,5},{5,4},{6,7},{7,6},{8,9},{9,8},{10,11... | collective-permute-start | bytes 1179656 | tf_op jit(solution)/shard_map/ppermute | solution.py:30
  44.9 1.7 %collective-permute-start.3 = (bf16[1536,128]{1,0:T(8,128)(2,1)S(1)}, bf16[1536,128]{1,0:T(8,128)(2,1)S(1)}, u32[]{:S(2)}, u32[]{:S(2)}) collective-permute-start(bf16[1536,128]{1,0:T(8,128)(2,1)S(1)} %get-tuple-element.29), channel_id=1, source_target_pairs={{0,1},{1,0},{2,3},{3,2},{4,5},{5,4},{6,7},{7,6},{8,9},{9,8},{10,11... | collective-permute-start | bytes 1179656 | tf_op jit(solution)/shard_map/ppermute | solution.py:30
  47.4 22.8 %all-to-all-start.2 = ((bf16[8,192,128]{2,1,0:T(8,128)(2,1)}), bf16[8,192,128]{2,1,0:T(8,128)(2,1)S(1)}, u32[]{:S(2)}, u32[]{:S(2)}) async-start(bf16[8,192,128]{2,1,0:T(8,128)(2,1)} %bitcast.8), calls=%async_computation.2 | async-start | bytes 786432 | tf_op jit(solution)/shard_map/all_to_all | solution.py:585
  67.8 2.5 %collective-permute-start.2 = (f32[1024,128]{1,0:T(8,128)S(1)}, f32[1024,128]{1,0:T(8,128)S(1)}, u32[]{:S(2)}, u32[]{:S(2)}) collective-permute-start(f32[1024,128]{1,0:T(8,128)S(1)} %get-tuple-element.27), channel_id=1, source_target_pairs={{0,1},{1,0},{2,3},{3,2},{4,5},{5,4},{6,7},{7,6},{8,9},{9,8},{10,11... | collective-permute-start | bytes 1572872 | tf_op jit(solution)/shard_map/ppermute | solution.py:30
